TPU v7x, 128 devices: a whole 4x4x4 slice. The times are simulated.
128 devices in a mesh: ctx: 32 (over x, y, core), tp: 4 (over z).
Axes of the slice: x: 4, y: 4, z: 4, core: 2. Of those that a mesh axis runs over, the one named last changes fastest.
Arguments:
- query_proj: bfloat16 [8192, 8192], P('ctx', 'tp'), may hold values from -6 to 6
- key_proj: bfloat16 [8192, 8192], P('ctx', 'tp'), may hold values from -6 to 6
- value_proj: bfloat16 [8192, 8192], P('ctx', 'tp'), may hold values from -6 to 6
- short_filter: float32 [3, 7, 8192], P(None, None, 'tp'), may hold values from -2 to 2
- residues: float32 [16, 8192], P(None, 'tp'), may hold values from -3 to 3
- decay_rate: float32 [16, 8192], P(None, 'tp'), may hold values from 3.6621094e-05 to 0.0333333333
- skip_gain: float32 [8192], P('tp'), may hold values from 0.5 to 1.5
- doc_lengths: int32 [8], replicated, may hold values from 1 to 4096, 8192 in all
Outputs:
- mixed: bfloat16 [8192, 8192], P('ctx', 'tp')
Inputs may be any that keep to these rules, and one draw needn't show every extreme that they name: `doc_lengths`: the lengths sum to 8192, and the longest is exactly 4096.
All inputs are finite; a program needn't handle non-finite values.
Results may differ from a plain program's by a relative error of at most 0.008.
Values may be sent and summed in bfloat16 or wider, within the bound.
A program may use at most 128 MiB of HBM per device.

v0:
```python
import jax
import jax.numpy as jnp
from jax import lax
from jax.sharding import PartitionSpec as P

MODES = 16
TAPS = 7


block_rows = 32
highest = lax.Precision.HIGHEST


def from_behind(value, axis, steps):
    count = lax.axis_size(axis)
    first, last = (max(0, -steps), min(count, count - steps))
    return lax.ppermute(value, axis, [(source, source + steps) for source in range(first, last)])


def body(
    query_proj, key_proj, value_proj, short_filter, residues, decay_rate, skip_gain, doc_lengths
):
    row_count, channels = query_proj.shape
    ctx_count = lax.axis_size("ctx")
    my_index = lax.axis_index("ctx")
    first_row = my_index * row_count
    local_rows = jnp.arange(row_count, dtype=jnp.int32)
    positions = first_row + local_rows
    doc_starts = jnp.cumsum(doc_lengths) - doc_lengths
    row_start = jnp.max(
        jnp.where(doc_starts[None, :] <= positions[:, None], doc_starts[None, :], 0), axis=1
    )
    stacked = jnp.stack([query_proj, key_proj, value_proj])
    upper_rim = from_behind(stacked[:, row_count - TAPS + 1 :, :], "ctx", 1)
    extended = jnp.concatenate([upper_rim, stacked], axis=1)
    filtered = jnp.zeros(stacked.shape, jnp.float32)
    for lag_step in range(TAPS):
        inside = (positions - lag_step >= row_start)[None, :, None]
        window = extended[:, TAPS - 1 - lag_step : TAPS - 1 - lag_step + row_count, :].astype(
            jnp.float32
        )
        filtered = filtered + jnp.where(
            inside, short_filter[:, lag_step, :][:, None, :] * window, 0.0
        )
    query_short = filtered[0]
    gated = (filtered[1] * filtered[2]).astype(jnp.bfloat16)
    gated_float = gated.astype(jnp.float32)
    log_decay = jnp.log1p(-decay_rate)
    scaled = residues * jnp.sqrt(decay_rate * (2.0 - decay_rate))
    offsets = jnp.arange(block_rows, dtype=jnp.int32)
    offset_float = offsets.astype(jnp.float32)
    short_kernel = jnp.sum(
        scaled[None] * jnp.exp(offset_float[:, None, None] * log_decay[None]), axis=1
    )
    lag_table = offsets[:, None] - offsets[None, :]
    kernel = short_kernel[jnp.maximum(lag_table, 0)]
    carry_decay = jnp.exp((offset_float + 1.0)[:, None, None] * log_decay[None])
    tail_power = jnp.exp((block_rows - 1.0 - offset_float)[:, None, None] * log_decay[None])
    block_decay = jnp.exp(float(block_rows) * log_decay)
    block_count = row_count // block_rows
    firsts = first_row + jnp.arange(block_count, dtype=jnp.int32) * block_rows
    blocks_z = gated_float.reshape(block_count, block_rows, channels)
    blocks_start = row_start.reshape(block_count, block_rows)

    def next_state(state, block_z, block_start, block_first):
        rows_here = block_first + offsets
        last_start = block_start[block_rows - 1]
        keep_old = (last_start < block_first).astype(jnp.float32)
        in_doc = (rows_here >= last_start).astype(jnp.float32)
        return (
            jnp.sum(tail_power * (in_doc[:, None] * block_z)[:, None, :], axis=0)
            + keep_old * block_decay * state
        )

    def fold_state(state, inputs):
        block_z, block_start, block_first = inputs
        return (next_state(state, block_z, block_start, block_first), None)

    zero_state = jnp.zeros((MODES, channels), jnp.float32)
    own_state, unused = lax.scan(fold_state, zero_state, (blocks_z, blocks_start, firsts))
    own_flag = (row_start[row_count - 1] >= first_row).astype(jnp.float32)
    all_states, all_flags = (
        lax.all_gather(own_state[None], "ctx", axis=0, tiled=True),
        lax.all_gather(own_flag[None], "ctx", axis=0, tiled=True),
    )
    sources = jnp.arange(ctx_count, dtype=jnp.int32)
    earlier = sources < my_index
    last_reset = jnp.max(jnp.where(earlier & (all_flags > 0.5), sources, 0))
    reach = (earlier & (sources >= last_reset)).astype(jnp.float32)
    distance = (jnp.maximum(my_index - 1 - sources, 0) * row_count).astype(jnp.float32)
    factors = reach[:, None, None] * jnp.exp(distance[:, None, None] * log_decay[None])
    incoming = jnp.sum(factors * all_states, axis=0)

    def advance(state, inputs):
        block_z, block_start, block_first = inputs
        rows_here = block_first + offsets
        valid = (lag_table >= 0) & (rows_here[None, :] >= block_start[:, None])
        weights = jnp.where(valid[:, :, None], kernel, 0.0)
        inner = jnp.einsum("tsc,sc->tc", weights, block_z, precision=highest)
        continuing = (block_start < block_first)[:, None]
        from_state = jnp.sum(scaled[None] * carry_decay * state[None], axis=1)
        output = inner + jnp.where(continuing, from_state, 0.0)
        return (next_state(state, block_z, block_start, block_first), output)

    unused_state, outputs = lax.scan(advance, incoming, (blocks_z, blocks_start, firsts))
    conv = outputs.reshape(row_count, channels)
    return (query_short * (conv + skip_gain[None, :] * gated_float)).astype(jnp.bfloat16)


def solution(mesh):
    in_specs = (
        P("ctx", "tp"),
        P("ctx", "tp"),
        P("ctx", "tp"),
        P(None, None, "tp"),
        P(None, "tp"),
        P(None, "tp"),
        P("tp"),
        P(),
    )
    out_specs = P("ctx", "tp")
    return jax.shard_map(body, mesh=mesh, in_specs=in_specs, out_specs=out_specs, check_vma=False)
```

profile of v0, /device:TPU:0, one launch (start us, length us, event | category | flops | bytes accessed | tf_op | source)
XLA Modules:
  0.0 265.4 jit_solution(10334279180787630583)
XLA Ops:
  6.6 2.3 pad_maximum_fusion
  9.6 1.9 collective-permute-start
  13.4 1.1 multiply_exponential_fusion
  15.0 1.9 maximum_maximum_fusion
  17.0 8.1 %select_add_fusion = f32[3,256,2048]{2,1,0:T(8,128)S(1)} fusion(bf16[3,262,2048]{2,1,0:T(8,128)(2,1)S(1)} %maximum_maximum_fusion, f32[3,2048]{1,0:T(4,128)S(1)} %get-tuple-element.278, f32[3,2048]{1,0:T(4,128)S(1)} %get-tuple-element.279, f32[3,2048]{1,0:T(4,128)S(1)} %get-tuple-element.280, f32[3,2048]{1,0:T(4,128)S(1)} %get-tuple-element.281, ...), kind=kLoop, calls=%fused_computation.32 | loop fusion | flops 45613056 | bytes 28485376 | tf_op jit(solution)/shard_map/add | solution.py:42
  25.1 2.7 %copy-done = f32[3,256,2048]{2,1,0:T(8,128)} copy-done((f32[3,256,2048]{2,1,0:T(8,128)}, f32[3,256,2048]{2,1,0:T(8,128)S(1)}, u32[]{:S(2)}) %copy-start) | copy-done | bytes 6291480
  28.7 38.9 %while.25 = (s32[]{:T(128)}, f32[16,2048]{1,0:T(8,128)S(1)}, s32[8]{0:T(128)S(1)}, s32[8,32]{1,0:T(8,128)S(1)}, f32[8,32,2048]{2,1,0:T(8,128)S(1)}, /*index=5*/f...) while((s32[]{:T(128)}, f32[16,2048]{1,0:T(8,128)S(1)}, ...), condition=%wide.region_5.6_spmd.clone, body=%wide.region_3.5_spmd.clone.sunk | while | flops 3309669 | bytes 1573677 | solution.py:80
  31.3 1.3 compare_convert_fusion.4
  36.2 1.3 compare_convert_fusion.4
  41.0 1.3 compare_convert_fusion.4
  45.9 1.3 compare_convert_fusion.4
  50.8 1.3 compare_convert_fusion.4
  55.6 1.3 compare_convert_fusion.4
  60.5 1.3 compare_convert_fusion.4
  65.3 1.3 compare_convert_fusion.4
  70.9 67.2 %all-reduce = f32[32]{0:T(128)S(1)} all-reduce(f32[32]{0:T(128)S(1)} %dynamic-update-slice), channel_id=1, replica_groups=mesh['ctx'=32,'tp'=4] {'ctx'}, use_global_device_ids=true, to_apply=%add | all-reduce | flops 32 | bytes 256
  139.5 4.4 %multiply_reduce_fusion.1 = (f32[32,2048]{1,0:T(8,128)S(1)}, f32[16,2048]{1,0:T(8,128)S(1)}) fusion(f32[32]{0:T(128)S(1)} %get-tuple-element.284, f32[16,2048]{1,0:T(8,128)S(1)} %get-tuple-element.456, f32[16,2048]{1,0:T(8,128)S(1)} %get-tuple-element.493, f32[32,16,2048]{2,1,0:T(8,128)} %bitcast.99, f32[32]{0:T(128)S(1)} %get-tuple-element.285, ...), kind=kLoop, calls=%fused_computation.33 | loop fusion | flops 7241728 | bytes 4850048 | tf_op jit(solution)/shard_map/reduce_sum | solution.py:52
  144.0 6.8 %gather_fusion = f32[1024,2048]{1,0:T(8,128)} fusion(f32[32,2048]{1,0:T(8,128)S(1)} %get-tuple-element.217, s32[1024]{0:T(1024)S(1)} %broadcast_clamp_fusion), kind=kCustom, calls=%fused_computation | custom fusion | bytes 16781312 | tf_op jit(solution)/shard_map/gather | solution.py:56
  150.7 102.5 %while.26 = (s32[]{:T(128)}, f32[16,2048]{1,0:T(8,128)S(1)}, f32[8,32,2048]{2,1,0:T(8,128)}, s32[8]{0:T(128)S(1)}, s32[8,32]{1,0:T(8,128)S(1)}, /*index=5*/f32[8...) while((s32[]{:T(128)}, f32[16,2048]{1,0:T(8,128)S(1)}, ...), condition=%wide.region_11.12_spmd.clone.clone, body=%wide.region_8.11_spmd.clone.clone.sunk | while | flops 13766820 | bytes 12324235 | solution.py:105
  154.4 1.2 compare_convert_fusion.5
  155.8 2.2 fusion.34
  158.1 4.7 %multiply_reduce_fusion.4 = f32[2048,32]{0,1:T(8,128)S(1)} fusion(f32[32,32,2048]{2,1,0:T(8,128)} %get-tuple-element.481, f32[2048,32]{0,1:T(8,128)S(1)} %dynamic-slice_bitcast_fusion.2, pred[32,32]{1,0:T(8,128)(4,1)S(1)} %fusion.35), kind=kLoop, calls=%fused_computation.15.clone.1 | loop fusion | flops 6225920 | bytes 8913920 | tf_op jit(solution)/shard_map/while/body/eval_jaxpr/tsc,sc->tc/dot_general | solution.py:99
  162.8 0.8 bitcast_dynamic-update-slice_fusion.2
  167.3 1.2 compare_convert_fusion.5
  168.7 2.2 fusion.34
  170.9 4.7 %multiply_reduce_fusion.4 = f32[2048,32]{0,1:T(8,128)S(1)} fusion(f32[32,32,2048]{2,1,0:T(8,128)} %get-tuple-element.481, f32[2048,32]{0,1:T(8,128)S(1)} %dynamic-slice_bitcast_fusion.2, pred[32,32]{1,0:T(8,128)(4,1)S(1)} %fusion.35), kind=kLoop, calls=%fused_computation.15.clone.1 | loop fusion | flops 6225920 | bytes 8913920 | tf_op jit(solution)/shard_map/while/body/eval_jaxpr/tsc,sc->tc/dot_general | solution.py:99
  180.1 1.2 compare_convert_fusion.5
  181.5 2.2 fusion.34
  183.7 4.7 %multiply_reduce_fusion.4 = f32[2048,32]{0,1:T(8,128)S(1)} fusion(f32[32,32,2048]{2,1,0:T(8,128)} %get-tuple-element.481, f32[2048,32]{0,1:T(8,128)S(1)} %dynamic-slice_bitcast_fusion.2, pred[32,32]{1,0:T(8,128)(4,1)S(1)} %fusion.35), kind=kLoop, calls=%fused_computation.15.clone.1 | loop fusion | flops 6225920 | bytes 8913920 | tf_op jit(solution)/shard_map/while/body/eval_jaxpr/tsc,sc->tc/dot_general | solution.py:99
  188.4 0.8 bitcast_dynamic-update-slice_fusion.2
  192.9 1.2 compare_convert_fusion.5
  194.3 2.2 fusion.34
  196.5 4.7 %multiply_reduce_fusion.4 = f32[2048,32]{0,1:T(8,128)S(1)} fusion(f32[32,32,2048]{2,1,0:T(8,128)} %get-tuple-element.481, f32[2048,32]{0,1:T(8,128)S(1)} %dynamic-slice_bitcast_fusion.2, pred[32,32]{1,0:T(8,128)(4,1)S(1)} %fusion.35), kind=kLoop, calls=%fused_computation.15.clone.1 | loop fusion | flops 6225920 | bytes 8913920 | tf_op jit(solution)/shard_map/while/body/eval_jaxpr/tsc,sc->tc/dot_general | solution.py:99
  201.2 0.8 bitcast_dynamic-update-slice_fusion.2
  205.7 1.2 compare_convert_fusion.5
  207.1 2.2 fusion.34
  209.4 4.7 %multiply_reduce_fusion.4 = f32[2048,32]{0,1:T(8,128)S(1)} fusion(f32[32,32,2048]{2,1,0:T(8,128)} %get-tuple-element.481, f32[2048,32]{0,1:T(8,128)S(1)} %dynamic-slice_bitcast_fusion.2, pred[32,32]{1,0:T(8,128)(4,1)S(1)} %fusion.35), kind=kLoop, calls=%fused_computation.15.clone.1 | loop fusion | flops 6225920 | bytes 8913920 | tf_op jit(solution)/shard_map/while/body/eval_jaxpr/tsc,sc->tc/dot_general | solution.py:99
  218.5 1.2 compare_convert_fusion.5
  219.9 2.2 fusion.34
  222.2 4.7 %multiply_reduce_fusion.4 = f32[2048,32]{0,1:T(8,128)S(1)} fusion(f32[32,32,2048]{2,1,0:T(8,128)} %get-tuple-element.481, f32[2048,32]{0,1:T(8,128)S(1)} %dynamic-slice_bitcast_fusion.2, pred[32,32]{1,0:T(8,128)(4,1)S(1)} %fusion.35), kind=kLoop, calls=%fused_computation.15.clone.1 | loop fusion | flops 6225920 | bytes 8913920 | tf_op jit(solution)/shard_map/while/body/eval_jaxpr/tsc,sc->tc/dot_general | solution.py:99
  231.3 1.2 compare_convert_fusion.5
  232.7 2.2 fusion.34
  235.0 4.7 %multiply_reduce_fusion.4 = f32[2048,32]{0,1:T(8,128)S(1)} fusion(f32[32,32,2048]{2,1,0:T(8,128)} %get-tuple-element.481, f32[2048,32]{0,1:T(8,128)S(1)} %dynamic-slice_bitcast_fusion.2, pred[32,32]{1,0:T(8,128)(4,1)S(1)} %fusion.35), kind=kLoop, calls=%fused_computation.15.clone.1 | loop fusion | flops 6225920 | bytes 8913920 | tf_op jit(solution)/shard_map/while/body/eval_jaxpr/tsc,sc->tc/dot_general | solution.py:99
  244.1 1.2 compare_convert_fusion.5
  245.5 2.2 fusion.34
  247.8 4.7 %multiply_reduce_fusion.4 = f32[2048,32]{0,1:T(8,128)S(1)} fusion(f32[32,32,2048]{2,1,0:T(8,128)} %get-tuple-element.481, f32[2048,32]{0,1:T(8,128)S(1)} %dynamic-slice_bitcast_fusion.2, pred[32,32]{1,0:T(8,128)(4,1)S(1)} %fusion.35), kind=kLoop, calls=%fused_computation.15.clone.1 | loop fusion | flops 6225920 | bytes 8913920 | tf_op jit(solution)/shard_map/while/body/eval_jaxpr/tsc,sc->tc/dot_general | solution.py:99
  252.4 0.8 bitcast_dynamic-update-slice_fusion.2
  253.3 5.3 %fusion.20 = bf16[256,2048]{1,0:T(8,128)(2,1)} fusion(f32[3,256,2048]{2,1,0:T(8,128)} %copy-done, f32[8,32,2048]{2,1,0:T(8,128)} %get-tuple-element.115, f32[2048]{0:T(1024)S(1)} %copy-done.7), kind=kLoop, calls=%fused_computation.41 | loop fusion | flops 3670016 | bytes 9445376 | tf_op jit(solution)/shard_map/convert_element_type | solution.py:107
  (182 shorter events, 50.3 us)
Async XLA Ops:
  6.5 8.5 %copy-start.1 = (bf16[256,2048]{1,0:T(8,128)(2,1)S(1)}, bf16[256,2048]{1,0:T(8,128)(2,1)}, u32[]{:S(2)}) copy-start(bf16[256,2048]{1,0:T(8,128)(2,1)} %param.14) | copy-start | bytes 3145732
  6.5 8.5 %copy-start.2 = (bf16[256,2048]{1,0:T(8,128)(2,1)S(1)}, bf16[256,2048]{1,0:T(8,128)(2,1)}, u32[]{:S(2)}) copy-start(bf16[256,2048]{1,0:T(8,128)(2,1)} %param.13) | copy-start | bytes 3145732
  6.5 8.5 %copy-start.3 = (bf16[256,2048]{1,0:T(8,128)(2,1)S(1)}, bf16[256,2048]{1,0:T(8,128)(2,1)}, u32[]{:S(2)}) copy-start(bf16[256,2048]{1,0:T(8,128)(2,1)} %param.12) | copy-start | bytes 3145732
  6.5 5.6 %copy-start.13 = (s32[8]{0:T(128)S(1)}, s32[8]{0:T(128)}, u32[]{:S(2)}) copy-start(s32[8]{0:T(128)} %param.19) | copy-start | bytes 100
  6.5 6.5 %copy-start.6 = (f32[3,7,2048]{2,1,0:T(8,128)S(1)}, f32[3,7,2048]{2,1,0:T(8,128)}, u32[]{:S(2)}) copy-start(f32[3,7,2048]{2,1,0:T(8,128)} %param.15) | copy-start | bytes 516100
  6.5 133.0 %all-gather.3.cloned.1.call-start = ((), (), s32[]{:S(2)}) async-start(), calls=%async_computation | async-start | bytes 4325376 | tf_op jit(solution)/shard_map/all_gather | solution.py:83
  9.6 5.4 %collective-permute-start = (bf16[3,6,2048]{2,1,0:T(8,128)(2,1)}, bf16[3,6,2048]{2,1,0:T(8,128)(2,1)}, u32[]{:S(2)}, u32[]{:S(2)}) collective-permute-start(bf16[3,6,2048]{2,1,0:T(8,128)(2,1)} %slice.85), channel_id=1, source_target_pairs={{0,4},{4,8},{8,12},{12,16},{16,20},{20,24},{24,28},{28,32},{32,36}... | collective-permute-start | bytes 221192 | tf_op jit(solution)/shard_map/ppermute | solution.py:17
  13.1 3.8 %copy-start.8 = (pred[256]{0:T(512)(128)(4,1)S(1)}, pred[256]{0:T(512)(128)(4,1)}, u32[]{:S(2)}) copy-start(pred[256]{0:T(512)(128)(4,1)} %get-tuple-element.273) | copy-start | bytes 772
  13.1 3.8 %copy-start.9 = (pred[256]{0:T(512)(128)(4,1)S(1)}, pred[256]{0:T(512)(128)(4,1)}, u32[]{:S(2)}) copy-start(pred[256]{0:T(512)(128)(4,1)} %get-tuple-element.274) | copy-start | bytes 772
  13.1 3.9 %copy-start.10 = (pred[256]{0:T(512)(128)(4,1)S(1)}, pred[256]{0:T(512)(128)(4,1)}, u32[]{:S(2)}) copy-start(pred[256]{0:T(512)(128)(4,1)} %get-tuple-element.275) | copy-start | bytes 772
  13.1 3.9 %copy-start.11 = (pred[256]{0:T(512)(128)(4,1)S(1)}, pred[256]{0:T(512)(128)(4,1)}, u32[]{:S(2)}) copy-start(pred[256]{0:T(512)(128)(4,1)} %get-tuple-element.276) | copy-start | bytes 772
  13.1 3.9 %copy-start.12 = (pred[256]{0:T(512)(128)(4,1)S(1)}, pred[256]{0:T(512)(128)(4,1)}, u32[]{:S(2)}) copy-start(pred[256]{0:T(512)(128)(4,1)} %get-tuple-element.277) | copy-start | bytes 772
  25.1 2.7 %copy-start = (f32[3,256,2048]{2,1,0:T(8,128)}, f32[3,256,2048]{2,1,0:T(8,128)S(1)}, u32[]{:S(2)}) copy-start(f32[3,256,2048]{2,1,0:T(8,128)S(1)} %select_add_fusion) | copy-start | bytes 18874372
  27.8 0.9 copy-start.4
  27.8 0.9 copy-start.14
  27.8 0.9 copy-start.17
  28.7 40.9 %copy-start.15 = (u32[128]{0:T(128)S(1)}, u32[128]{0:T(128)}, u32[]{:S(2)}) copy-start(u32[128]{0:T(128)} %constant.81) | copy-start | bytes 1540
  67.6 0.7 copy-start.5
  144.0 6.8 %copy-start.16 = (f32[32]{0:T(128)S(1)}, f32[32]{0:T(128)}, u32[]{:S(2)}) copy-start(f32[32]{0:T(128)} %get-tuple-element.459) | copy-start | bytes 388
  150.7 102.5 %copy-start.7 = (f32[2048]{0:T(1024)S(1)}, f32[2048]{0:T(1024)}, u32[]{:S(2)}) copy-start(f32[2048]{0:T(1024)} %param.18) | copy-start | bytes 24580
Sparse Core Ops, SparseCore 0:
  68.4 49.4 all-gather.2
where the time goes:
time: 266 us; the launch traced here: 265 us
  other arithmetic  128 us (48%)
  blocking collectives  67.2 us (25%)
  local copies, waits for them, and re-layouts  33.2 us (12%)
  loops' own time  21 us (8%)
  between operations  14.3 us (5%)
    unnamed x1, blocking collectives  67.2 us
    dot_general x8, other arithmetic, advance(): inner = jnp.einsum('tsc,sc->tc', weights, block_z, precision=highest)  37.3 us
    convert_element_type x16, other arithmetic, next_state(): in_doc = (rows_here >= last_start).astype(jnp.float32)  20.2 us
    reduce_sum x8, other arithmetic, advance(): from_state = jnp.sum(scaled[None] * carry_decay * state[None], axis=1)  17.3 us
    another operation x1, loops' own time, body(): lax.scan(fold_state, zero_state, (blocks_z, blocks_start, firsts))  10.9 us
    another operation x1, loops' own time, body(): lax.scan(advance, incoming, (blocks_z, blocks_start, firsts))  10.2 us
    dynamic_slice x24, local copies, waits for them, and re-layouts, body(): lax.scan(fold_state, zero_state, (blocks_z, blocks_start, firsts))  9.96 us
    slice x16, local copies, waits for them, and re-layouts, next_state(): last_start = block_start[block_rows - 1]  9.28 us
  transfers between devices with their start and end apart: 2, of which 0 were waited for; matrix products, arithmetic and copies ran while one was open for 3% of the time, Pallas kernels for 0%

commit v1 on v0

--- a/solution.py
+++ b/solution.py
@@ -78,18 +78,24 @@
 
     zero_state = jnp.zeros((MODES, channels), jnp.float32)
     own_state, unused = lax.scan(fold_state, zero_state, (blocks_z, blocks_start, firsts))
-    own_flag = (row_start[row_count - 1] >= first_row).astype(jnp.float32)
-    all_states, all_flags = (
-        lax.all_gather(own_state[None], "ctx", axis=0, tiled=True),
-        lax.all_gather(own_flag[None], "ctx", axis=0, tiled=True),
-    )
-    sources = jnp.arange(ctx_count, dtype=jnp.int32)
-    earlier = sources < my_index
-    last_reset = jnp.max(jnp.where(earlier & (all_flags > 0.5), sources, 0))
-    reach = (earlier & (sources >= last_reset)).astype(jnp.float32)
-    distance = (jnp.maximum(my_index - 1 - sources, 0) * row_count).astype(jnp.float32)
-    factors = reach[:, None, None] * jnp.exp(distance[:, None, None] * log_decay[None])
-    incoming = jnp.sum(factors * all_states, axis=0)
+    rows_total = row_count
+
+    def starts_between(low_device, high_device):
+        low_row = jnp.maximum(low_device, 0) * row_count
+        high_row = (high_device + 1) * row_count
+        return jnp.any((doc_starts >= low_row) & (doc_starts < high_row)).astype(jnp.float32)
+
+    summary = own_state
+    span = 1
+    while 2 * span < ctx_count:
+        behind = from_behind(summary, "ctx", span)
+        open_path = 1.0 - starts_between(my_index - span + 1, my_index)
+        summary = summary + open_path * jnp.exp(float(span * rows_total) * log_decay) * behind
+        span *= 2
+    near = from_behind(summary, "ctx", 1)
+    far = from_behind(summary, "ctx", 1 + span)
+    open_path = 1.0 - starts_between(my_index - span, my_index - 1)
+    incoming = near + open_path * jnp.exp(float(span * rows_total) * log_decay) * far
 
     def advance(state, inputs):
         block_z, block_start, block_first = inputs

time: 266 us -> 223 us (0.84)
  the two profiles are of different devices: /device:TPU:0 before, /device:TPU:25 now
where the time goes in v1:
time: 223 us; the launch traced here: 222 us
  other arithmetic  124 us (56%)
  local copies, waits for them, and re-layouts  32.5 us (15%)
  starting transfers between devices  30.5 us (14%)
  loops' own time  21.1 us (9%)
  waiting for transfers between devices  10.4 us (5%)
  between operations  3.64 us (2%)
    dot_general x8, other arithmetic, advance(): inner = jnp.einsum('tsc,sc->tc', weights, block_z, precision=highest)  37.3 us
    ppermute x7, starting transfers between devices, from_behind(): lax.ppermute(value, axis, [(source, source + steps) for source in range(f...  30.5 us
    convert_element_type x16, other arithmetic, next_state(): in_doc = (rows_here >= last_start).astype(jnp.float32)  20.3 us
    reduce_sum x8, other arithmetic, advance(): from_state = jnp.sum(scaled[None] * carry_decay * state[None], axis=1)  17.3 us
    another operation x1, loops' own time, body(): lax.scan(advance, incoming, (blocks_z, blocks_start, firsts))  11.2 us
    ppermute x7, waiting for transfers between devices, from_behind(): lax.ppermute(value, axis, [(source, source + steps) for source in range(f...  10.4 us
    another operation x1, loops' own time, body(): lax.scan(fold_state, zero_state, (blocks_z, blocks_start, firsts))  9.96 us
    slice x16, local copies, waits for them, and re-layouts, next_state(): last_start = block_start[block_rows - 1]  9.94 us
  transfers between devices with their start and end apart: 7, of which 4 were waited for; matrix products, arithmetic and copies ran while one was open for 6% of the time, Pallas kernels for 0%

profile of v1, /device:TPU:25, one launch (start us, length us, event | category | flops | bytes accessed | tf_op | source)
XLA Modules:
  0.0 222.0 jit_solution(4067910205860057109)
XLA Ops:
  0.0 2.3 %pad_maximum_fusion = bf16[3,256,2048]{2,1,0:T(8,128)(2,1)S(1)} fusion(bf16[1,256,2048]{2,1,0:T(8,128)(2,1)} %bitcast.87, bf16[1,256,2048]{2,1,0:T(8,128)(2,1)} %bitcast.90, bf16[1,256,2048]{2,1,0:T(8,128)(2,1)} %bitcast.93), kind=kLoop, calls=%fused_computation.35 | loop fusion | flops 3145728 | bytes 6291456 | tf_op jit(solution)/shard_map/stack | solution.py:33
  3.1 3.3 %collective-permute-start = (bf16[3,6,2048]{2,1,0:T(8,128)(2,1)}, bf16[3,6,2048]{2,1,0:T(8,128)(2,1)}, u32[]{:S(2)}, u32[]{:S(2)}) collective-permute-start(bf16[3,6,2048]{2,1,0:T(8,128)(2,1)} %slice.81), channel_id=1, source_target_pairs={{0,4},{4,8},{8,12},{12,16},{16,20},{20,24},{24,28},{28,32},{32,36}... | collective-permute-start | bytes 221192 | tf_op jit(solution)/shard_map/ppermute | solution.py:17
  8.8 1.9 fusion.26
  11.7 2.1 maximum_maximum_fusion
  13.8 8.1 %select_add_fusion = f32[3,256,2048]{2,1,0:T(8,128)S(1)} fusion(bf16[3,262,2048]{2,1,0:T(8,128)(2,1)S(1)} %maximum_maximum_fusion, f32[3,2048]{1,0:T(4,128)S(1)} %get-tuple-element.282, f32[3,2048]{1,0:T(4,128)S(1)} %get-tuple-element.283, f32[3,2048]{1,0:T(4,128)S(1)} %get-tuple-element.284, f32[3,2048]{1,0:T(4,128)S(1)} %get-tuple-element.285, ...), kind=kLoop, calls=%fused_computation.32 | loop fusion | flops 45613056 | bytes 28485376 | tf_op jit(solution)/shard_map/add | solution.py:42
  21.9 2.7 %copy-done = f32[3,256,2048]{2,1,0:T(8,128)} copy-done((f32[3,256,2048]{2,1,0:T(8,128)}, f32[3,256,2048]{2,1,0:T(8,128)S(1)}, u32[]{:S(2)}) %copy-start) | copy-done | bytes 6291480
  25.6 36.4 %while.25 = (s32[]{:T(128)}, f32[16,2048]{1,0:T(8,128)S(1)}, s32[8]{0:T(128)S(1)}, s32[8,32]{1,0:T(8,128)S(1)}, f32[8,32,2048]{2,1,0:T(8,128)S(1)}, /*index=5*/f...) while((s32[]{:T(128)}, f32[16,2048]{1,0:T(8,128)S(1)}, ...), condition=%wide.region_4.5_spmd.clone, body=%wide.region_2.4_spmd.clone.sunk | while | flops 3309669 | bytes 1573677 | solution.py:80
  28.0 1.2 compare_convert_fusion.4
  32.5 1.2 compare_convert_fusion.4
  37.1 1.2 compare_convert_fusion.4
  41.7 1.2 compare_convert_fusion.4
  62.0 3.1 %collective-permute-start.1 = (f32[16,2048]{1,0:T(8,128)S(1)}, f32[16,2048]{1,0:T(8,128)S(1)}, u32[]{:S(2)}, u32[]{:S(2)}) collective-permute-start(f32[16,2048]{1,0:T(8,128)S(1)} %get-tuple-element.114), channel_id=1, source_target_pairs={{0,4},{4,8},{8,12},{12,16},{16,20},{20,24},{24,28},{28,32},{32,36}... | collective-permute-start | bytes 393224 | tf_op jit(solution)/shard_map/ppermute | solution.py:17
  65.8 1.2 collective-permute-done.1
  67.1 2.0 collective-permute-start.2
  69.8 3.8 %collective-permute-done.2 = f32[16,2048]{1,0:T(8,128)S(1)} collective-permute-done((f32[16,2048]{1,0:T(8,128)S(1)}, f32[16,2048]{1,0:T(8,128)S(1)}, u32[]{:S(2)}, u32[]{:S(2)}) %collective-permute-start.2) | collective-permute-done | bytes 131104 | tf_op jit(solution)/shard_map/ppermute | solution.py:17
  73.6 2.3 %collective-permute-start.3 = (f32[16,2048]{1,0:T(8,128)S(1)}, f32[16,2048]{1,0:T(8,128)S(1)}, u32[]{:S(2)}, u32[]{:S(2)}) collective-permute-start(f32[16,2048]{1,0:T(8,128)S(1)} %multiply_add_fusion.4), channel_id=1, source_target_pairs={{0,16},{4,20},{8,24},{12,28},{16,32},{20,36},{24,40},{28,44},{32,4... | collective-permute-start | bytes 393224 | tf_op jit(solution)/shard_map/ppermute | solution.py:17
  76.8 4.1 %collective-permute-done.3 = f32[16,2048]{1,0:T(8,128)S(1)} collective-permute-done((f32[16,2048]{1,0:T(8,128)S(1)}, f32[16,2048]{1,0:T(8,128)S(1)}, u32[]{:S(2)}, u32[]{:S(2)}) %collective-permute-start.3) | collective-permute-done | bytes 131104 | tf_op jit(solution)/shard_map/ppermute | solution.py:17
  80.9 3.1 %collective-permute-start.4 = (f32[16,2048]{1,0:T(8,128)S(1)}, f32[16,2048]{1,0:T(8,128)S(1)}, u32[]{:S(2)}, u32[]{:S(2)}) collective-permute-start(f32[16,2048]{1,0:T(8,128)S(1)} %multiply_add_fusion.3), channel_id=1, source_target_pairs={{0,32},{4,36},{8,40},{12,44},{16,48},{20,52},{24,56},{28,60},{32,6... | collective-permute-start | bytes 393224 | tf_op jit(solution)/shard_map/ppermute | solution.py:17
  84.7 1.3 collective-permute-done.4
  86.1 14.5 %collective-permute-start.6 = (f32[16,2048]{1,0:T(8,128)S(1)}, f32[16,2048]{1,0:T(8,128)S(1)}, u32[]{:S(2)}, u32[]{:S(2)}) collective-permute-start(f32[16,2048]{1,0:T(8,128)S(1)} %multiply_add_fusion.2), channel_id=1, source_target_pairs={{0,68},{4,72},{8,76},{12,80},{16,84},{20,88},{24,92},{28,96},{32,1... | collective-permute-start | bytes 393224 | tf_op jit(solution)/shard_map/ppermute | solution.py:17
  100.6 2.1 collective-permute-start.5
  104.6 6.8 %gather_fusion = f32[1024,2048]{1,0:T(8,128)} fusion(f32[32,2048]{1,0:T(8,128)S(1)} %multiply_reduce_fusion.1, s32[1024]{0:T(1024)S(1)} %broadcast_clamp_fusion), kind=kCustom, calls=%fused_computation | custom fusion | bytes 16781312 | tf_op jit(solution)/shard_map/gather | solution.py:56
  111.5 105.2 %while.26 = (s32[]{:T(128)}, f32[16,2048]{1,0:T(8,128)S(1)}, f32[8,32,2048]{2,1,0:T(8,128)}, s32[8]{0:T(128)S(1)}, s32[8,32]{1,0:T(8,128)S(1)}, /*index=5*/f32[8...) while((s32[]{:T(128)}, f32[16,2048]{1,0:T(8,128)S(1)}, ...), condition=%wide.region_14.15_spmd.clone.clone, body=%wide.region_11.14_spmd.clone.clone.sunk | while | flops 13766820 | bytes 12324235 | solution.py:111
  115.4 1.3 compare_convert_fusion.5
  116.9 2.2 fusion.33
  119.1 4.7 %multiply_reduce_fusion.3 = f32[2048,32]{0,1:T(8,128)S(1)} fusion(f32[32,32,2048]{2,1,0:T(8,128)} %get-tuple-element.481, f32[2048,32]{0,1:T(8,128)S(1)} %dynamic-slice_bitcast_fusion.2, pred[32,32]{1,0:T(8,128)(4,1)S(1)} %fusion.34), kind=kLoop, calls=%fused_computation.15.clone.1 | loop fusion | flops 6225920 | bytes 8913920 | tf_op jit(solution)/shard_map/while/body/eval_jaxpr/tsc,sc->tc/dot_general | solution.py:105
  128.5 1.3 compare_convert_fusion.5
  130.0 2.2 fusion.33
  132.3 4.7 %multiply_reduce_fusion.3 = f32[2048,32]{0,1:T(8,128)S(1)} fusion(f32[32,32,2048]{2,1,0:T(8,128)} %get-tuple-element.481, f32[2048,32]{0,1:T(8,128)S(1)} %dynamic-slice_bitcast_fusion.2, pred[32,32]{1,0:T(8,128)(4,1)S(1)} %fusion.34), kind=kLoop, calls=%fused_computation.15.clone.1 | loop fusion | flops 6225920 | bytes 8913920 | tf_op jit(solution)/shard_map/while/body/eval_jaxpr/tsc,sc->tc/dot_general | solution.py:105
  141.7 1.3 compare_convert_fusion.5
  143.2 2.2 fusion.33
  145.5 4.7 %multiply_reduce_fusion.3 = f32[2048,32]{0,1:T(8,128)S(1)} fusion(f32[32,32,2048]{2,1,0:T(8,128)} %get-tuple-element.481, f32[2048,32]{0,1:T(8,128)S(1)} %dynamic-slice_bitcast_fusion.2, pred[32,32]{1,0:T(8,128)(4,1)S(1)} %fusion.34), kind=kLoop, calls=%fused_computation.15.clone.1 | loop fusion | flops 6225920 | bytes 8913920 | tf_op jit(solution)/shard_map/while/body/eval_jaxpr/tsc,sc->tc/dot_general | solution.py:105
  154.8 1.3 compare_convert_fusion.5
  156.3 2.2 fusion.33
  158.6 4.7 %multiply_reduce_fusion.3 = f32[2048,32]{0,1:T(8,128)S(1)} fusion(f32[32,32,2048]{2,1,0:T(8,128)} %get-tuple-element.481, f32[2048,32]{0,1:T(8,128)S(1)} %dynamic-slice_bitcast_fusion.2, pred[32,32]{1,0:T(8,128)(4,1)S(1)} %fusion.34), kind=kLoop, calls=%fused_computation.15.clone.1 | loop fusion | flops 6225920 | bytes 8913920 | tf_op jit(solution)/shard_map/while/body/eval_jaxpr/tsc,sc->tc/dot_general | solution.py:105
  168.0 1.3 compare_convert_fusion.5
  169.5 2.2 fusion.33
  171.7 4.7 %multiply_reduce_fusion.3 = f32[2048,32]{0,1:T(8,128)S(1)} fusion(f32[32,32,2048]{2,1,0:T(8,128)} %get-tuple-element.481, f32[2048,32]{0,1:T(8,128)S(1)} %dynamic-slice_bitcast_fusion.2, pred[32,32]{1,0:T(8,128)(4,1)S(1)} %fusion.34), kind=kLoop, calls=%fused_computation.15.clone.1 | loop fusion | flops 6225920 | bytes 8913920 | tf_op jit(solution)/shard_map/while/body/eval_jaxpr/tsc,sc->tc/dot_general | solution.py:105
  181.1 1.3 compare_convert_fusion.5
  182.6 2.2 fusion.33
  184.9 4.7 %multiply_reduce_fusion.3 = f32[2048,32]{0,1:T(8,128)S(1)} fusion(f32[32,32,2048]{2,1,0:T(8,128)} %get-tuple-element.481, f32[2048,32]{0,1:T(8,128)S(1)} %dynamic-slice_bitcast_fusion.2, pred[32,32]{1,0:T(8,128)(4,1)S(1)} %fusion.34), kind=kLoop, calls=%fused_computation.15.clone.1 | loop fusion | flops 6225920 | bytes 8913920 | tf_op jit(solution)/shard_map/while/body/eval_jaxpr/tsc,sc->tc/dot_general | solution.py:105
  194.3 1.3 compare_convert_fusion.5
  195.8 2.2 fusion.33
  198.0 4.7 %multiply_reduce_fusion.3 = f32[2048,32]{0,1:T(8,128)S(1)} fusion(f32[32,32,2048]{2,1,0:T(8,128)} %get-tuple-element.481, f32[2048,32]{0,1:T(8,128)S(1)} %dynamic-slice_bitcast_fusion.2, pred[32,32]{1,0:T(8,128)(4,1)S(1)} %fusion.34), kind=kLoop, calls=%fused_computation.15.clone.1 | loop fusion | flops 6225920 | bytes 8913920 | tf_op jit(solution)/shard_map/while/body/eval_jaxpr/tsc,sc->tc/dot_general | solution.py:105
  207.4 1.3 compare_convert_fusion.5
  208.9 2.2 fusion.33
  211.2 4.7 %multiply_reduce_fusion.3 = f32[2048,32]{0,1:T(8,128)S(1)} fusion(f32[32,32,2048]{2,1,0:T(8,128)} %get-tuple-element.481, f32[2048,32]{0,1:T(8,128)S(1)} %dynamic-slice_bitcast_fusion.2, pred[32,32]{1,0:T(8,128)(4,1)S(1)} %fusion.34), kind=kLoop, calls=%fused_computation.15.clone.1 | loop fusion | flops 6225920 | bytes 8913920 | tf_op jit(solution)/shard_map/while/body/eval_jaxpr/tsc,sc->tc/dot_general | solution.py:105
  216.7 5.3 %fusion.20 = bf16[256,2048]{1,0:T(8,128)(2,1)} fusion(f32[3,256,2048]{2,1,0:T(8,128)} %copy-done, f32[8,32,2048]{2,1,0:T(8,128)} %get-tuple-element.115, f32[2048]{0:T(1024)S(1)} %copy-done.10), kind=kLoop, calls=%fused_computation.40 | loop fusion | flops 3670016 | bytes 9445376 | tf_op jit(solution)/shard_map/convert_element_type | solution.py:113
  (188 shorter events, 57.0 us)
Async XLA Ops:
  0.0 11.6 %copy-start.1 = (bf16[256,2048]{1,0:T(8,128)(2,1)S(1)}, bf16[256,2048]{1,0:T(8,128)(2,1)}, u32[]{:S(2)}) copy-start(bf16[256,2048]{1,0:T(8,128)(2,1)} %param.14) | copy-start | bytes 3145732
  0.0 11.6 %copy-start.2 = (bf16[256,2048]{1,0:T(8,128)(2,1)S(1)}, bf16[256,2048]{1,0:T(8,128)(2,1)}, u32[]{:S(2)}) copy-start(bf16[256,2048]{1,0:T(8,128)(2,1)} %param.13) | copy-start | bytes 3145732
  0.0 11.7 %copy-start.3 = (bf16[256,2048]{1,0:T(8,128)(2,1)S(1)}, bf16[256,2048]{1,0:T(8,128)(2,1)}, u32[]{:S(2)}) copy-start(bf16[256,2048]{1,0:T(8,128)(2,1)} %param.12) | copy-start | bytes 3145732
  0.0 7.0 %copy-start.15 = (s32[8]{0:T(128)S(1)}, s32[8]{0:T(128)}, u32[]{:S(2)}) copy-start(s32[8]{0:T(128)} %param.19) | copy-start | bytes 100
  0.0 10.8 %copy-start.4 = (f32[16,2048]{1,0:T(8,128)S(1)}, f32[16,2048]{1,0:T(8,128)}, u32[]{:S(2)}) copy-start(f32[16,2048]{1,0:T(8,128)} %param.17) | copy-start | bytes 393220
  0.0 10.8 %copy-start.7 = (f32[16,2048]{1,0:T(8,128)S(1)}, f32[16,2048]{1,0:T(8,128)}, u32[]{:S(2)}) copy-start(f32[16,2048]{1,0:T(8,128)} %param.16) | copy-start | bytes 393220
  3.1 8.6 %collective-permute-start = (bf16[3,6,2048]{2,1,0:T(8,128)(2,1)}, bf16[3,6,2048]{2,1,0:T(8,128)(2,1)}, u32[]{:S(2)}, u32[]{:S(2)}) collective-permute-start(bf16[3,6,2048]{2,1,0:T(8,128)(2,1)} %slice.81), channel_id=1, source_target_pairs={{0,4},{4,8},{8,12},{12,16},{16,20},{20,24},{24,28},{28,32},{32,36}... | collective-permute-start | bytes 221192 | tf_op jit(solution)/shard_map/ppermute | solution.py:17
  8.7 5.0 %copy-start.11 = (pred[256]{0:T(512)(128)(4,1)S(1)}, pred[256]{0:T(512)(128)(4,1)}, u32[]{:S(2)}) copy-start(pred[256]{0:T(512)(128)(4,1)} %get-tuple-element.278) | copy-start | bytes 772
  8.7 5.0 %copy-start.12 = (pred[256]{0:T(512)(128)(4,1)S(1)}, pred[256]{0:T(512)(128)(4,1)}, u32[]{:S(2)}) copy-start(pred[256]{0:T(512)(128)(4,1)} %get-tuple-element.279) | copy-start | bytes 772
  8.7 5.0 %copy-start.13 = (pred[256]{0:T(512)(128)(4,1)S(1)}, pred[256]{0:T(512)(128)(4,1)}, u32[]{:S(2)}) copy-start(pred[256]{0:T(512)(128)(4,1)} %get-tuple-element.280) | copy-start | bytes 772
  8.7 5.0 %copy-start.14 = (pred[256]{0:T(512)(128)(4,1)S(1)}, pred[256]{0:T(512)(128)(4,1)}, u32[]{:S(2)}) copy-start(pred[256]{0:T(512)(128)(4,1)} %get-tuple-element.281) | copy-start | bytes 772
  21.9 2.7 %copy-start = (f32[3,256,2048]{2,1,0:T(8,128)}, f32[3,256,2048]{2,1,0:T(8,128)S(1)}, u32[]{:S(2)}) copy-start(f32[3,256,2048]{2,1,0:T(8,128)S(1)} %select_add_fusion) | copy-start | bytes 18874372
  24.6 0.9 copy-start.6
  24.6 1.0 copy-start.9
  24.6 1.0 copy-start.16
  25.6 41.4 %copy-start.5 = (f32[16,2048]{1,0:T(8,128)S(1)}, f32[16,2048]{1,0:T(8,128)}, u32[]{:S(2)}) copy-start(f32[16,2048]{1,0:T(8,128)} %param.17) | copy-start | bytes 393220
  25.6 77.1 %copy-start.8 = (f32[16,2048]{1,0:T(8,128)S(1)}, f32[16,2048]{1,0:T(8,128)}, u32[]{:S(2)}) copy-start(f32[16,2048]{1,0:T(8,128)} %get-tuple-element.456) | copy-start | bytes 393220
  62.0 5.0 %collective-permute-start.1 = (f32[16,2048]{1,0:T(8,128)S(1)}, f32[16,2048]{1,0:T(8,128)S(1)}, u32[]{:S(2)}, u32[]{:S(2)}) collective-permute-start(f32[16,2048]{1,0:T(8,128)S(1)} %get-tuple-element.114), channel_id=1, source_target_pairs={{0,4},{4,8},{8,12},{12,16},{16,20},{20,24},{24,28},{28,32},{32,36}... | collective-permute-start | bytes 393224 | tf_op jit(solution)/shard_map/ppermute | solution.py:17
  67.1 6.4 %collective-permute-start.2 = (f32[16,2048]{1,0:T(8,128)S(1)}, f32[16,2048]{1,0:T(8,128)S(1)}, u32[]{:S(2)}, u32[]{:S(2)}) collective-permute-start(f32[16,2048]{1,0:T(8,128)S(1)} %multiply_add_fusion.5), channel_id=1, source_target_pairs={{0,8},{4,12},{8,16},{12,20},{16,24},{20,28},{24,32},{28,36},{32,40... | collective-permute-start | bytes 393224 | tf_op jit(solution)/shard_map/ppermute | solution.py:17
  73.6 7.2 %collective-permute-start.3 = (f32[16,2048]{1,0:T(8,128)S(1)}, f32[16,2048]{1,0:T(8,128)S(1)}, u32[]{:S(2)}, u32[]{:S(2)}) collective-permute-start(f32[16,2048]{1,0:T(8,128)S(1)} %multiply_add_fusion.4), channel_id=1, source_target_pairs={{0,16},{4,20},{8,24},{12,28},{16,32},{20,36},{24,40},{28,44},{32,4... | collective-permute-start | bytes 393224 | tf_op jit(solution)/shard_map/ppermute | solution.py:17
  80.9 5.1 %collective-permute-start.4 = (f32[16,2048]{1,0:T(8,128)S(1)}, f32[16,2048]{1,0:T(8,128)S(1)}, u32[]{:S(2)}, u32[]{:S(2)}) collective-permute-start(f32[16,2048]{1,0:T(8,128)S(1)} %multiply_add_fusion.3), channel_id=1, source_target_pairs={{0,32},{4,36},{8,40},{12,44},{16,48},{20,52},{24,56},{28,60},{32,6... | collective-permute-start | bytes 393224 | tf_op jit(solution)/shard_map/ppermute | solution.py:17
  86.1 25.3 %collective-permute-start.6 = (f32[16,2048]{1,0:T(8,128)S(1)}, f32[16,2048]{1,0:T(8,128)S(1)}, u32[]{:S(2)}, u32[]{:S(2)}) collective-permute-start(f32[16,2048]{1,0:T(8,128)S(1)} %multiply_add_fusion.2), channel_id=1, source_target_pairs={{0,68},{4,72},{8,76},{12,80},{16,84},{20,88},{24,92},{28,96},{32,1... | collective-permute-start | bytes 393224 | tf_op jit(solution)/shard_map/ppermute | solution.py:17
  100.6 10.7 %collective-permute-start.5 = (f32[16,2048]{1,0:T(8,128)S(1)}, f32[16,2048]{1,0:T(8,128)S(1)}, u32[]{:S(2)}, u32[]{:S(2)}) collective-permute-start(f32[16,2048]{1,0:T(8,128)S(1)} %multiply_add_fusion.2), channel_id=1, source_target_pairs={{0,4},{4,8},{8,12},{12,16},{16,20},{20,24},{24,28},{28,32},{32,36}... | collective-permute-start | bytes 393224 | tf_op jit(solution)/shard_map/ppermute | solution.py:17
  111.4 105.2 %copy-start.10 = (f32[2048]{0:T(1024)S(1)}, f32[2048]{0:T(1024)}, u32[]{:S(2)}) copy-start(f32[2048]{0:T(1024)} %param.18) | copy-start | bytes 24580

commit v2 on v1

v2 whole, which is shorter than its diff:
```python
import functools

import jax
import jax.numpy as jnp
from jax import lax
from jax.experimental import pallas as pl
from jax.experimental.pallas import tpu as pltpu
from jax.sharding import PartitionSpec as P

MODES = 16
TAPS = 7
LANES = 128
SEGMENTS = 8
INTERPRET = False


def from_behind(value, axis, steps):
    count = lax.axis_size(axis)
    first, last = (max(0, -steps), min(count, count - steps))
    return lax.ppermute(value, axis, [(source, source + steps) for source in range(first, last)])


def local_kernel(q_ref, k_ref, v_ref, rim_ref, filt_ref, amp_ref, lam_ref, skip_ref, since_ref, keep_ref,
                 segkeep_ref, acc_ref, qs_ref, cl_ref, ext_ref, g_ref):
    rows = q_ref.shape[0]
    seg_rows = rows // SEGMENTS
    since = since_ref[...]
    filtered = []
    for branch, src in enumerate((q_ref, k_ref, v_ref)):
        ext_ref[0:8, :] = rim_ref[branch].astype(jnp.float32)
        ext_ref[8:8 + rows, :] = src[...].astype(jnp.float32)
        total = jnp.zeros((rows, LANES), jnp.float32)
        for lag in range(TAPS):
            window = ext_ref[8 - lag:8 - lag + rows, :]
            tap = filt_ref[branch, lag:lag + 1, :]
            total = total + jnp.where(since >= float(lag), tap * window, 0.0)
        filtered.append(total)
    qs_ref[...] = filtered[0]
    g_ref[...] = (filtered[1] * filtered[2]).astype(jnp.bfloat16).astype(jnp.float32)
    lam = [jnp.broadcast_to(lam_ref[m:m + 1, :], (SEGMENTS, LANES)) for m in range(MODES)]
    amp = [jnp.broadcast_to(amp_ref[m:m + 1, :], (SEGMENTS, LANES)) for m in range(MODES)]
    skip = jnp.broadcast_to(skip_ref[...], (SEGMENTS, LANES))

    def step(j, states):
        x = g_ref[pl.ds(j, SEGMENTS, stride=seg_rows), :]
        keep = keep_ref[pl.ds(j, SEGMENTS, stride=seg_rows), :]
        new_states = []
        y = skip * x
        for m in range(MODES):
            h = lam[m] * (keep * states[m]) + x
            new_states.append(h)
            y = y + amp[m] * h
        acc_ref[pl.ds(j, SEGMENTS, stride=seg_rows), :] = y
        return tuple(new_states)

    zero = jnp.zeros((SEGMENTS, LANES), jnp.float32)
    ends = lax.fori_loop(0, seg_rows, step, tuple([zero] * MODES))
    segkeep = segkeep_ref[...]
    for m in range(MODES):
        seg_decay = jnp.exp(float(seg_rows) * jnp.log(lam_ref[m:m + 1, :]))
        carried = jnp.zeros((1, LANES), jnp.float32)
        cl_ref[m, 0:1, :] = carried
        for p in range(SEGMENTS):
            carried = ends[m][p:p + 1, :] + segkeep[p:p + 1, :] * seg_decay * carried
            cl_ref[m, p + 1:p + 2, :] = carried
        cl_ref[m, SEGMENTS + 1:, :] = jnp.zeros((16 - SEGMENTS - 1, LANES), jnp.float32)


def fix_kernel(acc_ref, qs_ref, cl_ref, hin_ref, amp_ref, logl_ref, cont_ref, open_ref, out_ref):
    rows = acc_ref.shape[0]
    seg_rows = rows // SEGMENTS
    seg_index = lax.broadcasted_iota(jnp.int32, (SEGMENTS, LANES), 0).astype(jnp.float32)
    lag_index = lax.broadcasted_iota(jnp.int32, (seg_rows, LANES), 0).astype(jnp.float32) + 1.0
    opened = open_ref[...]
    starts = []
    powers = []
    for m in range(MODES):
        logl = logl_ref[m:m + 1, :]
        start = cl_ref[m, 0:SEGMENTS, :] + opened * jnp.exp(seg_index * (float(seg_rows) * logl)) * hin_ref[m:m + 1, :]
        starts.append(start)
        powers.append(amp_ref[m:m + 1, :] * jnp.exp(lag_index * logl))
    for p in range(SEGMENTS):
        lo = p * seg_rows
        corr = jnp.zeros((seg_rows, LANES), jnp.float32)
        for m in range(MODES):
            corr = corr + powers[m] * starts[m][p:p + 1, :]
        conv = acc_ref[lo:lo + seg_rows, :] + cont_ref[lo:lo + seg_rows, :] * corr
        out_ref[lo:lo + seg_rows, :] = (qs_ref[lo:lo + seg_rows, :] * conv).astype(out_ref.dtype)


def body(query_proj, key_proj, value_proj, short_filter, residues, decay_rate, skip_gain, doc_lengths):
    row_count, channels = query_proj.shape
    ctx_count = lax.axis_size("ctx")
    my_index = lax.axis_index("ctx")
    first_row = my_index * row_count
    seg_rows = row_count // SEGMENTS
    local_rows = jnp.arange(row_count, dtype=jnp.int32)
    positions = first_row + local_rows
    doc_starts = jnp.cumsum(doc_lengths) - doc_lengths
    row_start = jnp.max(
        jnp.where(doc_starts[None, :] <= positions[:, None], doc_starts[None, :], 0), axis=1
    )
    since = (positions - row_start).astype(jnp.float32)
    keep = (positions != row_start).astype(jnp.float32)
    seg_first = first_row + (local_rows // seg_rows) * seg_rows
    cont = (row_start < seg_first).astype(jnp.float32)
    seg_ids = jnp.arange(SEGMENTS, dtype=jnp.int32)
    seg_lo = first_row + seg_ids * seg_rows
    in_seg = (doc_starts[None, :] >= seg_lo[:, None]) & (doc_starts[None, :] < seg_lo[:, None] + seg_rows)
    segkeep = 1.0 - jnp.any(in_seg, axis=1).astype(jnp.float32)
    before = (doc_starts[None, :] >= first_row) & (doc_starts[None, :] < seg_lo[:, None])
    opened = 1.0 - jnp.any(before, axis=1).astype(jnp.float32)

    def lanes(column):
        return jnp.broadcast_to(column[:, None], (column.shape[0], LANES))

    stacked = jnp.stack([query_proj, key_proj, value_proj])
    rim = from_behind(stacked[:, row_count - TAPS + 1:, :], "ctx", 1)
    rim = jnp.concatenate([jnp.zeros((3, 8 - TAPS + 1, channels), rim.dtype), rim], axis=1)
    log_decay = jnp.log1p(-decay_rate)
    lam = jnp.exp(log_decay)
    amp = residues * jnp.sqrt(decay_rate * (2.0 - decay_rate))
    tiles = channels // LANES
    col = lambda *lead: pl.BlockSpec(tuple(lead) + (LANES,), lambda c: (0,) * len(lead) + (c,))
    fixed = lambda *shape: pl.BlockSpec(shape, lambda c: (0,) * len(shape))
    f32 = jnp.float32
    acc, q_short, cl = pl.pallas_call(
        local_kernel,
        grid=(tiles,),
        in_specs=[col(row_count), col(row_count), col(row_count), col(3, 8), col(3, TAPS), col(MODES), col(MODES),
                  col(1), fixed(row_count, LANES), fixed(row_count, LANES), fixed(SEGMENTS, LANES)],
        out_specs=[col(row_count), col(row_count), col(MODES, 16)],
        out_shape=[jax.ShapeDtypeStruct((row_count, channels), f32), jax.ShapeDtypeStruct((row_count, channels), f32),
                   jax.ShapeDtypeStruct((MODES, 16, channels), f32)],
        scratch_shapes=[pltpu.VMEM((row_count + 8, LANES), f32), pltpu.VMEM((row_count, LANES), f32)],
        interpret=INTERPRET,
    )(query_proj, key_proj, value_proj, rim, short_filter, amp, lam, skip_gain[None, :], lanes(since), lanes(keep),
      lanes(segkeep))
    own_state = cl[:, SEGMENTS, :]

    def starts_between(low_device, high_device):
        low_row = jnp.maximum(low_device, 0) * row_count
        high_row = (high_device + 1) * row_count
        return jnp.any((doc_starts >= low_row) & (doc_starts < high_row)).astype(jnp.float32)

    summary = own_state
    span = 1
    while 2 * span < ctx_count:
        behind = from_behind(summary, "ctx", span)
        open_path = 1.0 - starts_between(my_index - span + 1, my_index)
        summary = summary + open_path * jnp.exp(float(span * row_count) * log_decay) * behind
        span *= 2
    near = from_behind(summary, "ctx", 1)
    far = from_behind(summary, "ctx", 1 + span)
    open_path = 1.0 - starts_between(my_index - span, my_index - 1)
    incoming = near + open_path * jnp.exp(float(span * row_count) * log_decay) * far

    return pl.pallas_call(
        fix_kernel,
        grid=(tiles,),
        in_specs=[col(row_count), col(row_count), col(MODES, 16), col(MODES), col(MODES), col(MODES),
                  fixed(row_count, LANES), fixed(SEGMENTS, LANES)],
        out_specs=col(row_count),
        out_shape=jax.ShapeDtypeStruct((row_count, channels), jnp.bfloat16),
        interpret=INTERPRET,
    )(acc, q_short, cl, incoming, amp, log_decay, lanes(cont), lanes(opened))


def solution(mesh):
    in_specs = (
        P("ctx", "tp"),
        P("ctx", "tp"),
        P("ctx", "tp"),
        P(None, None, "tp"),
        P(None, "tp"),
        P(None, "tp"),
        P("tp"),
        P(),
    )
    out_specs = P("ctx", "tp")
    return jax.shard_map(body, mesh=mesh, in_specs=in_specs, out_specs=out_specs, check_vma=False)
```

time: 223 us -> 105 us (0.47)
  the two profiles are of different devices: /device:TPU:25 before, /device:TPU:6 now
where the time goes in v2:
time: 105 us; the launch traced here: 104 us
  Pallas kernels  41.7 us (40%)
  waiting for transfers between devices  35.9 us (34%)
  starting transfers between devices  12.2 us (12%)
  local copies, waits for them, and re-layouts  7.06 us (7%)
  other arithmetic  4 us (4%)
  between operations  3.3 us (3%)
    ppermute x7, waiting for transfers between devices, from_behind(): lax.ppermute(value, axis, [(source, source + steps) for source in range(f...  35.9 us
    pallas_call x1, Pallas kernels, body(): pl.pallas_call(local_kernel, grid=(tiles,), in_specs=[col(row_count), col...  29.7 us
    ppermute x7, starting transfers between devices, from_behind(): lax.ppermute(value, axis, [(source, source + steps) for source in range(f...  12.2 us
    pallas_call x1, Pallas kernels, body(): pl.pallas_call(fix_kernel, grid=(tiles,), in_specs=[col(row_count), col(r...  12.1 us
    broadcast_in_dim x5, local copies, waits for them, and re-layouts, lanes(): return jnp.broadcast_to(column[:, None], (column.shape[0], LANES))  3.56 us
    pallas_call x1, local copies, waits for them, and re-layouts, body(): pl.pallas_call(local_kernel, grid=(tiles,), in_specs=[col(row_count), col...  2.81 us
  transfers between devices with their start and end apart: 7, of which 7 were waited for; matrix products, arithmetic and copies ran while one was open for 2% of the time, Pallas kernels for 0%

profile of v2, /device:TPU:6, one launch (start us, length us, event | category | flops | bytes accessed | tf_op | source)
XLA Modules:
  0.0 104.2 jit_solution(16185810181756284424)
XLA Ops:
  0.0 0.0 copy-start.2
  0.0 0.0 copy-start
  0.0 0.0 copy-start.1
  0.0 0.9 pad_maximum_fusion
  0.9 1.9 %collective-permute-start = (bf16[3,6,2048]{2,1,0:T(8,128)(2,1)S(1)}, bf16[3,6,2048]{2,1,0:T(8,128)(2,1)S(1)}, u32[]{:S(2)}, u32[]{:S(2)}) collective-permute-start(bf16[3,6,2048]{2,1,0:T(8,128)(2,1)S(1)} %pad_maximum_fusion), channel_id=1, source_target_pairs={{0,4},{4,8},{8,12},{12,16},{16,20},{20,24},{24,28},{28,32},{32,36}... | collective-permute-start | bytes 221192 | tf_op jit(solution)/shard_map/ppermute | solution.py:20
  2.8 0.0 copy-done.2
  2.8 0.2 reduce-window.9
  3.0 0.8 and_reduce_fusion.2
  3.8 0.1 select_reduce_fusion
  3.9 0.0 copy-done
  3.9 0.0 copy-done.1
  4.0 0.8 negate_log-plus-one_fusion
  4.7 0.2 and_reduce_fusion
  5.0 4.0 %collective-permute-done = bf16[3,6,2048]{2,1,0:T(8,128)(2,1)S(1)} collective-permute-done((bf16[3,6,2048]{2,1,0:T(8,128)(2,1)S(1)}, bf16[3,6,2048]{2,1,0:T(8,128)(2,1)S(1)}, u32[]{:S(2)}, u32[]{:S(2)}) %collective-permute-start) | collective-permute-done | bytes 73760 | tf_op jit(solution)/shard_map/ppermute | solution.py:20
  8.9 0.7 concatenate.3.rim_ref
  9.6 0.7 broadcast_in_dim.24.since_ref
  10.3 0.7 broadcast_in_dim.25.keep_ref
  11.1 0.7 broadcast_in_dim.26.segkeep_ref
  11.7 29.7 %shard_map.82 = (f32[256,2048]{1,0:T(8,128)}, f32[256,2048]{1,0:T(8,128)}, f32[16,16,2048]{2,1,0:T(8,128)}) custom-call(bf16[256,2048]{1,0:T(8,128)(2,1)} %q_ref.1, bf16[256,2048]{1,0:T(8,128)(2,1)} %k_ref.1, bf16[256,2048]{1,0:T(8,128)(2,1)} %v_ref.1, bf16[3,8,2048]{2,1,0:T(8,128)(2,1)} %concatenate.3.rim_ref, f32[3,7,2048]{2,1,0:T(8,128)} %filt_ref.1, ...), custom_call_target="tpu_custom_call" | custom-call | tf_op jit(solution)/shard_map/pallas_call | solution.py:127
  41.4 2.8 %copy.10 = f32[16,16,2048]{2,0,1:T(8,128)S(1)} copy(f32[16,16,2048]{2,1,0:T(8,128)} %get-tuple-element.10.cl_ref) | data formatting | bytes 4194304 | tf_op jit(solution)/shard_map/pallas_call | solution.py:127
  44.2 1.9 %collective-permute-start.1 = (f32[16,2048]{1,0:T(8,128)S(1)}, f32[16,2048]{1,0:T(8,128)S(1)}, u32[]{:S(2)}, u32[]{:S(2)}) collective-permute-start(f32[16,2048]{1,0:T(8,128)S(1)} %slice_bitcast_fusion), channel_id=1, source_target_pairs={{0,4},{4,8},{8,12},{12,16},{16,20},{20,24},{24,28},{28,32},{32,36}... | collective-permute-start | bytes 393224 | tf_op jit(solution)/shard_map/ppermute | solution.py:20
  46.8 5.8 %collective-permute-done.1 = f32[16,2048]{1,0:T(8,128)S(1)} collective-permute-done((f32[16,2048]{1,0:T(8,128)S(1)}, f32[16,2048]{1,0:T(8,128)S(1)}, u32[]{:S(2)}, u32[]{:S(2)}) %collective-permute-start.1) | collective-permute-done | bytes 131104 | tf_op jit(solution)/shard_map/ppermute | solution.py:20
  52.6 0.1 multiply_add_fusion.4
  52.7 1.9 %collective-permute-start.2 = (f32[16,2048]{1,0:T(8,128)S(1)}, f32[16,2048]{1,0:T(8,128)S(1)}, u32[]{:S(2)}, u32[]{:S(2)}) collective-permute-start(f32[16,2048]{1,0:T(8,128)S(1)} %multiply_add_fusion.4), channel_id=1, source_target_pairs={{0,8},{4,12},{8,16},{12,20},{16,24},{20,28},{24,32},{28,36},{32,40... | collective-permute-start | bytes 393224 | tf_op jit(solution)/shard_map/ppermute | solution.py:20
  55.3 6.4 %collective-permute-done.2 = f32[16,2048]{1,0:T(8,128)S(1)} collective-permute-done((f32[16,2048]{1,0:T(8,128)S(1)}, f32[16,2048]{1,0:T(8,128)S(1)}, u32[]{:S(2)}, u32[]{:S(2)}) %collective-permute-start.2) | collective-permute-done | bytes 131104 | tf_op jit(solution)/shard_map/ppermute | solution.py:20
  61.7 0.1 multiply_add_fusion.3
  61.8 1.9 %collective-permute-start.3 = (f32[16,2048]{1,0:T(8,128)S(1)}, f32[16,2048]{1,0:T(8,128)S(1)}, u32[]{:S(2)}, u32[]{:S(2)}) collective-permute-start(f32[16,2048]{1,0:T(8,128)S(1)} %multiply_add_fusion.3), channel_id=1, source_target_pairs={{0,16},{4,20},{8,24},{12,28},{16,32},{20,36},{24,40},{28,44},{32,4... | collective-permute-start | bytes 393224 | tf_op jit(solution)/shard_map/ppermute | solution.py:20
  64.3 7.1 %collective-permute-done.3 = f32[16,2048]{1,0:T(8,128)S(1)} collective-permute-done((f32[16,2048]{1,0:T(8,128)S(1)}, f32[16,2048]{1,0:T(8,128)S(1)}, u32[]{:S(2)}, u32[]{:S(2)}) %collective-permute-start.3) | collective-permute-done | bytes 131104 | tf_op jit(solution)/shard_map/ppermute | solution.py:20
  71.4 0.1 multiply_add_fusion.2
  71.5 1.3 %collective-permute-start.4 = (f32[16,2048]{1,0:T(8,128)S(1)}, f32[16,2048]{1,0:T(8,128)S(1)}, u32[]{:S(2)}, u32[]{:S(2)}) collective-permute-start(f32[16,2048]{1,0:T(8,128)S(1)} %multiply_add_fusion.2), channel_id=1, source_target_pairs={{0,32},{4,36},{8,40},{12,44},{16,48},{20,52},{24,56},{28,60},{32,6... | collective-permute-start | bytes 393224 | tf_op jit(solution)/shard_map/ppermute | solution.py:20
  74.1 4.3 %collective-permute-done.4 = f32[16,2048]{1,0:T(8,128)S(1)} collective-permute-done((f32[16,2048]{1,0:T(8,128)S(1)}, f32[16,2048]{1,0:T(8,128)S(1)}, u32[]{:S(2)}, u32[]{:S(2)}) %collective-permute-start.4) | collective-permute-done | bytes 131104 | tf_op jit(solution)/shard_map/ppermute | solution.py:20
  78.4 0.1 multiply_add_fusion.1
  78.4 1.9 %collective-permute-start.5 = (f32[16,2048]{1,0:T(8,128)S(1)}, f32[16,2048]{1,0:T(8,128)S(1)}, u32[]{:S(2)}, u32[]{:S(2)}) collective-permute-start(f32[16,2048]{1,0:T(8,128)S(1)} %multiply_add_fusion.1), channel_id=1, source_target_pairs={{0,4},{4,8},{8,12},{12,16},{16,20},{20,24},{24,28},{28,32},{32,36}... | collective-permute-start | bytes 393224 | tf_op jit(solution)/shard_map/ppermute | solution.py:20
  80.4 1.3 %collective-permute-start.6 = (f32[16,2048]{1,0:T(8,128)S(1)}, f32[16,2048]{1,0:T(8,128)S(1)}, u32[]{:S(2)}, u32[]{:S(2)}) collective-permute-start(f32[16,2048]{1,0:T(8,128)S(1)} %multiply_add_fusion.1), channel_id=1, source_target_pairs={{0,68},{4,72},{8,76},{12,80},{16,84},{20,88},{24,92},{28,96},{32,1... | collective-permute-start | bytes 393224 | tf_op jit(solution)/shard_map/ppermute | solution.py:20
  81.7 5.2 %collective-permute-done.5 = f32[16,2048]{1,0:T(8,128)S(1)} collective-permute-done((f32[16,2048]{1,0:T(8,128)S(1)}, f32[16,2048]{1,0:T(8,128)S(1)}, u32[]{:S(2)}, u32[]{:S(2)}) %collective-permute-start.5) | collective-permute-done | bytes 131104 | tf_op jit(solution)/shard_map/ppermute | solution.py:20
  86.8 3.1 %collective-permute-done.6 = f32[16,2048]{1,0:T(8,128)S(1)} collective-permute-done((f32[16,2048]{1,0:T(8,128)S(1)}, f32[16,2048]{1,0:T(8,128)S(1)}, u32[]{:S(2)}, u32[]{:S(2)}) %collective-permute-start.6) | collective-permute-done | bytes 131104 | tf_op jit(solution)/shard_map/ppermute | solution.py:20
  90.0 0.7 multiply_add_fusion.hin_ref
  90.7 0.7 broadcast_in_dim.27.cont_ref
  91.5 0.7 broadcast_in_dim.28.open_ref
  92.1 12.1 %shard_map.83 = bf16[256,2048]{1,0:T(8,128)(2,1)} custom-call(f32[256,2048]{1,0:T(8,128)} %get-tuple-element.8.acc_ref, f32[256,2048]{1,0:T(8,128)} %get-tuple-element.9.qs_ref, f32[16,16,2048]{2,1,0:T(8,128)} %get-tuple-element.10.cl_ref, f32[16,2048]{1,0:T(8,128)} %multiply_add_fusion.hin_ref, f32[16,2048]{1,0:T(8,128)} %get-tuple-element.21.amp_ref, ...), custom_call_target="tpu_custom_call" | custom-call | tf_op jit(solution)/shard_map/pallas_call | solution.py:158
  (8 shorter events, 0.1 us)
Async XLA Ops:
  0.0 2.8 %copy-start.2 = (s32[8]{0:T(128)S(1)}, s32[8]{0:T(128)}, u32[]{:S(2)}) copy-start(s32[8]{0:T(128)} %param.15) | copy-start | bytes 100
  0.0 3.9 %copy-start = (f32[16,2048]{1,0:T(8,128)S(1)}, f32[16,2048]{1,0:T(8,128)}, u32[]{:S(2)}) copy-start(f32[16,2048]{1,0:T(8,128)} %param.13) | copy-start | bytes 393220
  0.0 3.9 %copy-start.1 = (f32[16,2048]{1,0:T(8,128)S(1)}, f32[16,2048]{1,0:T(8,128)}, u32[]{:S(2)}) copy-start(f32[16,2048]{1,0:T(8,128)} %param.12) | copy-start | bytes 393220
  0.9 8.0 %collective-permute-start = (bf16[3,6,2048]{2,1,0:T(8,128)(2,1)S(1)}, bf16[3,6,2048]{2,1,0:T(8,128)(2,1)S(1)}, u32[]{:S(2)}, u32[]{:S(2)}) collective-permute-start(bf16[3,6,2048]{2,1,0:T(8,128)(2,1)S(1)} %pad_maximum_fusion), channel_id=1, source_target_pairs={{0,4},{4,8},{8,12},{12,16},{16,20},{20,24},{24,28},{28,32},{32,36}... | collective-permute-start | bytes 221192 | tf_op jit(solution)/shard_map/ppermute | solution.py:20
  44.2 8.4 %collective-permute-start.1 = (f32[16,2048]{1,0:T(8,128)S(1)}, f32[16,2048]{1,0:T(8,128)S(1)}, u32[]{:S(2)}, u32[]{:S(2)}) collective-permute-start(f32[16,2048]{1,0:T(8,128)S(1)} %slice_bitcast_fusion), channel_id=1, source_target_pairs={{0,4},{4,8},{8,12},{12,16},{16,20},{20,24},{24,28},{28,32},{32,36}... | collective-permute-start | bytes 393224 | tf_op jit(solution)/shard_map/ppermute | solution.py:20
  52.7 9.0 %collective-permute-start.2 = (f32[16,2048]{1,0:T(8,128)S(1)}, f32[16,2048]{1,0:T(8,128)S(1)}, u32[]{:S(2)}, u32[]{:S(2)}) collective-permute-start(f32[16,2048]{1,0:T(8,128)S(1)} %multiply_add_fusion.4), channel_id=1, source_target_pairs={{0,8},{4,12},{8,16},{12,20},{16,24},{20,28},{24,32},{28,36},{32,40... | collective-permute-start | bytes 393224 | tf_op jit(solution)/shard_map/ppermute | solution.py:20
  61.8 9.6 %collective-permute-start.3 = (f32[16,2048]{1,0:T(8,128)S(1)}, f32[16,2048]{1,0:T(8,128)S(1)}, u32[]{:S(2)}, u32[]{:S(2)}) collective-permute-start(f32[16,2048]{1,0:T(8,128)S(1)} %multiply_add_fusion.3), channel_id=1, source_target_pairs={{0,16},{4,20},{8,24},{12,28},{16,32},{20,36},{24,40},{28,44},{32,4... | collective-permute-start | bytes 393224 | tf_op jit(solution)/shard_map/ppermute | solution.py:20
  71.5 6.9 %collective-permute-start.4 = (f32[16,2048]{1,0:T(8,128)S(1)}, f32[16,2048]{1,0:T(8,128)S(1)}, u32[]{:S(2)}, u32[]{:S(2)}) collective-permute-start(f32[16,2048]{1,0:T(8,128)S(1)} %multiply_add_fusion.2), channel_id=1, source_target_pairs={{0,32},{4,36},{8,40},{12,44},{16,48},{20,52},{24,56},{28,60},{32,6... | collective-permute-start | bytes 393224 | tf_op jit(solution)/shard_map/ppermute | solution.py:20
  78.4 8.4 %collective-permute-start.5 = (f32[16,2048]{1,0:T(8,128)S(1)}, f32[16,2048]{1,0:T(8,128)S(1)}, u32[]{:S(2)}, u32[]{:S(2)}) collective-permute-start(f32[16,2048]{1,0:T(8,128)S(1)} %multiply_add_fusion.1), channel_id=1, source_target_pairs={{0,4},{4,8},{8,12},{12,16},{16,20},{20,24},{24,28},{28,32},{32,36}... | collective-permute-start | bytes 393224 | tf_op jit(solution)/shard_map/ppermute | solution.py:20
  80.4 9.6 %collective-permute-start.6 = (f32[16,2048]{1,0:T(8,128)S(1)}, f32[16,2048]{1,0:T(8,128)S(1)}, u32[]{:S(2)}, u32[]{:S(2)}) collective-permute-start(f32[16,2048]{1,0:T(8,128)S(1)} %multiply_add_fusion.1), channel_id=1, source_target_pairs={{0,68},{4,72},{8,76},{12,80},{16,84},{20,88},{24,92},{28,96},{32,1... | collective-permute-start | bytes 393224 | tf_op jit(solution)/shard_map/ppermute | solution.py:20

commit v3 on v2

--- a/solution.py
+++ b/solution.py
@@ -21,7 +21,7 @@
 
 
 def local_kernel(q_ref, k_ref, v_ref, rim_ref, filt_ref, amp_ref, lam_ref, skip_ref, since_ref, keep_ref,
-                 segkeep_ref, acc_ref, qs_ref, cl_ref, ext_ref, g_ref):
+                 segkeep_ref, acc_ref, qs_ref, cl_ref, end_ref, ext_ref, g_ref):
     rows = q_ref.shape[0]
     seg_rows = rows // SEGMENTS
     since = since_ref[...]
@@ -64,6 +64,7 @@
             carried = ends[m][p:p + 1, :] + segkeep[p:p + 1, :] * seg_decay * carried
             cl_ref[m, p + 1:p + 2, :] = carried
         cl_ref[m, SEGMENTS + 1:, :] = jnp.zeros((16 - SEGMENTS - 1, LANES), jnp.float32)
+        end_ref[m:m + 1, :] = carried
 
 
 def fix_kernel(acc_ref, qs_ref, cl_ref, hin_ref, amp_ref, logl_ref, cont_ref, open_ref, out_ref):
@@ -86,6 +87,69 @@
             corr = corr + powers[m] * starts[m][p:p + 1, :]
         conv = acc_ref[lo:lo + seg_rows, :] + cont_ref[lo:lo + seg_rows, :] * corr
         out_ref[lo:lo + seg_rows, :] = (qs_ref[lo:lo + seg_rows, :] * conv).astype(out_ref.dtype)
+
+
+def scan_kernel(count, spans, own_ref, fac_ref, out_ref, sums, slots, send_sems, recv_sems):
+    me = lax.axis_index("ctx")
+    lane = lax.axis_index("tp")
+    last = spans[-1] * 2 if spans else 1
+    offsets = sorted(set(spans) | {1, 1 + last})
+    barrier = pltpu.get_barrier_semaphore()
+    for d in offsets:
+        for other in (me - d, me + d):
+            @pl.when((other >= 0) & (other < count))
+            def _():
+                pl.semaphore_signal(barrier, inc=1, device_id=(other, lane), device_id_type=pl.DeviceIdType.MESH)
+    partners = 0
+    for d in offsets:
+        partners = partners + (me + count - d) // count + (2 * count - 1 - me - d) // count
+    pl.semaphore_wait(barrier, partners)
+
+    def transfer(src, slot, target):
+        return pltpu.make_async_remote_copy(
+            src_ref=src, dst_ref=slots.at[slot], send_sem=send_sems.at[slot], recv_sem=recv_sems.at[slot],
+            device_id=(target, lane), device_id_type=pl.DeviceIdType.MESH)
+
+    def exchange(src, sends):
+        for slot, d in sends:
+            @pl.when(me + d < count)
+            def _():
+                transfer(src, slot, me + d).start()
+
+    def settle(src, sends):
+        for slot, d in sends:
+            @pl.when(me + d < count)
+            def _():
+                transfer(src, slot, me + d).wait_send()
+
+    current = own_ref
+    for r, d in enumerate(spans):
+        exchange(current, [(r, d)])
+        @pl.when(me - d >= 0)
+        def _():
+            transfer(current, r, me - d).wait_recv()
+            sums[r] = current[...] + fac_ref[r] * slots[r]
+
+        @pl.when(me - d < 0)
+        def _():
+            sums[r] = current[...]
+        settle(current, [(r, d)])
+        current = sums.at[r]
+    near, far = len(spans), len(spans) + 1
+    final = [(near, 1), (far, 1 + last)]
+    exchange(current, final)
+    out_ref[...] = jnp.zeros(out_ref.shape, out_ref.dtype)
+
+    @pl.when(me - 1 >= 0)
+    def _():
+        transfer(current, near, me - 1).wait_recv()
+        out_ref[...] = slots[near]
+
+    @pl.when(me - 1 - last >= 0)
+    def _():
+        transfer(current, far, me - 1 - last).wait_recv()
+        out_ref[...] = out_ref[...] + fac_ref[len(spans)] * slots[far]
+    settle(current, final)
 
 
 def body(query_proj, key_proj, value_proj, short_filter, residues, decay_rate, skip_gain, doc_lengths):
@@ -124,36 +188,51 @@
     col = lambda *lead: pl.BlockSpec(tuple(lead) + (LANES,), lambda c: (0,) * len(lead) + (c,))
     fixed = lambda *shape: pl.BlockSpec(shape, lambda c: (0,) * len(shape))
     f32 = jnp.float32
-    acc, q_short, cl = pl.pallas_call(
+    acc, q_short, cl, own_state = pl.pallas_call(
         local_kernel,
         grid=(tiles,),
         in_specs=[col(row_count), col(row_count), col(row_count), col(3, 8), col(3, TAPS), col(MODES), col(MODES),
                   col(1), fixed(row_count, LANES), fixed(row_count, LANES), fixed(SEGMENTS, LANES)],
-        out_specs=[col(row_count), col(row_count), col(MODES, 16)],
+        out_specs=[col(row_count), col(row_count), col(MODES, 16), col(MODES)],
         out_shape=[jax.ShapeDtypeStruct((row_count, channels), f32), jax.ShapeDtypeStruct((row_count, channels), f32),
-                   jax.ShapeDtypeStruct((MODES, 16, channels), f32)],
+                   jax.ShapeDtypeStruct((MODES, 16, channels), f32), jax.ShapeDtypeStruct((MODES, channels), f32)],
         scratch_shapes=[pltpu.VMEM((row_count + 8, LANES), f32), pltpu.VMEM((row_count, LANES), f32)],
         interpret=INTERPRET,
     )(query_proj, key_proj, value_proj, rim, short_filter, amp, lam, skip_gain[None, :], lanes(since), lanes(keep),
       lanes(segkeep))
-    own_state = cl[:, SEGMENTS, :]
 
     def starts_between(low_device, high_device):
         low_row = jnp.maximum(low_device, 0) * row_count
         high_row = (high_device + 1) * row_count
         return jnp.any((doc_starts >= low_row) & (doc_starts < high_row)).astype(jnp.float32)
 
-    summary = own_state
+    spans = []
     span = 1
     while 2 * span < ctx_count:
-        behind = from_behind(summary, "ctx", span)
-        open_path = 1.0 - starts_between(my_index - span + 1, my_index)
-        summary = summary + open_path * jnp.exp(float(span * row_count) * log_decay) * behind
+        spans.append(span)
         span *= 2
-    near = from_behind(summary, "ctx", 1)
-    far = from_behind(summary, "ctx", 1 + span)
+    factors = []
+    for d in spans:
+        open_path = 1.0 - starts_between(my_index - d + 1, my_index)
+        factors.append(open_path * jnp.exp(float(d * row_count) * log_decay))
     open_path = 1.0 - starts_between(my_index - span, my_index - 1)
-    incoming = near + open_path * jnp.exp(float(span * row_count) * log_decay) * far
+    factors.append(open_path * jnp.exp(float(span * row_count) * log_decay))
+    factors = jnp.stack(factors)
+    vmem = pl.BlockSpec(memory_space=pltpu.VMEM)
+    incoming = pl.pallas_call(
+        functools.partial(scan_kernel, ctx_count, tuple(spans)),
+        out_shape=jax.ShapeDtypeStruct((MODES, channels), f32),
+        in_specs=[vmem, vmem],
+        out_specs=vmem,
+        scratch_shapes=[
+            pltpu.VMEM((len(spans), MODES, channels), f32),
+            pltpu.VMEM((len(spans) + 2, MODES, channels), f32),
+            pltpu.SemaphoreType.DMA((len(spans) + 2,)),
+            pltpu.SemaphoreType.DMA((len(spans) + 2,)),
+        ],
+        compiler_params=pltpu.CompilerParams(collective_id=0, has_side_effects=True),
+        interpret=INTERPRET,
+    )(own_state, factors)
 
     return pl.pallas_call(
         fix_kernel,

time: 105 us -> 83.4 us (0.79)
  the two profiles are of different devices: /device:TPU:6 before, /device:TPU:31 now
where the time goes in v3:
time: 83.4 us; the launch traced here: 82.9 us
  Pallas kernels  70.6 us (85%)
  local copies, waits for them, and re-layouts  4.33 us (5%)
  other arithmetic  3.35 us (4%)
  between operations  3.32 us (4%)
  starting transfers between devices  1.29 us (2%)
    pallas_call x1, Pallas kernels, body(): pl.pallas_call(local_kernel, grid=(tiles,), in_specs=[col(row_count), col...  29.7 us
    pallas_call x1, Pallas kernels, body(): pl.pallas_call(functools.partial(scan_kernel, ctx_count, tuple(spans)), o...  28.9 us
    pallas_call x1, Pallas kernels, body(): pl.pallas_call(fix_kernel, grid=(tiles,), in_specs=[col(row_count), col(r...  12.1 us
    broadcast_in_dim x5, local copies, waits for them, and re-layouts, lanes(): return jnp.broadcast_to(column[:, None], (column.shape[0], LANES))  3.56 us
  transfers between devices with their start and end apart: 1, of which 0 were waited for; matrix products, arithmetic and copies ran while one was open for 3% of the time, Pallas kernels for 0%

profile of v3, /device:TPU:31, one launch (start us, length us, event | category | flops | bytes accessed | tf_op | source)
XLA Modules:
  0.0 82.9 jit_solution(9157274880696979179)
XLA Ops:
  0.0 0.0 copy-start.3
  0.0 0.0 copy-start
  0.0 0.0 copy-start.2
  0.0 0.9 %pad_maximum_fusion = bf16[3,6,2048]{2,1,0:T(8,128)(2,1)S(1)} fusion(bf16[1,256,2048]{2,1,0:T(8,128)(2,1)} %bitcast.20, bf16[1,256,2048]{2,1,0:T(8,128)(2,1)} %bitcast.19, bf16[1,256,2048]{2,1,0:T(8,128)(2,1)} %bitcast.18), kind=kLoop, calls=%fused_computation.9 | loop fusion | flops 221184 | bytes 3219456 | tf_op jit(solution)/shard_map/stack | solution.py:181
  0.9 1.3 %collective-permute-start = (bf16[3,6,2048]{2,1,0:T(8,128)(2,1)S(1)}, bf16[3,6,2048]{2,1,0:T(8,128)(2,1)S(1)}, u32[]{:S(2)}, u32[]{:S(2)}) collective-permute-start(bf16[3,6,2048]{2,1,0:T(8,128)(2,1)S(1)} %pad_maximum_fusion), channel_id=1, source_target_pairs={{0,4},{4,8},{8,12},{12,16},{16,20},{20,24},{24,28},{28,32},{32,36}... | collective-permute-start | bytes 221192 | tf_op jit(solution)/shard_map/ppermute | solution.py:20
  2.2 0.0 copy-done.3
  2.2 0.2 reduce-window.9
  2.4 0.8 and_reduce_fusion.2
  3.2 0.1 select_reduce_fusion
  6.4 0.2 and_reduce_fusion
  6.7 0.0 copy-done
  6.7 0.0 copy-done.2
  6.7 0.8 negate_log-plus-one_fusion
  7.5 0.1 bitcast_dynamic-update-slice_fusion.4
  7.6 0.1 bitcast_dynamic-update-slice_fusion.3
  7.7 0.1 bitcast_dynamic-update-slice_fusion.2
  7.8 0.1 bitcast_dynamic-update-slice_fusion.1
  7.8 0.1 bitcast_dynamic-update-slice_fusion.fac_ref
  7.9 0.0 copy-start.1
  7.9 0.0 collective-permute-done
  8.0 0.8 concatenate.3.rim_ref
  8.7 0.7 broadcast_in_dim.26.segkeep_ref
  9.4 0.7 broadcast_in_dim.24.since_ref
  10.1 0.8 broadcast_in_dim.25.keep_ref
  10.9 29.7 %shard_map.82 = (f32[256,2048]{1,0:T(8,128)}, f32[256,2048]{1,0:T(8,128)}, f32[16,16,2048]{2,1,0:T(8,128)}, f32[16,2048]{1,0:T(8,128)}) custom-call(bf16[256,2048]{1,0:T(8,128)(2,1)} %q_ref.1, bf16[256,2048]{1,0:T(8,128)(2,1)} %k_ref.1, bf16[256,2048]{1,0:T(8,128)(2,1)} %v_ref.1, bf16[3,8,2048]{2,1,0:T(8,128)(2,1)} %concatenate.3.rim_ref, ...), custom_call_target="tpu_custom_call" | custom-call | tf_op jit(solution)/shard_map/pallas_call | solution.py:191
  40.5 0.0 copy-done.1
  40.5 28.9 %shard_map.83.hin_ref = f32[16,2048]{1,0:T(8,128)} custom-call(f32[16,2048]{1,0:T(8,128)} %get-tuple-element.12.own_ref, f32[5,16,2048]{2,1,0:T(8,128)} %copy-done.1), custom_call_target="tpu_custom_call" | custom-call | tf_op jit(solution)/shard_map/pallas_call | solution.py:222
  69.4 0.7 broadcast_in_dim.28.open_ref
  70.1 0.7 broadcast_in_dim.27.cont_ref
  70.9 12.1 %shard_map.84 = bf16[256,2048]{1,0:T(8,128)(2,1)} custom-call(f32[256,2048]{1,0:T(8,128)} %get-tuple-element.9.acc_ref, f32[256,2048]{1,0:T(8,128)} %get-tuple-element.10.qs_ref, f32[16,16,2048]{2,1,0:T(8,128)} %get-tuple-element.11.cl_ref, f32[16,2048]{1,0:T(8,128)} %shard_map.83.hin_ref, f32[16,2048]{1,0:T(8,128)} %get-tuple-element.23.amp_ref, ...), custom_call_target="tpu_custom_call" | custom-call | tf_op jit(solution)/shard_map/pallas_call | solution.py:237
  (7 shorter events, 0.0 us)
Async XLA Ops:
  0.0 2.2 %copy-start.3 = (s32[8]{0:T(128)S(1)}, s32[8]{0:T(128)}, u32[]{:S(2)}) copy-start(s32[8]{0:T(128)} %param.15) | copy-start | bytes 100
  0.0 6.7 %copy-start = (f32[16,2048]{1,0:T(8,128)S(1)}, f32[16,2048]{1,0:T(8,128)}, u32[]{:S(2)}) copy-start(f32[16,2048]{1,0:T(8,128)} %param.13) | copy-start | bytes 393220
  0.0 6.7 %copy-start.2 = (f32[16,2048]{1,0:T(8,128)S(1)}, f32[16,2048]{1,0:T(8,128)}, u32[]{:S(2)}) copy-start(f32[16,2048]{1,0:T(8,128)} %param.12) | copy-start | bytes 393220
  0.9 7.1 %collective-permute-start = (bf16[3,6,2048]{2,1,0:T(8,128)(2,1)S(1)}, bf16[3,6,2048]{2,1,0:T(8,128)(2,1)S(1)}, u32[]{:S(2)}, u32[]{:S(2)}) collective-permute-start(bf16[3,6,2048]{2,1,0:T(8,128)(2,1)S(1)} %pad_maximum_fusion), channel_id=1, source_target_pairs={{0,4},{4,8},{8,12},{12,16},{16,20},{20,24},{24,28},{28,32},{32,36}... | collective-permute-start | bytes 221192 | tf_op jit(solution)/shard_map/ppermute | solution.py:20
  7.9 32.6 %copy-start.1 = (f32[5,16,2048]{2,1,0:T(8,128)}, f32[5,16,2048]{2,1,0:T(8,128)S(1)}, u32[]{:S(2)}) copy-start(f32[5,16,2048]{2,1,0:T(8,128)S(1)} %bitcast_dynamic-update-slice_fusion.fac_ref) | copy-start | bytes 1966084

commit v4 on v3

--- a/solution.py
+++ b/solution.py
@@ -10,6 +10,7 @@
 MODES = 16
 TAPS = 7
 LANES = 128
+LANES_FIX = 256
 SEGMENTS = 8
 INTERPRET = False
 
@@ -20,14 +21,15 @@
     return lax.ppermute(value, axis, [(source, source + steps) for source in range(first, last)])
 
 
-def local_kernel(q_ref, k_ref, v_ref, rim_ref, filt_ref, amp_ref, lam_ref, skip_ref, since_ref, keep_ref,
-                 segkeep_ref, acc_ref, qs_ref, cl_ref, end_ref, ext_ref, g_ref):
+def local_kernel(q_ref, k_ref, v_ref, rim_ref, filt_ref, amp_ref, lam_ref, skip_ref, mask_ref,
+                 acc_ref, qs_ref, cl_ref, end_ref, ext_ref, g_ref):
+    since_ref, keep_ref = mask_ref.at[0], mask_ref.at[1]
     rows = q_ref.shape[0]
     seg_rows = rows // SEGMENTS
     since = since_ref[...]
     filtered = []
     for branch, src in enumerate((q_ref, k_ref, v_ref)):
-        ext_ref[0:8, :] = rim_ref[branch].astype(jnp.float32)
+        ext_ref[8 - TAPS + 1:8, :] = rim_ref[branch].astype(jnp.float32)
         ext_ref[8:8 + rows, :] = src[...].astype(jnp.float32)
         total = jnp.zeros((rows, LANES), jnp.float32)
         for lag in range(TAPS):
@@ -55,7 +57,7 @@
 
     zero = jnp.zeros((SEGMENTS, LANES), jnp.float32)
     ends = lax.fori_loop(0, seg_rows, step, tuple([zero] * MODES))
-    segkeep = segkeep_ref[...]
+    segkeep = mask_ref[3, 0:SEGMENTS, :]
     for m in range(MODES):
         seg_decay = jnp.exp(float(seg_rows) * jnp.log(lam_ref[m:m + 1, :]))
         carried = jnp.zeros((1, LANES), jnp.float32)
@@ -67,12 +69,14 @@
         end_ref[m:m + 1, :] = carried
 
 
-def fix_kernel(acc_ref, qs_ref, cl_ref, hin_ref, amp_ref, logl_ref, cont_ref, open_ref, out_ref):
-    rows = acc_ref.shape[0]
+def fix_kernel(acc_ref, qs_ref, cl_ref, hin_ref, amp_ref, logl_ref, mask_ref, out_ref):
+    rows, width = acc_ref.shape
     seg_rows = rows // SEGMENTS
-    seg_index = lax.broadcasted_iota(jnp.int32, (SEGMENTS, LANES), 0).astype(jnp.float32)
-    lag_index = lax.broadcasted_iota(jnp.int32, (seg_rows, LANES), 0).astype(jnp.float32) + 1.0
-    opened = open_ref[...]
+    copies = width // LANES
+    widen = lambda part: jnp.concatenate([part] * copies, axis=1) if copies > 1 else part
+    seg_index = lax.broadcasted_iota(jnp.int32, (SEGMENTS, width), 0).astype(jnp.float32)
+    lag_index = lax.broadcasted_iota(jnp.int32, (seg_rows, width), 0).astype(jnp.float32) + 1.0
+    opened = widen(mask_ref[3, 8:8 + SEGMENTS, :])
     starts = []
     powers = []
     for m in range(MODES):
@@ -82,10 +86,10 @@
         powers.append(amp_ref[m:m + 1, :] * jnp.exp(lag_index * logl))
     for p in range(SEGMENTS):
         lo = p * seg_rows
-        corr = jnp.zeros((seg_rows, LANES), jnp.float32)
+        corr = jnp.zeros((seg_rows, width), jnp.float32)
         for m in range(MODES):
             corr = corr + powers[m] * starts[m][p:p + 1, :]
-        conv = acc_ref[lo:lo + seg_rows, :] + cont_ref[lo:lo + seg_rows, :] * corr
+        conv = acc_ref[lo:lo + seg_rows, :] + widen(mask_ref[2, lo:lo + seg_rows, :]) * corr
         out_ref[lo:lo + seg_rows, :] = (qs_ref[lo:lo + seg_rows, :] * conv).astype(out_ref.dtype)
 
 
@@ -175,12 +179,11 @@
     before = (doc_starts[None, :] >= first_row) & (doc_starts[None, :] < seg_lo[:, None])
     opened = 1.0 - jnp.any(before, axis=1).astype(jnp.float32)
 
-    def lanes(column):
-        return jnp.broadcast_to(column[:, None], (column.shape[0], LANES))
+    small = jnp.zeros((row_count,), jnp.float32).at[0:SEGMENTS].set(segkeep).at[8:8 + SEGMENTS].set(opened)
+    masks = jnp.broadcast_to(jnp.stack([since, keep, cont, small])[:, :, None], (4, row_count, LANES))
 
     stacked = jnp.stack([query_proj, key_proj, value_proj])
     rim = from_behind(stacked[:, row_count - TAPS + 1:, :], "ctx", 1)
-    rim = jnp.concatenate([jnp.zeros((3, 8 - TAPS + 1, channels), rim.dtype), rim], axis=1)
     log_decay = jnp.log1p(-decay_rate)
     lam = jnp.exp(log_decay)
     amp = residues * jnp.sqrt(decay_rate * (2.0 - decay_rate))
@@ -191,15 +194,14 @@
     acc, q_short, cl, own_state = pl.pallas_call(
         local_kernel,
         grid=(tiles,),
-        in_specs=[col(row_count), col(row_count), col(row_count), col(3, 8), col(3, TAPS), col(MODES), col(MODES),
-                  col(1), fixed(row_count, LANES), fixed(row_count, LANES), fixed(SEGMENTS, LANES)],
+        in_specs=[col(row_count), col(row_count), col(row_count), col(3, TAPS - 1), col(3, TAPS), col(MODES), col(MODES),
+                  col(1), fixed(4, row_count, LANES)],
         out_specs=[col(row_count), col(row_count), col(MODES, 16), col(MODES)],
         out_shape=[jax.ShapeDtypeStruct((row_count, channels), f32), jax.ShapeDtypeStruct((row_count, channels), f32),
                    jax.ShapeDtypeStruct((MODES, 16, channels), f32), jax.ShapeDtypeStruct((MODES, channels), f32)],
         scratch_shapes=[pltpu.VMEM((row_count + 8, LANES), f32), pltpu.VMEM((row_count, LANES), f32)],
         interpret=INTERPRET,
-    )(query_proj, key_proj, value_proj, rim, short_filter, amp, lam, skip_gain[None, :], lanes(since), lanes(keep),
-      lanes(segkeep))
+    )(query_proj, key_proj, value_proj, rim, short_filter, amp, lam, skip_gain[None, :], masks)
 
     def starts_between(low_device, high_device):
         low_row = jnp.maximum(low_device, 0) * row_count
@@ -234,15 +236,16 @@
         interpret=INTERPRET,
     )(own_state, factors)
 
+    wide = lambda *lead: pl.BlockSpec(tuple(lead) + (LANES_FIX,), lambda c: (0,) * len(lead) + (c,))
     return pl.pallas_call(
         fix_kernel,
-        grid=(tiles,),
-        in_specs=[col(row_count), col(row_count), col(MODES, 16), col(MODES), col(MODES), col(MODES),
-                  fixed(row_count, LANES), fixed(SEGMENTS, LANES)],
-        out_specs=col(row_count),
+        grid=(channels // LANES_FIX,),
+        in_specs=[wide(row_count), wide(row_count), wide(MODES, 16), wide(MODES), wide(MODES), wide(MODES),
+                  fixed(4, row_count, LANES)],
+        out_specs=wide(row_count),
         out_shape=jax.ShapeDtypeStruct((row_count, channels), jnp.bfloat16),
         interpret=INTERPRET,
-    )(acc, q_short, cl, incoming, amp, log_decay, lanes(cont), lanes(opened))
+    )(acc, q_short, cl, incoming, amp, log_decay, masks)
 
 
 def solution(mesh):

time: 83.4 us -> 76.5 us (0.917)
  Pallas kernels: 70.6 us -> 66.8 us
  local copies, waits for them, and re-layouts: 4.33 us -> 1.3 us
    pallas_call x1, Pallas kernels: 12.1 us -> 8.3 us  [body(): pl.pallas_call(fix_kernel, grid=(channels // LANES_FIX,), in_specs=[wide(...]
    broadcast_in_dim x5 -> x1, local copies, waits for them, and re-layouts: 3.56 us -> 1.01 us  [body(): jnp.broadcast_to(jnp.stack([since, keep, cont, small])[:, :, None], (4, r...]
  transfers between devices with their start and end apart: 1 -> 1, of which waited for: 0 -> 0; matrix products, arithmetic and copies ran while one was open for 3% -> 4% of each run, Pallas kernels for 0% -> 0%
where the time goes in v4:
time: 76.5 us; the launch traced here: 76.1 us
  Pallas kernels  66.8 us (87%)
  other arithmetic  3.36 us (4%)
  between operations  3.35 us (4%)
  local copies, waits for them, and re-layouts  1.3 us (2%)
  starting transfers between devices  1.29 us (2%)
    pallas_call x1, Pallas kernels, body(): pl.pallas_call(local_kernel, grid=(tiles,), in_specs=[col(row_count), col...  29.6 us
    pallas_call x1, Pallas kernels, body(): pl.pallas_call(functools.partial(scan_kernel, ctx_count, tuple(spans)), o...  28.9 us
    pallas_call x1, Pallas kernels, body(): pl.pallas_call(fix_kernel, grid=(channels // LANES_FIX,), in_specs=[wide(...  8.3 us
  transfers between devices with their start and end apart: 1, of which 0 were waited for; matrix products, arithmetic and copies ran while one was open for 4% of the time, Pallas kernels for 0%

profile of v4, /device:TPU:31, one launch (start us, length us, event | category | flops | bytes accessed | tf_op | source)
XLA Modules:
  0.0 76.1 jit_solution(3199403926515534588)
XLA Ops:
  0.0 0.0 copy-start.4
  0.0 0.0 copy-start
  0.0 0.0 copy-start.2
  0.0 0.9 %pad_maximum_fusion = bf16[3,6,2048]{2,1,0:T(8,128)(2,1)S(1)} fusion(bf16[1,256,2048]{2,1,0:T(8,128)(2,1)} %bitcast.24, bf16[1,256,2048]{2,1,0:T(8,128)(2,1)} %bitcast.23, bf16[1,256,2048]{2,1,0:T(8,128)(2,1)} %bitcast.22), kind=kLoop, calls=%fused_computation.9 | loop fusion | flops 221184 | bytes 3219456 | tf_op jit(solution)/shard_map/stack | solution.py:185
  0.9 1.3 %collective-permute-start = (bf16[3,6,2048]{2,1,0:T(8,128)(2,1)S(1)}, bf16[3,6,2048]{2,1,0:T(8,128)(2,1)S(1)}, u32[]{:S(2)}, u32[]{:S(2)}) collective-permute-start(bf16[3,6,2048]{2,1,0:T(8,128)(2,1)S(1)} %pad_maximum_fusion), channel_id=1, source_target_pairs={{0,4},{4,8},{8,12},{12,16},{16,20},{20,24},{24,28},{28,32},{32,36}... | collective-permute-start | bytes 221192 | tf_op jit(solution)/shard_map/ppermute | solution.py:21
  2.2 0.0 copy-done.4
  2.2 0.2 reduce-window.9
  2.4 0.8 %and_reduce_fusion.2 = (pred[]{:T(512)}, pred[]{:T(512)}, pred[]{:T(512)}, pred[]{:T(512)}, pred[]{:T(512)}, /*index=5*/s32[8]{0:T(128)S(1)}) fusion(s32[]{:T(128)S(6)} %mul.138, s32[]{:T(128)S(6)} %mul.114, s32[]{:T(128)S(6)} %mul.118, s32[]{:T(128)S(6)} %mul.133, s32[]{:T(128)S(6)} %mul.128, s32[]{:T(128)S(6)} %mul.123, s32[]{:T(128)S(6)} %mul.117, ...), kind=kLoop, calls=%fused_computation.21 | loop fusion | flops 139 | bytes 129 | tf_op jit(solution)/shard_map/reduce_or | solution.py:209
  3.2 0.1 select_reduce_fusion
  6.5 0.2 and_reduce_fusion
  6.7 0.0 copy-done
  6.7 0.0 copy-done.2
  6.7 0.8 %negate_log-plus-one_fusion = (f32[16,2048]{1,0:T(8,128)}, f32[16,2048]{1,0:T(8,128)}, f32[16,2048]{1,0:T(8,128)}) fusion(f32[16,2048]{1,0:T(8,128)S(1)} %copy-done, f32[16,2048]{1,0:T(8,128)S(1)} %copy-done.2), kind=kLoop, calls=%fused_computation.8 | loop fusion | flops 131072 | bytes 655360 | tf_op jit(solution)/shard_map/log1p | solution.py:187
  7.5 0.1 bitcast_dynamic-update-slice_fusion.4
  7.6 0.1 bitcast_dynamic-update-slice_fusion.3
  7.7 0.1 bitcast_dynamic-update-slice_fusion.2
  7.8 0.1 bitcast_dynamic-update-slice_fusion.1
  7.9 0.1 bitcast_dynamic-update-slice_fusion.fac_ref
  7.9 0.0 copy-start.1
  8.0 0.3 scatter.9
  8.2 0.0 collective-permute-done.rim_ref
  8.3 0.0 copy-start.3
  8.3 1.0 %broadcast_in_dim.16.mask_ref = f32[4,256,128]{2,1,0:T(8,128)} broadcast(f32[4,256]{1,0:T(4,128)S(1)} %pad_maximum_fusion.2), dimensions={0,1} | broadcast | bytes 528384 | tf_op jit(solution)/shard_map/broadcast_in_dim | solution.py:183
  9.3 0.0 copy-done.3
  9.3 29.6 %shard_map.82 = (f32[256,2048]{1,0:T(8,128)}, f32[256,2048]{1,0:T(8,128)}, f32[16,16,2048]{2,1,0:T(8,128)}, f32[16,2048]{1,0:T(8,128)}) custom-call(bf16[256,2048]{1,0:T(8,128)(2,1)} %q_ref.1, bf16[256,2048]{1,0:T(8,128)(2,1)} %k_ref.1, bf16[256,2048]{1,0:T(8,128)(2,1)} %v_ref.1, bf16[3,6,2048]{2,1,0:T(8,128)(2,1)} %copy-done.3, f32[3,7,2048]{2,1,0:T(8,128)} %filt_ref.1, ...), custom_call_target="tpu_custom_call" | custom-call | tf_op jit(solution)/shard_map/pallas_call | solution.py:194
  38.9 0.0 copy-done.1
  38.9 28.9 %shard_map.83.hin_ref = f32[16,2048]{1,0:T(8,128)} custom-call(f32[16,2048]{1,0:T(8,128)} %get-tuple-element.36.own_ref, f32[5,16,2048]{2,1,0:T(8,128)} %copy-done.1), custom_call_target="tpu_custom_call" | custom-call | tf_op jit(solution)/shard_map/pallas_call | solution.py:224
  67.8 8.3 %shard_map.84 = bf16[256,2048]{1,0:T(8,128)(2,1)} custom-call(f32[256,2048]{1,0:T(8,128)} %get-tuple-element.33.acc_ref, f32[256,2048]{1,0:T(8,128)} %get-tuple-element.34.qs_ref, f32[16,16,2048]{2,1,0:T(8,128)} %get-tuple-element.35.cl_ref, f32[16,2048]{1,0:T(8,128)} %shard_map.83.hin_ref, f32[16,2048]{1,0:T(8,128)} %get-tuple-element.47.amp_ref, ...), custom_call_target="tpu_custom_call" | custom-call | tf_op jit(solution)/shard_map/pallas_call | solution.py:240
  (9 shorter events, 0.1 us)
Async XLA Ops:
  0.0 2.2 %copy-start.4 = (s32[8]{0:T(128)S(1)}, s32[8]{0:T(128)}, u32[]{:S(2)}) copy-start(s32[8]{0:T(128)} %param.19) | copy-start | bytes 100
  0.0 6.7 %copy-start = (f32[16,2048]{1,0:T(8,128)S(1)}, f32[16,2048]{1,0:T(8,128)}, u32[]{:S(2)}) copy-start(f32[16,2048]{1,0:T(8,128)} %param.17) | copy-start | bytes 393220
  0.0 6.7 %copy-start.2 = (f32[16,2048]{1,0:T(8,128)S(1)}, f32[16,2048]{1,0:T(8,128)}, u32[]{:S(2)}) copy-start(f32[16,2048]{1,0:T(8,128)} %param.16) | copy-start | bytes 393220
  0.9 7.4 %collective-permute-start = (bf16[3,6,2048]{2,1,0:T(8,128)(2,1)S(1)}, bf16[3,6,2048]{2,1,0:T(8,128)(2,1)S(1)}, u32[]{:S(2)}, u32[]{:S(2)}) collective-permute-start(bf16[3,6,2048]{2,1,0:T(8,128)(2,1)S(1)} %pad_maximum_fusion), channel_id=1, source_target_pairs={{0,4},{4,8},{8,12},{12,16},{16,20},{20,24},{24,28},{28,32},{32,36}... | collective-permute-start | bytes 221192 | tf_op jit(solution)/shard_map/ppermute | solution.py:21
  7.9 30.9 %copy-start.1 = (f32[5,16,2048]{2,1,0:T(8,128)}, f32[5,16,2048]{2,1,0:T(8,128)S(1)}, u32[]{:S(2)}) copy-start(f32[5,16,2048]{2,1,0:T(8,128)S(1)} %bitcast_dynamic-update-slice_fusion.fac_ref) | copy-start | bytes 1966084
  8.3 1.0 %copy-start.3 = (bf16[3,6,2048]{2,1,0:T(8,128)(2,1)}, bf16[3,6,2048]{2,1,0:T(8,128)(2,1)S(1)}, u32[]{:S(2)}) copy-start(bf16[3,6,2048]{2,1,0:T(8,128)(2,1)S(1)} %collective-permute-done.rim_ref) | copy-start | bytes 221188

commit v5 on v4

--- a/solution.py
+++ b/solution.py
@@ -93,11 +93,10 @@
         out_ref[lo:lo + seg_rows, :] = (qs_ref[lo:lo + seg_rows, :] * conv).astype(out_ref.dtype)
 
 
-def scan_kernel(count, spans, own_ref, fac_ref, out_ref, sums, slots, send_sems, recv_sems):
+def scan_kernel(count, rounds, span, own_ref, fac_ref, out_ref, sums, slots, send_sems, recv_sems):
     me = lax.axis_index("ctx")
     lane = lax.axis_index("tp")
-    last = spans[-1] * 2 if spans else 1
-    offsets = sorted(set(spans) | {1, 1 + last})
+    offsets = sorted({k * d for d, radix in rounds for k in range(1, radix)} | {1, 1 + span})
     barrier = pltpu.get_barrier_semaphore()
     for d in offsets:
         for other in (me - d, me + d):
@@ -126,33 +125,27 @@
             def _():
                 transfer(src, slot, me + d).wait_send()
 
+    def gather(src, dst, sends, first):
+        for slot, d in sends:
+            @pl.when(me - d >= 0)
+            def _():
+                transfer(src, slot, me - d).wait_recv()
+                dst[...] = dst[...] + fac_ref[slot] * slots[slot]
+
     current = own_ref
-    for r, d in enumerate(spans):
-        exchange(current, [(r, d)])
-        @pl.when(me - d >= 0)
-        def _():
-            transfer(current, r, me - d).wait_recv()
-            sums[r] = current[...] + fac_ref[r] * slots[r]
-
-        @pl.when(me - d < 0)
-        def _():
-            sums[r] = current[...]
-        settle(current, [(r, d)])
+    slot = 0
+    for r, (d, radix) in enumerate(rounds):
+        sends = [(slot + k - 1, k * d) for k in range(1, radix)]
+        slot += radix - 1
+        exchange(current, sends)
+        sums[r] = current[...]
+        gather(current, sums.at[r], sends, True)
+        settle(current, sends)
         current = sums.at[r]
-    near, far = len(spans), len(spans) + 1
-    final = [(near, 1), (far, 1 + last)]
+    final = [(slot, 1), (slot + 1, 1 + span)]
     exchange(current, final)
     out_ref[...] = jnp.zeros(out_ref.shape, out_ref.dtype)
-
-    @pl.when(me - 1 >= 0)
-    def _():
-        transfer(current, near, me - 1).wait_recv()
-        out_ref[...] = slots[near]
-
-    @pl.when(me - 1 - last >= 0)
-    def _():
-        transfer(current, far, me - 1 - last).wait_recv()
-        out_ref[...] = out_ref[...] + fac_ref[len(spans)] * slots[far]
+    gather(current, out_ref, final, False)
     settle(current, final)
 
 
@@ -208,29 +201,33 @@
         high_row = (high_device + 1) * row_count
         return jnp.any((doc_starts >= low_row) & (doc_starts < high_row)).astype(jnp.float32)
 
-    spans = []
+    rounds = []
     span = 1
     while 2 * span < ctx_count:
-        spans.append(span)
-        span *= 2
+        radix = max(2, min(4, -(-(ctx_count // 2) // span)))
+        rounds.append((span, radix))
+        span *= radix
     factors = []
-    for d in spans:
-        open_path = 1.0 - starts_between(my_index - d + 1, my_index)
-        factors.append(open_path * jnp.exp(float(d * row_count) * log_decay))
+    for d, radix in rounds:
+        for k in range(1, radix):
+            open_path = 1.0 - starts_between(my_index - k * d + 1, my_index)
+            factors.append(open_path * jnp.exp(float(k * d * row_count) * log_decay))
+    factors.append(jnp.ones_like(log_decay))
     open_path = 1.0 - starts_between(my_index - span, my_index - 1)
     factors.append(open_path * jnp.exp(float(span * row_count) * log_decay))
     factors = jnp.stack(factors)
+    slot_count = factors.shape[0]
     vmem = pl.BlockSpec(memory_space=pltpu.VMEM)
     incoming = pl.pallas_call(
-        functools.partial(scan_kernel, ctx_count, tuple(spans)),
+        functools.partial(scan_kernel, ctx_count, tuple(rounds), span),
         out_shape=jax.ShapeDtypeStruct((MODES, channels), f32),
         in_specs=[vmem, vmem],
         out_specs=vmem,
         scratch_shapes=[
-            pltpu.VMEM((len(spans), MODES, channels), f32),
-            pltpu.VMEM((len(spans) + 2, MODES, channels), f32),
-            pltpu.SemaphoreType.DMA((len(spans) + 2,)),
-            pltpu.SemaphoreType.DMA((len(spans) + 2,)),
+            pltpu.VMEM((len(rounds), MODES, channels), f32),
+            pltpu.VMEM((slot_count, MODES, channels), f32),
+            pltpu.SemaphoreType.DMA((slot_count,)),
+            pltpu.SemaphoreType.DMA((slot_count,)),
         ],
         compiler_params=pltpu.CompilerParams(collective_id=0, has_side_effects=True),
         interpret=INTERPRET,

time: 76.5 us -> 80.5 us (1.052)
  the two profiles are of different devices: /device:TPU:31 before, /device:TPU:6 now
where the time goes in v5:
time: 80.5 us; the launch traced here: 80.1 us
  Pallas kernels  68.8 us (85%)
  between operations  4.6 us (6%)
  other arithmetic  3.51 us (4%)
  starting transfers between devices  1.92 us (2%)
  local copies, waits for them, and re-layouts  1.31 us (2%)
    pallas_call x1, Pallas kernels, body(): pl.pallas_call(functools.partial(scan_kernel, ctx_count, tuple(rounds), s...  30.9 us
    pallas_call x1, Pallas kernels, body(): pl.pallas_call(local_kernel, grid=(tiles,), in_specs=[col(row_count), col...  29.6 us
    pallas_call x1, Pallas kernels, body(): pl.pallas_call(fix_kernel, grid=(channels // LANES_FIX,), in_specs=[wide(...  8.3 us
    ppermute x1, starting transfers between devices, from_behind(): lax.ppermute(value, axis, [(source, source + steps) for source in range(f...  1.92 us
  transfers between devices with their start and end apart: 1, of which 0 were waited for; matrix products, arithmetic and copies ran while one was open for 4% of the time, Pallas kernels for 0%

profile of v5, /device:TPU:6, one launch (start us, length us, event | category | flops | bytes accessed | tf_op | source)
XLA Modules:
  0.0 80.1 jit_solution(17087139134350783683)
XLA Ops:
  0.0 0.0 copy-start.4
  0.0 0.0 copy-start
  0.0 0.0 copy-start.2
  0.0 0.9 %pad_maximum_fusion = bf16[3,6,2048]{2,1,0:T(8,128)(2,1)S(1)} fusion(bf16[1,256,2048]{2,1,0:T(8,128)(2,1)} %bitcast.28, bf16[1,256,2048]{2,1,0:T(8,128)(2,1)} %bitcast.27, bf16[1,256,2048]{2,1,0:T(8,128)(2,1)} %bitcast.26), kind=kLoop, calls=%fused_computation.11 | loop fusion | flops 221184 | bytes 3219456 | tf_op jit(solution)/shard_map/stack | solution.py:178
  0.9 1.9 %collective-permute-start = (bf16[3,6,2048]{2,1,0:T(8,128)(2,1)S(1)}, bf16[3,6,2048]{2,1,0:T(8,128)(2,1)S(1)}, u32[]{:S(2)}, u32[]{:S(2)}) collective-permute-start(bf16[3,6,2048]{2,1,0:T(8,128)(2,1)S(1)} %pad_maximum_fusion), channel_id=1, source_target_pairs={{0,4},{4,8},{8,12},{12,16},{16,20},{20,24},{24,28},{28,32},{32,36}... | collective-permute-start | bytes 221192 | tf_op jit(solution)/shard_map/ppermute | solution.py:21
  2.8 0.0 copy-done.4
  2.8 0.2 reduce-window.9
  3.0 0.8 and_reduce_fusion.2
  3.8 0.1 select_reduce_fusion
  8.3 0.2 and_reduce_fusion
  8.6 0.0 copy-done
  8.6 0.0 copy-done.2
  8.6 0.8 %negate_log-plus-one_fusion = (f32[16,2048]{1,0:T(8,128)}, f32[16,2048]{1,0:T(8,128)}, f32[16,2048]{1,0:T(8,128)}) fusion(f32[16,2048]{1,0:T(8,128)S(1)} %copy-done, f32[16,2048]{1,0:T(8,128)S(1)} %copy-done.2), kind=kLoop, calls=%fused_computation.10 | loop fusion | flops 131072 | bytes 655360 | tf_op jit(solution)/shard_map/log1p | solution.py:180
  9.4 0.1 bitcast_dynamic-update-slice_fusion.6
  9.5 0.1 bitcast_dynamic-update-slice_fusion.5
  9.5 0.1 bitcast_dynamic-update-slice_fusion.4
  9.6 0.1 bitcast_dynamic-update-slice_fusion.3
  9.7 0.1 bitcast_dynamic-update-slice_fusion.2
  9.8 0.1 bitcast_dynamic-update-slice_fusion.1
  9.9 0.1 bitcast_dynamic-update-slice_fusion.fac_ref
  10.0 0.0 copy-start.1
  10.0 0.3 scatter.9
  10.3 0.0 collective-permute-done.rim_ref
  10.3 0.0 copy-start.3
  10.3 1.0 %broadcast_in_dim.16.mask_ref = f32[4,256,128]{2,1,0:T(8,128)} broadcast(f32[4,256]{1,0:T(4,128)S(1)} %pad_maximum_fusion.2), dimensions={0,1} | broadcast | bytes 528384 | tf_op jit(solution)/shard_map/broadcast_in_dim | solution.py:176
  11.3 0.0 copy-done.3
  11.3 29.6 %shard_map.82 = (f32[256,2048]{1,0:T(8,128)}, f32[256,2048]{1,0:T(8,128)}, f32[16,16,2048]{2,1,0:T(8,128)}, f32[16,2048]{1,0:T(8,128)}) custom-call(bf16[256,2048]{1,0:T(8,128)(2,1)} %q_ref.1, bf16[256,2048]{1,0:T(8,128)(2,1)} %k_ref.1, bf16[256,2048]{1,0:T(8,128)(2,1)} %v_ref.1, bf16[3,6,2048]{2,1,0:T(8,128)(2,1)} %copy-done.3, f32[3,7,2048]{2,1,0:T(8,128)} %filt_ref.1, ...), custom_call_target="tpu_custom_call" | custom-call | tf_op jit(solution)/shard_map/pallas_call | solution.py:187
  40.9 0.0 copy-done.1
  40.9 30.9 %shard_map.83.hin_ref = f32[16,2048]{1,0:T(8,128)} custom-call(f32[16,2048]{1,0:T(8,128)} %get-tuple-element.36.own_ref, f32[8,16,2048]{2,1,0:T(8,128)} %copy-done.1), custom_call_target="tpu_custom_call" | custom-call | tf_op jit(solution)/shard_map/pallas_call | solution.py:221
  71.8 8.3 %shard_map.84 = bf16[256,2048]{1,0:T(8,128)(2,1)} custom-call(f32[256,2048]{1,0:T(8,128)} %get-tuple-element.33.acc_ref, f32[256,2048]{1,0:T(8,128)} %get-tuple-element.34.qs_ref, f32[16,16,2048]{2,1,0:T(8,128)} %get-tuple-element.35.cl_ref, f32[16,2048]{1,0:T(8,128)} %shard_map.83.hin_ref, f32[16,2048]{1,0:T(8,128)} %get-tuple-element.49.amp_ref, ...), custom_call_target="tpu_custom_call" | custom-call | tf_op jit(solution)/shard_map/pallas_call | solution.py:237
  (10 shorter events, 0.1 us)
Async XLA Ops:
  0.0 2.8 %copy-start.4 = (s32[8]{0:T(128)S(1)}, s32[8]{0:T(128)}, u32[]{:S(2)}) copy-start(s32[8]{0:T(128)} %param.19) | copy-start | bytes 100
  0.0 8.6 %copy-start = (f32[16,2048]{1,0:T(8,128)S(1)}, f32[16,2048]{1,0:T(8,128)}, u32[]{:S(2)}) copy-start(f32[16,2048]{1,0:T(8,128)} %param.17) | copy-start | bytes 393220
  0.0 8.6 %copy-start.2 = (f32[16,2048]{1,0:T(8,128)S(1)}, f32[16,2048]{1,0:T(8,128)}, u32[]{:S(2)}) copy-start(f32[16,2048]{1,0:T(8,128)} %param.16) | copy-start | bytes 393220
  0.9 9.4 %collective-permute-start = (bf16[3,6,2048]{2,1,0:T(8,128)(2,1)S(1)}, bf16[3,6,2048]{2,1,0:T(8,128)(2,1)S(1)}, u32[]{:S(2)}, u32[]{:S(2)}) collective-permute-start(bf16[3,6,2048]{2,1,0:T(8,128)(2,1)S(1)} %pad_maximum_fusion), channel_id=1, source_target_pairs={{0,4},{4,8},{8,12},{12,16},{16,20},{20,24},{24,28},{28,32},{32,36}... | collective-permute-start | bytes 221192 | tf_op jit(solution)/shard_map/ppermute | solution.py:21
  10.0 30.9 %copy-start.1 = (f32[8,16,2048]{2,1,0:T(8,128)}, f32[8,16,2048]{2,1,0:T(8,128)S(1)}, u32[]{:S(2)}) copy-start(f32[8,16,2048]{2,1,0:T(8,128)S(1)} %bitcast_dynamic-update-slice_fusion.fac_ref) | copy-start | bytes 3145732
  10.3 1.0 %copy-start.3 = (bf16[3,6,2048]{2,1,0:T(8,128)(2,1)}, bf16[3,6,2048]{2,1,0:T(8,128)(2,1)S(1)}, u32[]{:S(2)}) copy-start(bf16[3,6,2048]{2,1,0:T(8,128)(2,1)S(1)} %collective-permute-done.rim_ref) | copy-start | bytes 221188

commit v6 on v4

--- a/solution.py
+++ b/solution.py
@@ -21,24 +21,26 @@
     return lax.ppermute(value, axis, [(source, source + steps) for source in range(first, last)])
 
 
-def local_kernel(q_ref, k_ref, v_ref, rim_ref, filt_ref, amp_ref, lam_ref, skip_ref, mask_ref,
-                 acc_ref, qs_ref, cl_ref, end_ref, ext_ref, g_ref):
+def short_conv(block, rim_rows, taps, since, ext_ref):
+    rows = block.shape[0]
+    ext_ref[8 - TAPS + 1:8, :] = rim_rows.astype(jnp.float32)
+    ext_ref[8:8 + rows, :] = block.astype(jnp.float32)
+    total = jnp.zeros((rows, LANES), jnp.float32)
+    for lag in range(TAPS):
+        window = ext_ref[8 - lag:8 - lag + rows, :]
+        total = total + jnp.where(since >= float(lag), taps[lag:lag + 1, :] * window, 0.0)
+    return total
+
+
+def local_kernel(k_ref, v_ref, rim_ref, filt_ref, amp_ref, lam_ref, skip_ref, mask_ref,
+                 acc_ref, cl_ref, end_ref, ext_ref, g_ref):
     since_ref, keep_ref = mask_ref.at[0], mask_ref.at[1]
-    rows = q_ref.shape[0]
+    rows = k_ref.shape[0]
     seg_rows = rows // SEGMENTS
     since = since_ref[...]
-    filtered = []
-    for branch, src in enumerate((q_ref, k_ref, v_ref)):
-        ext_ref[8 - TAPS + 1:8, :] = rim_ref[branch].astype(jnp.float32)
-        ext_ref[8:8 + rows, :] = src[...].astype(jnp.float32)
-        total = jnp.zeros((rows, LANES), jnp.float32)
-        for lag in range(TAPS):
-            window = ext_ref[8 - lag:8 - lag + rows, :]
-            tap = filt_ref[branch, lag:lag + 1, :]
-            total = total + jnp.where(since >= float(lag), tap * window, 0.0)
-        filtered.append(total)
-    qs_ref[...] = filtered[0]
-    g_ref[...] = (filtered[1] * filtered[2]).astype(jnp.bfloat16).astype(jnp.float32)
+    filtered = [short_conv(src[...], rim_ref[branch], filt_ref[branch], since, ext_ref)
+                for branch, src in ((1, k_ref), (2, v_ref))]
+    g_ref[...] = (filtered[0] * filtered[1]).astype(jnp.bfloat16).astype(jnp.float32)
     lam = [jnp.broadcast_to(lam_ref[m:m + 1, :], (SEGMENTS, LANES)) for m in range(MODES)]
     amp = [jnp.broadcast_to(amp_ref[m:m + 1, :], (SEGMENTS, LANES)) for m in range(MODES)]
     skip = jnp.broadcast_to(skip_ref[...], (SEGMENTS, LANES))
@@ -93,7 +95,17 @@
         out_ref[lo:lo + seg_rows, :] = (qs_ref[lo:lo + seg_rows, :] * conv).astype(out_ref.dtype)
 
 
-def scan_kernel(count, spans, own_ref, fac_ref, out_ref, sums, slots, send_sems, recv_sems):
+def scan_kernel(count, spans, own_ref, fac_ref, q_ref, rim_ref, filt_ref, mask_ref, out_ref, qs_ref, sums, slots,
+                send_sems, recv_sems, ext_ref):
+    columns = q_ref.shape[1] // LANES
+    groups = len(spans) + 1
+    since = mask_ref[0]
+
+    def filter_columns(group):
+        for c in range(group * columns // groups, (group + 1) * columns // groups):
+            lanes = slice(c * LANES, (c + 1) * LANES)
+            qs_ref[:, lanes] = short_conv(q_ref[:, lanes], rim_ref[0, :, lanes], filt_ref[0, :, lanes], since, ext_ref)
+
     me = lax.axis_index("ctx")
     lane = lax.axis_index("tp")
     last = spans[-1] * 2 if spans else 1
@@ -129,6 +141,8 @@
     current = own_ref
     for r, d in enumerate(spans):
         exchange(current, [(r, d)])
+        filter_columns(r)
+
         @pl.when(me - d >= 0)
         def _():
             transfer(current, r, me - d).wait_recv()
@@ -142,6 +156,7 @@
     near, far = len(spans), len(spans) + 1
     final = [(near, 1), (far, 1 + last)]
     exchange(current, final)
+    filter_columns(len(spans))
     out_ref[...] = jnp.zeros(out_ref.shape, out_ref.dtype)
 
     @pl.when(me - 1 >= 0)
@@ -191,17 +206,17 @@
     col = lambda *lead: pl.BlockSpec(tuple(lead) + (LANES,), lambda c: (0,) * len(lead) + (c,))
     fixed = lambda *shape: pl.BlockSpec(shape, lambda c: (0,) * len(shape))
     f32 = jnp.float32
-    acc, q_short, cl, own_state = pl.pallas_call(
+    acc, cl, own_state = pl.pallas_call(
         local_kernel,
         grid=(tiles,),
-        in_specs=[col(row_count), col(row_count), col(row_count), col(3, TAPS - 1), col(3, TAPS), col(MODES), col(MODES),
+        in_specs=[col(row_count), col(row_count), col(3, TAPS - 1), col(3, TAPS), col(MODES), col(MODES),
                   col(1), fixed(4, row_count, LANES)],
-        out_specs=[col(row_count), col(row_count), col(MODES, 16), col(MODES)],
-        out_shape=[jax.ShapeDtypeStruct((row_count, channels), f32), jax.ShapeDtypeStruct((row_count, channels), f32),
+        out_specs=[col(row_count), col(MODES, 16), col(MODES)],
+        out_shape=[jax.ShapeDtypeStruct((row_count, channels), f32),
                    jax.ShapeDtypeStruct((MODES, 16, channels), f32), jax.ShapeDtypeStruct((MODES, channels), f32)],
         scratch_shapes=[pltpu.VMEM((row_count + 8, LANES), f32), pltpu.VMEM((row_count, LANES), f32)],
         interpret=INTERPRET,
-    )(query_proj, key_proj, value_proj, rim, short_filter, amp, lam, skip_gain[None, :], masks)
+    )(key_proj, value_proj, rim, short_filter, amp, lam, skip_gain[None, :], masks)
 
     def starts_between(low_device, high_device):
         low_row = jnp.maximum(low_device, 0) * row_count
@@ -221,20 +236,21 @@
     factors.append(open_path * jnp.exp(float(span * row_count) * log_decay))
     factors = jnp.stack(factors)
     vmem = pl.BlockSpec(memory_space=pltpu.VMEM)
-    incoming = pl.pallas_call(
+    incoming, q_short = pl.pallas_call(
         functools.partial(scan_kernel, ctx_count, tuple(spans)),
-        out_shape=jax.ShapeDtypeStruct((MODES, channels), f32),
-        in_specs=[vmem, vmem],
-        out_specs=vmem,
+        out_shape=[jax.ShapeDtypeStruct((MODES, channels), f32), jax.ShapeDtypeStruct((row_count, channels), f32)],
+        in_specs=[vmem] * 6,
+        out_specs=[vmem, vmem],
         scratch_shapes=[
             pltpu.VMEM((len(spans), MODES, channels), f32),
             pltpu.VMEM((len(spans) + 2, MODES, channels), f32),
             pltpu.SemaphoreType.DMA((len(spans) + 2,)),
             pltpu.SemaphoreType.DMA((len(spans) + 2,)),
+            pltpu.VMEM((row_count + 8, LANES), f32),
         ],
         compiler_params=pltpu.CompilerParams(collective_id=0, has_side_effects=True),
         interpret=INTERPRET,
-    )(own_state, factors)
+    )(own_state, factors, query_proj, rim, short_filter, masks)
 
     wide = lambda *lead: pl.BlockSpec(tuple(lead) + (LANES_FIX,), lambda c: (0,) * len(lead) + (c,))
     return pl.pallas_call(

time: 76.5 us -> 75.3 us (0.984)
  Pallas kernels: 66.8 us -> 65.6 us
    pallas_call x1, Pallas kernels: 29.6 us -> 27.2 us  [body(): pl.pallas_call(local_kernel, grid=(tiles,), in_specs=[col(row_count), col...]
    pallas_call x1, Pallas kernels: 28.9 us -> 30.1 us  [body(): pl.pallas_call(functools.partial(scan_kernel, ctx_count, tuple(spans)), o...]
where the time goes in v6:
time: 75.3 us; the launch traced here: 74.9 us
  Pallas kernels  65.6 us (87%)
  other arithmetic  3.37 us (4%)
  between operations  3.34 us (4%)
  local copies, waits for them, and re-layouts  1.3 us (2%)
  starting transfers between devices  1.29 us (2%)
    pallas_call x1, Pallas kernels, body(): pl.pallas_call(functools.partial(scan_kernel, ctx_count, tuple(spans)), o...  30.1 us
    pallas_call x1, Pallas kernels, body(): pl.pallas_call(local_kernel, grid=(tiles,), in_specs=[col(row_count), col...  27.2 us
    pallas_call x1, Pallas kernels, body(): pl.pallas_call(fix_kernel, grid=(channels // LANES_FIX,), in_specs=[wide(...  8.3 us
  transfers between devices with their start and end apart: 1, of which 0 were waited for; matrix products, arithmetic and copies ran while one was open for 4% of the time, Pallas kernels for 0%

profile of v6, /device:TPU:31, one launch (start us, length us, event | category | flops | bytes accessed | tf_op | source)
XLA Modules:
  0.0 74.9 jit_solution(8845643927233877966)
XLA Ops:
  0.0 0.0 copy-start.4
  0.0 0.0 copy-start
  0.0 0.0 copy-start.3
  0.0 0.9 %pad_maximum_fusion = bf16[3,6,2048]{2,1,0:T(8,128)(2,1)S(1)} fusion(bf16[1,256,2048]{2,1,0:T(8,128)(2,1)} %bitcast.23, bf16[1,256,2048]{2,1,0:T(8,128)(2,1)} %bitcast.22, bf16[1,256,2048]{2,1,0:T(8,128)(2,1)} %bitcast.24), kind=kLoop, calls=%fused_computation.9 | loop fusion | flops 221184 | bytes 3219456 | tf_op jit(solution)/shard_map/stack | solution.py:200
  0.9 1.3 %collective-permute-start = (bf16[3,6,2048]{2,1,0:T(8,128)(2,1)S(1)}, bf16[3,6,2048]{2,1,0:T(8,128)(2,1)S(1)}, u32[]{:S(2)}, u32[]{:S(2)}) collective-permute-start(bf16[3,6,2048]{2,1,0:T(8,128)(2,1)S(1)} %pad_maximum_fusion), channel_id=1, source_target_pairs={{0,4},{4,8},{8,12},{12,16},{16,20},{20,24},{24,28},{28,32},{32,36}... | collective-permute-start | bytes 221192 | tf_op jit(solution)/shard_map/ppermute | solution.py:21
  2.2 0.0 copy-done.4
  2.2 0.2 reduce-window.9
  2.4 0.8 %and_reduce_fusion.2 = (pred[]{:T(512)}, pred[]{:T(512)}, pred[]{:T(512)}, pred[]{:T(512)}, pred[]{:T(512)}, /*index=5*/s32[8]{0:T(128)S(1)}) fusion(s32[]{:T(128)S(6)} %mul.138, s32[]{:T(128)S(6)} %mul.114, s32[]{:T(128)S(6)} %mul.118, s32[]{:T(128)S(6)} %mul.133, s32[]{:T(128)S(6)} %mul.128, s32[]{:T(128)S(6)} %mul.123, s32[]{:T(128)S(6)} %mul.117, ...), kind=kLoop, calls=%fused_computation.21 | loop fusion | flops 139 | bytes 129 | tf_op jit(solution)/shard_map/reduce_or | solution.py:224
  3.2 0.1 select_reduce_fusion
  6.5 0.2 and_reduce_fusion
  6.7 0.0 copy-done
  6.7 0.0 copy-done.3
  6.7 0.8 %negate_log-plus-one_fusion = (f32[16,2048]{1,0:T(8,128)}, f32[16,2048]{1,0:T(8,128)}, f32[16,2048]{1,0:T(8,128)}) fusion(f32[16,2048]{1,0:T(8,128)S(1)} %copy-done, f32[16,2048]{1,0:T(8,128)S(1)} %copy-done.3), kind=kLoop, calls=%fused_computation.8 | loop fusion | flops 131072 | bytes 655360 | tf_op jit(solution)/shard_map/log1p | solution.py:202
  7.5 0.1 bitcast_dynamic-update-slice_fusion.4
  7.6 0.1 bitcast_dynamic-update-slice_fusion.3
  7.7 0.1 bitcast_dynamic-update-slice_fusion.2
  7.8 0.1 bitcast_dynamic-update-slice_fusion.1
  7.9 0.1 bitcast_dynamic-update-slice_fusion.fac_ref
  8.0 0.0 copy-start.1
  8.0 0.3 scatter.9
  8.2 0.0 collective-permute-done.rim_ref
  8.3 0.0 copy-start.2
  8.3 1.0 %broadcast_in_dim.16.mask_ref = f32[4,256,128]{2,1,0:T(8,128)} broadcast(f32[4,256]{1,0:T(4,128)S(1)} %pad_maximum_fusion.2), dimensions={0,1} | broadcast | bytes 528384 | tf_op jit(solution)/shard_map/broadcast_in_dim | solution.py:198
  9.3 0.0 copy-done.2
  9.3 27.2 %shard_map.82 = (f32[256,2048]{1,0:T(8,128)}, f32[16,16,2048]{2,1,0:T(8,128)}, f32[16,2048]{1,0:T(8,128)}) custom-call(bf16[256,2048]{1,0:T(8,128)(2,1)} %k_ref.1, bf16[256,2048]{1,0:T(8,128)(2,1)} %v_ref.1, bf16[3,6,2048]{2,1,0:T(8,128)(2,1)} %copy-done.2, f32[3,7,2048]{2,1,0:T(8,128)} %filt_ref.3, f32[16,2048]{1,0:T(8,128)} %get-tuple-element.49.amp_ref, ...), custom_call_target="tpu_custom_call" | custom-call | tf_op jit(solution)/shard_map/pallas_call | solution.py:209
  36.5 0.0 copy-done.1
  36.5 30.1 %shard_map.83 = (f32[16,2048]{1,0:T(8,128)}, f32[256,2048]{1,0:T(8,128)}) custom-call(f32[16,2048]{1,0:T(8,128)} %get-tuple-element.35.own_ref, f32[5,16,2048]{2,1,0:T(8,128)} %copy-done.1, bf16[256,2048]{1,0:T(8,128)(2,1)} %q_ref.1, bf16[3,6,2048]{2,1,0:T(8,128)(2,1)} %copy-done.2, f32[3,7,2048]{2,1,0:T(8,128)} %filt_ref.3, ...), custom_call_target="tpu_custom_call" | custom-call | tf_op jit(solution)/shard_map/pallas_call | solution.py:239
  66.6 8.3 %shard_map.84 = bf16[256,2048]{1,0:T(8,128)(2,1)} custom-call(f32[256,2048]{1,0:T(8,128)} %get-tuple-element.34.acc_ref, f32[256,2048]{1,0:T(8,128)} %get-tuple-element.36.qs_ref, f32[16,16,2048]{2,1,0:T(8,128)} %get-tuple-element.37.cl_ref, f32[16,2048]{1,0:T(8,128)} %get-tuple-element.38.hin_ref, f32[16,2048]{1,0:T(8,128)} %get-tuple-element.49.amp_ref, ...), custom_call_target="tpu_custom_call" | custom-call | tf_op jit(solution)/shard_map/pallas_call | solution.py:256
  (9 shorter events, 0.1 us)
Async XLA Ops:
  0.0 2.2 %copy-start.4 = (s32[8]{0:T(128)S(1)}, s32[8]{0:T(128)}, u32[]{:S(2)}) copy-start(s32[8]{0:T(128)} %param.19) | copy-start | bytes 100
  0.0 6.7 %copy-start = (f32[16,2048]{1,0:T(8,128)S(1)}, f32[16,2048]{1,0:T(8,128)}, u32[]{:S(2)}) copy-start(f32[16,2048]{1,0:T(8,128)} %param.17) | copy-start | bytes 393220
  0.0 6.7 %copy-start.3 = (f32[16,2048]{1,0:T(8,128)S(1)}, f32[16,2048]{1,0:T(8,128)}, u32[]{:S(2)}) copy-start(f32[16,2048]{1,0:T(8,128)} %param.16) | copy-start | bytes 393220
  0.9 7.4 %collective-permute-start = (bf16[3,6,2048]{2,1,0:T(8,128)(2,1)S(1)}, bf16[3,6,2048]{2,1,0:T(8,128)(2,1)S(1)}, u32[]{:S(2)}, u32[]{:S(2)}) collective-permute-start(bf16[3,6,2048]{2,1,0:T(8,128)(2,1)S(1)} %pad_maximum_fusion), channel_id=1, source_target_pairs={{0,4},{4,8},{8,12},{12,16},{16,20},{20,24},{24,28},{28,32},{32,36}... | collective-permute-start | bytes 221192 | tf_op jit(solution)/shard_map/ppermute | solution.py:21
  8.0 28.6 %copy-start.1 = (f32[5,16,2048]{2,1,0:T(8,128)}, f32[5,16,2048]{2,1,0:T(8,128)S(1)}, u32[]{:S(2)}) copy-start(f32[5,16,2048]{2,1,0:T(8,128)S(1)} %bitcast_dynamic-update-slice_fusion.fac_ref) | copy-start | bytes 1966084
  8.3 1.0 %copy-start.2 = (bf16[3,6,2048]{2,1,0:T(8,128)(2,1)}, bf16[3,6,2048]{2,1,0:T(8,128)(2,1)S(1)}, u32[]{:S(2)}) copy-start(bf16[3,6,2048]{2,1,0:T(8,128)(2,1)S(1)} %collective-permute-done.rim_ref) | copy-start | bytes 221188

commit v7 on v6

--- a/solution.py
+++ b/solution.py
@@ -48,17 +48,15 @@
     def step(j, states):
         x = g_ref[pl.ds(j, SEGMENTS, stride=seg_rows), :]
         keep = keep_ref[pl.ds(j, SEGMENTS, stride=seg_rows), :]
-        new_states = []
-        y = skip * x
-        for m in range(MODES):
-            h = lam[m] * (keep * states[m]) + x
-            new_states.append(h)
-            y = y + amp[m] * h
-        acc_ref[pl.ds(j, SEGMENTS, stride=seg_rows), :] = y
+        new_states = [lam[m] * (keep * states[m]) + x for m in range(MODES)]
+        terms = [amp[m] * new_states[m] for m in range(MODES)] + [skip * x]
+        while len(terms) > 1:
+            terms = [terms[i] + terms[i + 1] for i in range(0, len(terms) - 1, 2)] + terms[len(terms) - len(terms) % 2:]
+        acc_ref[pl.ds(j, SEGMENTS, stride=seg_rows), :] = terms[0]
         return tuple(new_states)
 
     zero = jnp.zeros((SEGMENTS, LANES), jnp.float32)
-    ends = lax.fori_loop(0, seg_rows, step, tuple([zero] * MODES))
+    ends = lax.fori_loop(0, seg_rows, step, tuple([zero] * MODES), unroll=2)
     segkeep = mask_ref[3, 0:SEGMENTS, :]
     for m in range(MODES):
         seg_decay = jnp.exp(float(seg_rows) * jnp.log(lam_ref[m:m + 1, :]))

time: 75.3 us -> 69.6 us (0.924)
  Pallas kernels: 65.6 us -> 59.8 us
    pallas_call x1, Pallas kernels: 27.2 us -> 21.5 us  [body(): pl.pallas_call(local_kernel, grid=(tiles,), in_specs=[col(row_count), col...]
where the time goes in v7:
time: 69.6 us; the launch traced here: 69.1 us
  Pallas kernels  59.8 us (86%)
  other arithmetic  3.37 us (5%)
  between operations  3.34 us (5%)
  local copies, waits for them, and re-layouts  1.3 us (2%)
  starting transfers between devices  1.29 us (2%)
    pallas_call x1, Pallas kernels, body(): pl.pallas_call(functools.partial(scan_kernel, ctx_count, tuple(spans)), o...  30.1 us
    pallas_call x1, Pallas kernels, body(): pl.pallas_call(local_kernel, grid=(tiles,), in_specs=[col(row_count), col...  21.5 us
    pallas_call x1, Pallas kernels, body(): pl.pallas_call(fix_kernel, grid=(channels // LANES_FIX,), in_specs=[wide(...  8.3 us
  transfers between devices with their start and end apart: 1, of which 0 were waited for; matrix products, arithmetic and copies ran while one was open for 4% of the time, Pallas kernels for 0%

profile of v7, /device:TPU:31, one launch (start us, length us, event | category | flops | bytes accessed | tf_op | source)
XLA Modules:
  0.0 69.1 jit_solution(8958234759651460830)
XLA Ops:
  0.0 0.0 copy-start.4
  0.0 0.0 copy-start
  0.0 0.0 copy-start.3
  0.0 0.9 %pad_maximum_fusion = bf16[3,6,2048]{2,1,0:T(8,128)(2,1)S(1)} fusion(bf16[1,256,2048]{2,1,0:T(8,128)(2,1)} %bitcast.23, bf16[1,256,2048]{2,1,0:T(8,128)(2,1)} %bitcast.22, bf16[1,256,2048]{2,1,0:T(8,128)(2,1)} %bitcast.24), kind=kLoop, calls=%fused_computation.9 | loop fusion | flops 221184 | bytes 3219456 | tf_op jit(solution)/shard_map/stack | solution.py:198
  0.9 1.3 %collective-permute-start = (bf16[3,6,2048]{2,1,0:T(8,128)(2,1)S(1)}, bf16[3,6,2048]{2,1,0:T(8,128)(2,1)S(1)}, u32[]{:S(2)}, u32[]{:S(2)}) collective-permute-start(bf16[3,6,2048]{2,1,0:T(8,128)(2,1)S(1)} %pad_maximum_fusion), channel_id=1, source_target_pairs={{0,4},{4,8},{8,12},{12,16},{16,20},{20,24},{24,28},{28,32},{32,36}... | collective-permute-start | bytes 221192 | tf_op jit(solution)/shard_map/ppermute | solution.py:21
  2.2 0.0 copy-done.4
  2.2 0.2 reduce-window.9
  2.4 0.8 %and_reduce_fusion.2 = (pred[]{:T(512)}, pred[]{:T(512)}, pred[]{:T(512)}, pred[]{:T(512)}, pred[]{:T(512)}, /*index=5*/s32[8]{0:T(128)S(1)}) fusion(s32[]{:T(128)S(6)} %mul.138, s32[]{:T(128)S(6)} %mul.114, s32[]{:T(128)S(6)} %mul.118, s32[]{:T(128)S(6)} %mul.133, s32[]{:T(128)S(6)} %mul.128, s32[]{:T(128)S(6)} %mul.123, s32[]{:T(128)S(6)} %mul.117, ...), kind=kLoop, calls=%fused_computation.21 | loop fusion | flops 139 | bytes 129 | tf_op jit(solution)/shard_map/reduce_or | solution.py:222
  3.2 0.1 select_reduce_fusion
  6.5 0.2 and_reduce_fusion
  6.7 0.0 copy-done
  6.7 0.0 copy-done.3
  6.7 0.8 %negate_log-plus-one_fusion = (f32[16,2048]{1,0:T(8,128)}, f32[16,2048]{1,0:T(8,128)}, f32[16,2048]{1,0:T(8,128)}) fusion(f32[16,2048]{1,0:T(8,128)S(1)} %copy-done, f32[16,2048]{1,0:T(8,128)S(1)} %copy-done.3), kind=kLoop, calls=%fused_computation.8 | loop fusion | flops 131072 | bytes 655360 | tf_op jit(solution)/shard_map/log1p | solution.py:200
  7.5 0.1 bitcast_dynamic-update-slice_fusion.4
  7.6 0.1 bitcast_dynamic-update-slice_fusion.3
  7.7 0.1 bitcast_dynamic-update-slice_fusion.2
  7.8 0.1 bitcast_dynamic-update-slice_fusion.1
  7.9 0.1 bitcast_dynamic-update-slice_fusion.fac_ref
  8.0 0.0 copy-start.1
  8.0 0.3 scatter.9
  8.2 0.0 collective-permute-done.rim_ref
  8.3 0.0 copy-start.2
  8.3 1.0 %broadcast_in_dim.16.mask_ref = f32[4,256,128]{2,1,0:T(8,128)} broadcast(f32[4,256]{1,0:T(4,128)S(1)} %pad_maximum_fusion.2), dimensions={0,1} | broadcast | bytes 528384 | tf_op jit(solution)/shard_map/broadcast_in_dim | solution.py:196
  9.3 0.0 copy-done.2
  9.3 21.5 %shard_map.82 = (f32[256,2048]{1,0:T(8,128)}, f32[16,16,2048]{2,1,0:T(8,128)}, f32[16,2048]{1,0:T(8,128)}) custom-call(bf16[256,2048]{1,0:T(8,128)(2,1)} %k_ref.1, bf16[256,2048]{1,0:T(8,128)(2,1)} %v_ref.1, bf16[3,6,2048]{2,1,0:T(8,128)(2,1)} %copy-done.2, f32[3,7,2048]{2,1,0:T(8,128)} %filt_ref.3, f32[16,2048]{1,0:T(8,128)} %get-tuple-element.49.amp_ref, ...), custom_call_target="tpu_custom_call" | custom-call | tf_op jit(solution)/shard_map/pallas_call | solution.py:207
  30.8 0.0 copy-done.1
  30.8 30.1 %shard_map.83 = (f32[16,2048]{1,0:T(8,128)}, f32[256,2048]{1,0:T(8,128)}) custom-call(f32[16,2048]{1,0:T(8,128)} %get-tuple-element.35.own_ref, f32[5,16,2048]{2,1,0:T(8,128)} %copy-done.1, bf16[256,2048]{1,0:T(8,128)(2,1)} %q_ref.1, bf16[3,6,2048]{2,1,0:T(8,128)(2,1)} %copy-done.2, f32[3,7,2048]{2,1,0:T(8,128)} %filt_ref.3, ...), custom_call_target="tpu_custom_call" | custom-call | tf_op jit(solution)/shard_map/pallas_call | solution.py:237
  60.8 8.3 %shard_map.84 = bf16[256,2048]{1,0:T(8,128)(2,1)} custom-call(f32[256,2048]{1,0:T(8,128)} %get-tuple-element.34.acc_ref, f32[256,2048]{1,0:T(8,128)} %get-tuple-element.36.qs_ref, f32[16,16,2048]{2,1,0:T(8,128)} %get-tuple-element.37.cl_ref, f32[16,2048]{1,0:T(8,128)} %get-tuple-element.38.hin_ref, f32[16,2048]{1,0:T(8,128)} %get-tuple-element.49.amp_ref, ...), custom_call_target="tpu_custom_call" | custom-call | tf_op jit(solution)/shard_map/pallas_call | solution.py:254
  (9 shorter events, 0.1 us)
Async XLA Ops:
  0.0 2.2 %copy-start.4 = (s32[8]{0:T(128)S(1)}, s32[8]{0:T(128)}, u32[]{:S(2)}) copy-start(s32[8]{0:T(128)} %param.19) | copy-start | bytes 100
  0.0 6.7 %copy-start = (f32[16,2048]{1,0:T(8,128)S(1)}, f32[16,2048]{1,0:T(8,128)}, u32[]{:S(2)}) copy-start(f32[16,2048]{1,0:T(8,128)} %param.17) | copy-start | bytes 393220
  0.0 6.7 %copy-start.3 = (f32[16,2048]{1,0:T(8,128)S(1)}, f32[16,2048]{1,0:T(8,128)}, u32[]{:S(2)}) copy-start(f32[16,2048]{1,0:T(8,128)} %param.16) | copy-start | bytes 393220
  0.9 7.4 %collective-permute-start = (bf16[3,6,2048]{2,1,0:T(8,128)(2,1)S(1)}, bf16[3,6,2048]{2,1,0:T(8,128)(2,1)S(1)}, u32[]{:S(2)}, u32[]{:S(2)}) collective-permute-start(bf16[3,6,2048]{2,1,0:T(8,128)(2,1)S(1)} %pad_maximum_fusion), channel_id=1, source_target_pairs={{0,4},{4,8},{8,12},{12,16},{16,20},{20,24},{24,28},{28,32},{32,36}... | collective-permute-start | bytes 221192 | tf_op jit(solution)/shard_map/ppermute | solution.py:21
  8.0 22.8 %copy-start.1 = (f32[5,16,2048]{2,1,0:T(8,128)}, f32[5,16,2048]{2,1,0:T(8,128)S(1)}, u32[]{:S(2)}) copy-start(f32[5,16,2048]{2,1,0:T(8,128)S(1)} %bitcast_dynamic-update-slice_fusion.fac_ref) | copy-start | bytes 1966084
  8.3 1.0 %copy-start.2 = (bf16[3,6,2048]{2,1,0:T(8,128)(2,1)}, bf16[3,6,2048]{2,1,0:T(8,128)(2,1)S(1)}, u32[]{:S(2)}) copy-start(bf16[3,6,2048]{2,1,0:T(8,128)(2,1)S(1)} %collective-permute-done.rim_ref) | copy-start | bytes 221188

commit v8 on v7

--- a/solution.py
+++ b/solution.py
@@ -21,15 +21,21 @@
     return lax.ppermute(value, axis, [(source, source + steps) for source in range(first, last)])
 
 
+def tree_sum(terms):
+    while len(terms) > 1:
+        terms = [terms[i] + terms[i + 1] for i in range(0, len(terms) - 1, 2)] + terms[len(terms) - len(terms) % 2:]
+    return terms[0]
+
+
 def short_conv(block, rim_rows, taps, since, ext_ref):
     rows = block.shape[0]
     ext_ref[8 - TAPS + 1:8, :] = rim_rows.astype(jnp.float32)
     ext_ref[8:8 + rows, :] = block.astype(jnp.float32)
-    total = jnp.zeros((rows, LANES), jnp.float32)
-    for lag in range(TAPS):
+    terms = [taps[0:1, :] * ext_ref[8:8 + rows, :]]
+    for lag in range(1, TAPS):
         window = ext_ref[8 - lag:8 - lag + rows, :]
-        total = total + jnp.where(since >= float(lag), taps[lag:lag + 1, :] * window, 0.0)
-    return total
+        terms.append(jnp.where(since >= float(lag), taps[lag:lag + 1, :] * window, 0.0))
+    return tree_sum(terms)
 
 
 def local_kernel(k_ref, v_ref, rim_ref, filt_ref, amp_ref, lam_ref, skip_ref, mask_ref,
@@ -50,9 +56,7 @@
         keep = keep_ref[pl.ds(j, SEGMENTS, stride=seg_rows), :]
         new_states = [lam[m] * (keep * states[m]) + x for m in range(MODES)]
         terms = [amp[m] * new_states[m] for m in range(MODES)] + [skip * x]
-        while len(terms) > 1:
-            terms = [terms[i] + terms[i + 1] for i in range(0, len(terms) - 1, 2)] + terms[len(terms) - len(terms) % 2:]
-        acc_ref[pl.ds(j, SEGMENTS, stride=seg_rows), :] = terms[0]
+        acc_ref[pl.ds(j, SEGMENTS, stride=seg_rows), :] = tree_sum(terms)
         return tuple(new_states)
 
     zero = jnp.zeros((SEGMENTS, LANES), jnp.float32)
@@ -86,9 +90,7 @@
         powers.append(amp_ref[m:m + 1, :] * jnp.exp(lag_index * logl))
     for p in range(SEGMENTS):
         lo = p * seg_rows
-        corr = jnp.zeros((seg_rows, width), jnp.float32)
-        for m in range(MODES):
-            corr = corr + powers[m] * starts[m][p:p + 1, :]
+        corr = tree_sum([powers[m] * starts[m][p:p + 1, :] for m in range(MODES)])
         conv = acc_ref[lo:lo + seg_rows, :] + widen(mask_ref[2, lo:lo + seg_rows, :]) * corr
         out_ref[lo:lo + seg_rows, :] = (qs_ref[lo:lo + seg_rows, :] * conv).astype(out_ref.dtype)
 

time: 69.6 us -> 70.2 us (level)
  no operation moved by 1% of the time
where the time goes in v8:
time: 70.2 us; the launch traced here: 69.8 us
  Pallas kernels  60.5 us (86%)
  other arithmetic  3.37 us (5%)
  between operations  3.34 us (5%)
  local copies, waits for them, and re-layouts  1.3 us (2%)
  starting transfers between devices  1.29 us (2%)
    pallas_call x1, Pallas kernels, body(): pl.pallas_call(functools.partial(scan_kernel, ctx_count, tuple(spans)), o...  30.1 us
    pallas_call x1, Pallas kernels, body(): pl.pallas_call(local_kernel, grid=(tiles,), in_specs=[col(row_count), col...  22 us
    pallas_call x1, Pallas kernels, body(): pl.pallas_call(fix_kernel, grid=(channels // LANES_FIX,), in_specs=[wide(...  8.42 us
  transfers between devices with their start and end apart: 1, of which 0 were waited for; matrix products, arithmetic and copies ran while one was open for 4% of the time, Pallas kernels for 0%

profile of v8, /device:TPU:31, one launch (start us, length us, event | category | flops | bytes accessed | tf_op | source)
XLA Modules:
  0.0 69.8 jit_solution(14590770231477112824)
XLA Ops:
  0.0 0.0 copy-start.4
  0.0 0.0 copy-start
  0.0 0.0 copy-start.3
  0.0 0.9 %pad_maximum_fusion = bf16[3,6,2048]{2,1,0:T(8,128)(2,1)S(1)} fusion(bf16[1,256,2048]{2,1,0:T(8,128)(2,1)} %bitcast.23, bf16[1,256,2048]{2,1,0:T(8,128)(2,1)} %bitcast.22, bf16[1,256,2048]{2,1,0:T(8,128)(2,1)} %bitcast.24), kind=kLoop, calls=%fused_computation.9 | loop fusion | flops 221184 | bytes 3219456 | tf_op jit(solution)/shard_map/stack | solution.py:200
  0.9 1.3 %collective-permute-start = (bf16[3,6,2048]{2,1,0:T(8,128)(2,1)S(1)}, bf16[3,6,2048]{2,1,0:T(8,128)(2,1)S(1)}, u32[]{:S(2)}, u32[]{:S(2)}) collective-permute-start(bf16[3,6,2048]{2,1,0:T(8,128)(2,1)S(1)} %pad_maximum_fusion), channel_id=1, source_target_pairs={{0,4},{4,8},{8,12},{12,16},{16,20},{20,24},{24,28},{28,32},{32,36}... | collective-permute-start | bytes 221192 | tf_op jit(solution)/shard_map/ppermute | solution.py:21
  2.2 0.0 copy-done.4
  2.2 0.2 reduce-window.9
  2.4 0.8 %and_reduce_fusion.2 = (pred[]{:T(512)}, pred[]{:T(512)}, pred[]{:T(512)}, pred[]{:T(512)}, pred[]{:T(512)}, /*index=5*/s32[8]{0:T(128)S(1)}) fusion(s32[]{:T(128)S(6)} %mul.138, s32[]{:T(128)S(6)} %mul.114, s32[]{:T(128)S(6)} %mul.118, s32[]{:T(128)S(6)} %mul.133, s32[]{:T(128)S(6)} %mul.128, s32[]{:T(128)S(6)} %mul.123, s32[]{:T(128)S(6)} %mul.117, ...), kind=kLoop, calls=%fused_computation.21 | loop fusion | flops 139 | bytes 129 | tf_op jit(solution)/shard_map/reduce_or | solution.py:224
  3.2 0.1 select_reduce_fusion
  6.5 0.2 and_reduce_fusion
  6.7 0.0 copy-done
  6.7 0.0 copy-done.3
  6.7 0.8 %negate_log-plus-one_fusion = (f32[16,2048]{1,0:T(8,128)}, f32[16,2048]{1,0:T(8,128)}, f32[16,2048]{1,0:T(8,128)}) fusion(f32[16,2048]{1,0:T(8,128)S(1)} %copy-done, f32[16,2048]{1,0:T(8,128)S(1)} %copy-done.3), kind=kLoop, calls=%fused_computation.8 | loop fusion | flops 131072 | bytes 655360 | tf_op jit(solution)/shard_map/log1p | solution.py:202
  7.5 0.1 bitcast_dynamic-update-slice_fusion.4
  7.6 0.1 bitcast_dynamic-update-slice_fusion.3
  7.7 0.1 bitcast_dynamic-update-slice_fusion.2
  7.8 0.1 bitcast_dynamic-update-slice_fusion.1
  7.9 0.1 bitcast_dynamic-update-slice_fusion.fac_ref
  8.0 0.0 copy-start.1
  8.0 0.3 scatter.9
  8.2 0.0 collective-permute-done.rim_ref
  8.3 0.0 copy-start.2
  8.3 1.0 %broadcast_in_dim.16.mask_ref = f32[4,256,128]{2,1,0:T(8,128)} broadcast(f32[4,256]{1,0:T(4,128)S(1)} %pad_maximum_fusion.2), dimensions={0,1} | broadcast | bytes 528384 | tf_op jit(solution)/shard_map/broadcast_in_dim | solution.py:198
  9.3 0.0 copy-done.2
  9.3 22.0 %shard_map.82 = (f32[256,2048]{1,0:T(8,128)}, f32[16,16,2048]{2,1,0:T(8,128)}, f32[16,2048]{1,0:T(8,128)}) custom-call(bf16[256,2048]{1,0:T(8,128)(2,1)} %k_ref.1, bf16[256,2048]{1,0:T(8,128)(2,1)} %v_ref.1, bf16[3,6,2048]{2,1,0:T(8,128)(2,1)} %copy-done.2, f32[3,7,2048]{2,1,0:T(8,128)} %filt_ref.3, f32[16,2048]{1,0:T(8,128)} %get-tuple-element.49.amp_ref, ...), custom_call_target="tpu_custom_call" | custom-call | tf_op jit(solution)/shard_map/pallas_call | solution.py:209
  31.3 0.0 copy-done.1
  31.3 30.1 %shard_map.83 = (f32[16,2048]{1,0:T(8,128)}, f32[256,2048]{1,0:T(8,128)}) custom-call(f32[16,2048]{1,0:T(8,128)} %get-tuple-element.35.own_ref, f32[5,16,2048]{2,1,0:T(8,128)} %copy-done.1, bf16[256,2048]{1,0:T(8,128)(2,1)} %q_ref.1, bf16[3,6,2048]{2,1,0:T(8,128)(2,1)} %copy-done.2, f32[3,7,2048]{2,1,0:T(8,128)} %filt_ref.3, ...), custom_call_target="tpu_custom_call" | custom-call | tf_op jit(solution)/shard_map/pallas_call | solution.py:239
  61.4 8.4 %shard_map.84 = bf16[256,2048]{1,0:T(8,128)(2,1)} custom-call(f32[256,2048]{1,0:T(8,128)} %get-tuple-element.34.acc_ref, f32[256,2048]{1,0:T(8,128)} %get-tuple-element.36.qs_ref, f32[16,16,2048]{2,1,0:T(8,128)} %get-tuple-element.37.cl_ref, f32[16,2048]{1,0:T(8,128)} %get-tuple-element.38.hin_ref, f32[16,2048]{1,0:T(8,128)} %get-tuple-element.49.amp_ref, ...), custom_call_target="tpu_custom_call" | custom-call | tf_op jit(solution)/shard_map/pallas_call | solution.py:256
  (9 shorter events, 0.1 us)
Async XLA Ops:
  0.0 2.2 %copy-start.4 = (s32[8]{0:T(128)S(1)}, s32[8]{0:T(128)}, u32[]{:S(2)}) copy-start(s32[8]{0:T(128)} %param.19) | copy-start | bytes 100
  0.0 6.7 %copy-start = (f32[16,2048]{1,0:T(8,128)S(1)}, f32[16,2048]{1,0:T(8,128)}, u32[]{:S(2)}) copy-start(f32[16,2048]{1,0:T(8,128)} %param.17) | copy-start | bytes 393220
  0.0 6.7 %copy-start.3 = (f32[16,2048]{1,0:T(8,128)S(1)}, f32[16,2048]{1,0:T(8,128)}, u32[]{:S(2)}) copy-start(f32[16,2048]{1,0:T(8,128)} %param.16) | copy-start | bytes 393220
  0.9 7.4 %collective-permute-start = (bf16[3,6,2048]{2,1,0:T(8,128)(2,1)S(1)}, bf16[3,6,2048]{2,1,0:T(8,128)(2,1)S(1)}, u32[]{:S(2)}, u32[]{:S(2)}) collective-permute-start(bf16[3,6,2048]{2,1,0:T(8,128)(2,1)S(1)} %pad_maximum_fusion), channel_id=1, source_target_pairs={{0,4},{4,8},{8,12},{12,16},{16,20},{20,24},{24,28},{28,32},{32,36}... | collective-permute-start | bytes 221192 | tf_op jit(solution)/shard_map/ppermute | solution.py:21
  8.0 23.3 %copy-start.1 = (f32[5,16,2048]{2,1,0:T(8,128)}, f32[5,16,2048]{2,1,0:T(8,128)S(1)}, u32[]{:S(2)}) copy-start(f32[5,16,2048]{2,1,0:T(8,128)S(1)} %bitcast_dynamic-update-slice_fusion.fac_ref) | copy-start | bytes 1966084
  8.3 1.0 %copy-start.2 = (bf16[3,6,2048]{2,1,0:T(8,128)(2,1)}, bf16[3,6,2048]{2,1,0:T(8,128)(2,1)S(1)}, u32[]{:S(2)}) copy-start(bf16[3,6,2048]{2,1,0:T(8,128)(2,1)S(1)} %collective-permute-done.rim_ref) | copy-start | bytes 221188

commit v9 on v7

--- a/solution.py
+++ b/solution.py
@@ -11,6 +11,7 @@
 TAPS = 7
 LANES = 128
 LANES_FIX = 256
+LANES_LOCAL = 512
 SEGMENTS = 8
 INTERPRET = False
 
@@ -33,40 +34,43 @@
 
 
 def local_kernel(k_ref, v_ref, rim_ref, filt_ref, amp_ref, lam_ref, skip_ref, mask_ref,
-                 acc_ref, cl_ref, end_ref, ext_ref, g_ref):
+                 acc_ref, cl_ref, end_ref, ext_ref, g_ref, sum_ref):
     since_ref, keep_ref = mask_ref.at[0], mask_ref.at[1]
     rows = k_ref.shape[0]
     seg_rows = rows // SEGMENTS
     since = since_ref[...]
-    filtered = [short_conv(src[...], rim_ref[branch], filt_ref[branch], since, ext_ref)
-                for branch, src in ((1, k_ref), (2, v_ref))]
-    g_ref[...] = (filtered[0] * filtered[1]).astype(jnp.bfloat16).astype(jnp.float32)
-    lam = [jnp.broadcast_to(lam_ref[m:m + 1, :], (SEGMENTS, LANES)) for m in range(MODES)]
-    amp = [jnp.broadcast_to(amp_ref[m:m + 1, :], (SEGMENTS, LANES)) for m in range(MODES)]
-    skip = jnp.broadcast_to(skip_ref[...], (SEGMENTS, LANES))
-
-    def step(j, states):
-        x = g_ref[pl.ds(j, SEGMENTS, stride=seg_rows), :]
-        keep = keep_ref[pl.ds(j, SEGMENTS, stride=seg_rows), :]
-        new_states = [lam[m] * (keep * states[m]) + x for m in range(MODES)]
-        terms = [amp[m] * new_states[m] for m in range(MODES)] + [skip * x]
-        while len(terms) > 1:
-            terms = [terms[i] + terms[i + 1] for i in range(0, len(terms) - 1, 2)] + terms[len(terms) - len(terms) % 2:]
-        acc_ref[pl.ds(j, SEGMENTS, stride=seg_rows), :] = terms[0]
-        return tuple(new_states)
-
-    zero = jnp.zeros((SEGMENTS, LANES), jnp.float32)
-    ends = lax.fori_loop(0, seg_rows, step, tuple([zero] * MODES), unroll=2)
     segkeep = mask_ref[3, 0:SEGMENTS, :]
-    for m in range(MODES):
-        seg_decay = jnp.exp(float(seg_rows) * jnp.log(lam_ref[m:m + 1, :]))
-        carried = jnp.zeros((1, LANES), jnp.float32)
-        cl_ref[m, 0:1, :] = carried
-        for p in range(SEGMENTS):
-            carried = ends[m][p:p + 1, :] + segkeep[p:p + 1, :] * seg_decay * carried
-            cl_ref[m, p + 1:p + 2, :] = carried
-        cl_ref[m, SEGMENTS + 1:, :] = jnp.zeros((16 - SEGMENTS - 1, LANES), jnp.float32)
-        end_ref[m:m + 1, :] = carried
+    for c in range(k_ref.shape[1] // LANES):
+        lanes = slice(c * LANES, (c + 1) * LANES)
+        filtered = [short_conv(src[:, lanes], rim_ref[branch, :, lanes], filt_ref[branch, :, lanes], since, ext_ref)
+                    for branch, src in ((1, k_ref), (2, v_ref))]
+        g_ref[...] = (filtered[0] * filtered[1]).astype(jnp.bfloat16).astype(jnp.float32)
+        lam = [jnp.broadcast_to(lam_ref[m:m + 1, lanes], (SEGMENTS, LANES)) for m in range(MODES)]
+        amp = [jnp.broadcast_to(amp_ref[m:m + 1, lanes], (SEGMENTS, LANES)) for m in range(MODES)]
+        skip = jnp.broadcast_to(skip_ref[:, lanes], (SEGMENTS, LANES))
+
+        def step(j, states):
+            x = g_ref[pl.ds(j, SEGMENTS, stride=seg_rows), :]
+            keep = keep_ref[pl.ds(j, SEGMENTS, stride=seg_rows), :]
+            new_states = [lam[m] * (keep * states[m]) + x for m in range(MODES)]
+            terms = [amp[m] * new_states[m] for m in range(MODES)] + [skip * x]
+            while len(terms) > 1:
+                terms = [terms[i] + terms[i + 1] for i in range(0, len(terms) - 1, 2)] + terms[len(terms) - len(terms) % 2:]
+            sum_ref[pl.ds(j, SEGMENTS, stride=seg_rows), :] = terms[0]
+            return tuple(new_states)
+
+        zero = jnp.zeros((SEGMENTS, LANES), jnp.float32)
+        ends = lax.fori_loop(0, seg_rows, step, tuple([zero] * MODES), unroll=2)
+        acc_ref[:, lanes] = sum_ref[...]
+        for m in range(MODES):
+            seg_decay = jnp.exp(float(seg_rows) * jnp.log(lam_ref[m:m + 1, lanes]))
+            carried = jnp.zeros((1, LANES), jnp.float32)
+            cl_ref[m, 0:1, lanes] = carried
+            for p in range(SEGMENTS):
+                carried = ends[m][p:p + 1, :] + segkeep[p:p + 1, :] * seg_decay * carried
+                cl_ref[m, p + 1:p + 2, lanes] = carried
+            cl_ref[m, SEGMENTS + 1:, lanes] = jnp.zeros((16 - SEGMENTS - 1, LANES), jnp.float32)
+            end_ref[m:m + 1, lanes] = carried
 
 
 def fix_kernel(acc_ref, qs_ref, cl_ref, hin_ref, amp_ref, logl_ref, mask_ref, out_ref):
@@ -204,15 +208,17 @@
     col = lambda *lead: pl.BlockSpec(tuple(lead) + (LANES,), lambda c: (0,) * len(lead) + (c,))
     fixed = lambda *shape: pl.BlockSpec(shape, lambda c: (0,) * len(shape))
     f32 = jnp.float32
+    cola = lambda *lead: pl.BlockSpec(tuple(lead) + (LANES_LOCAL,), lambda c: (0,) * len(lead) + (c,))
     acc, cl, own_state = pl.pallas_call(
         local_kernel,
-        grid=(tiles,),
-        in_specs=[col(row_count), col(row_count), col(3, TAPS - 1), col(3, TAPS), col(MODES), col(MODES),
-                  col(1), fixed(4, row_count, LANES)],
-        out_specs=[col(row_count), col(MODES, 16), col(MODES)],
+        grid=(channels // LANES_LOCAL,),
+        in_specs=[cola(row_count), cola(row_count), cola(3, TAPS - 1), cola(3, TAPS), cola(MODES), cola(MODES),
+                  cola(1), fixed(4, row_count, LANES)],
+        out_specs=[cola(row_count), cola(MODES, 16), cola(MODES)],
         out_shape=[jax.ShapeDtypeStruct((row_count, channels), f32),
                    jax.ShapeDtypeStruct((MODES, 16, channels), f32), jax.ShapeDtypeStruct((MODES, channels), f32)],
-        scratch_shapes=[pltpu.VMEM((row_count + 8, LANES), f32), pltpu.VMEM((row_count, LANES), f32)],
+        scratch_shapes=[pltpu.VMEM((row_count + 8, LANES), f32), pltpu.VMEM((row_count, LANES), f32),
+                        pltpu.VMEM((row_count, LANES), f32)],
         interpret=INTERPRET,
     )(key_proj, value_proj, rim, short_filter, amp, lam, skip_gain[None, :], masks)
 

time: 69.6 us -> 69 us (level)
  no operation moved by 1% of the time
where the time goes in v9:
time: 69 us; the launch traced here: 68.6 us
  Pallas kernels  59.3 us (86%)
  other arithmetic  3.37 us (5%)
  between operations  3.34 us (5%)
  local copies, waits for them, and re-layouts  1.3 us (2%)
  starting transfers between devices  1.29 us (2%)
    pallas_call x1, Pallas kernels, body(): pl.pallas_call(functools.partial(scan_kernel, ctx_count, tuple(spans)), o...  30.1 us
    pallas_call x1, Pallas kernels, body(): pl.pallas_call(local_kernel, grid=(channels // LANES_LOCAL,), in_specs=[c...  20.9 us
    pallas_call x1, Pallas kernels, body(): pl.pallas_call(fix_kernel, grid=(channels // LANES_FIX,), in_specs=[wide(...  8.3 us
  transfers between devices with their start and end apart: 1, of which 0 were waited for; matrix products, arithmetic and copies ran while one was open for 4% of the time, Pallas kernels for 0%

profile of v9, /device:TPU:31, one launch (start us, length us, event | category | flops | bytes accessed | tf_op | source)
XLA Modules:
  0.0 68.6 jit_solution(2261307871430631189)
XLA Ops:
  0.0 0.0 copy-start.4
  0.0 0.0 copy-start
  0.0 0.0 copy-start.3
  0.0 0.9 %pad_maximum_fusion = bf16[3,6,2048]{2,1,0:T(8,128)(2,1)S(1)} fusion(bf16[1,256,2048]{2,1,0:T(8,128)(2,1)} %bitcast.23, bf16[1,256,2048]{2,1,0:T(8,128)(2,1)} %bitcast.22, bf16[1,256,2048]{2,1,0:T(8,128)(2,1)} %bitcast.24), kind=kLoop, calls=%fused_computation.9 | loop fusion | flops 221184 | bytes 3219456 | tf_op jit(solution)/shard_map/stack | solution.py:202
  0.9 1.3 %collective-permute-start = (bf16[3,6,2048]{2,1,0:T(8,128)(2,1)S(1)}, bf16[3,6,2048]{2,1,0:T(8,128)(2,1)S(1)}, u32[]{:S(2)}, u32[]{:S(2)}) collective-permute-start(bf16[3,6,2048]{2,1,0:T(8,128)(2,1)S(1)} %pad_maximum_fusion), channel_id=1, source_target_pairs={{0,4},{4,8},{8,12},{12,16},{16,20},{20,24},{24,28},{28,32},{32,36}... | collective-permute-start | bytes 221192 | tf_op jit(solution)/shard_map/ppermute | solution.py:22
  2.2 0.0 copy-done.4
  2.2 0.2 reduce-window.9
  2.4 0.8 %and_reduce_fusion.2 = (pred[]{:T(512)}, pred[]{:T(512)}, pred[]{:T(512)}, pred[]{:T(512)}, pred[]{:T(512)}, /*index=5*/s32[8]{0:T(128)S(1)}) fusion(s32[]{:T(128)S(6)} %mul.138, s32[]{:T(128)S(6)} %mul.114, s32[]{:T(128)S(6)} %mul.118, s32[]{:T(128)S(6)} %mul.133, s32[]{:T(128)S(6)} %mul.128, s32[]{:T(128)S(6)} %mul.123, s32[]{:T(128)S(6)} %mul.117, ...), kind=kLoop, calls=%fused_computation.21 | loop fusion | flops 139 | bytes 129 | tf_op jit(solution)/shard_map/reduce_or | solution.py:228
  3.2 0.1 select_reduce_fusion
  6.5 0.2 and_reduce_fusion
  6.7 0.0 copy-done
  6.7 0.0 copy-done.3
  6.7 0.8 %negate_log-plus-one_fusion = (f32[16,2048]{1,0:T(8,128)}, f32[16,2048]{1,0:T(8,128)}, f32[16,2048]{1,0:T(8,128)}) fusion(f32[16,2048]{1,0:T(8,128)S(1)} %copy-done, f32[16,2048]{1,0:T(8,128)S(1)} %copy-done.3), kind=kLoop, calls=%fused_computation.8 | loop fusion | flops 131072 | bytes 655360 | tf_op jit(solution)/shard_map/log1p | solution.py:204
  7.5 0.1 bitcast_dynamic-update-slice_fusion.4
  7.6 0.1 bitcast_dynamic-update-slice_fusion.3
  7.7 0.1 bitcast_dynamic-update-slice_fusion.2
  7.8 0.1 bitcast_dynamic-update-slice_fusion.1
  7.9 0.1 bitcast_dynamic-update-slice_fusion.fac_ref
  8.0 0.0 copy-start.1
  8.0 0.3 scatter.9
  8.2 0.0 collective-permute-done.rim_ref
  8.3 0.0 copy-start.2
  8.3 1.0 %broadcast_in_dim.16.mask_ref = f32[4,256,128]{2,1,0:T(8,128)} broadcast(f32[4,256]{1,0:T(4,128)S(1)} %pad_maximum_fusion.2), dimensions={0,1} | broadcast | bytes 528384 | tf_op jit(solution)/shard_map/broadcast_in_dim | solution.py:200
  9.3 0.0 copy-done.2
  9.3 20.9 %shard_map.82 = (f32[256,2048]{1,0:T(8,128)}, f32[16,16,2048]{2,1,0:T(8,128)}, f32[16,2048]{1,0:T(8,128)}) custom-call(bf16[256,2048]{1,0:T(8,128)(2,1)} %k_ref.1, bf16[256,2048]{1,0:T(8,128)(2,1)} %v_ref.1, bf16[3,6,2048]{2,1,0:T(8,128)(2,1)} %copy-done.2, f32[3,7,2048]{2,1,0:T(8,128)} %filt_ref.3, f32[16,2048]{1,0:T(8,128)} %get-tuple-element.49.amp_ref, ...), custom_call_target="tpu_custom_call" | custom-call | tf_op jit(solution)/shard_map/pallas_call | solution.py:212
  30.2 0.0 copy-done.1
  30.2 30.1 %shard_map.83 = (f32[16,2048]{1,0:T(8,128)}, f32[256,2048]{1,0:T(8,128)}) custom-call(f32[16,2048]{1,0:T(8,128)} %get-tuple-element.35.own_ref, f32[5,16,2048]{2,1,0:T(8,128)} %copy-done.1, bf16[256,2048]{1,0:T(8,128)(2,1)} %q_ref.1, bf16[3,6,2048]{2,1,0:T(8,128)(2,1)} %copy-done.2, f32[3,7,2048]{2,1,0:T(8,128)} %filt_ref.3, ...), custom_call_target="tpu_custom_call" | custom-call | tf_op jit(solution)/shard_map/pallas_call | solution.py:243
  60.3 8.3 %shard_map.84 = bf16[256,2048]{1,0:T(8,128)(2,1)} custom-call(f32[256,2048]{1,0:T(8,128)} %get-tuple-element.34.acc_ref, f32[256,2048]{1,0:T(8,128)} %get-tuple-element.36.qs_ref, f32[16,16,2048]{2,1,0:T(8,128)} %get-tuple-element.37.cl_ref, f32[16,2048]{1,0:T(8,128)} %get-tuple-element.38.hin_ref, f32[16,2048]{1,0:T(8,128)} %get-tuple-element.49.amp_ref, ...), custom_call_target="tpu_custom_call" | custom-call | tf_op jit(solution)/shard_map/pallas_call | solution.py:260
  (9 shorter events, 0.1 us)
Async XLA Ops:
  0.0 2.2 %copy-start.4 = (s32[8]{0:T(128)S(1)}, s32[8]{0:T(128)}, u32[]{:S(2)}) copy-start(s32[8]{0:T(128)} %param.19) | copy-start | bytes 100
  0.0 6.7 %copy-start = (f32[16,2048]{1,0:T(8,128)S(1)}, f32[16,2048]{1,0:T(8,128)}, u32[]{:S(2)}) copy-start(f32[16,2048]{1,0:T(8,128)} %param.17) | copy-start | bytes 393220
  0.0 6.7 %copy-start.3 = (f32[16,2048]{1,0:T(8,128)S(1)}, f32[16,2048]{1,0:T(8,128)}, u32[]{:S(2)}) copy-start(f32[16,2048]{1,0:T(8,128)} %param.16) | copy-start | bytes 393220
  0.9 7.4 %collective-permute-start = (bf16[3,6,2048]{2,1,0:T(8,128)(2,1)S(1)}, bf16[3,6,2048]{2,1,0:T(8,128)(2,1)S(1)}, u32[]{:S(2)}, u32[]{:S(2)}) collective-permute-start(bf16[3,6,2048]{2,1,0:T(8,128)(2,1)S(1)} %pad_maximum_fusion), channel_id=1, source_target_pairs={{0,4},{4,8},{8,12},{12,16},{16,20},{20,24},{24,28},{28,32},{32,36}... | collective-permute-start | bytes 221192 | tf_op jit(solution)/shard_map/ppermute | solution.py:22
  8.0 22.2 %copy-start.1 = (f32[5,16,2048]{2,1,0:T(8,128)}, f32[5,16,2048]{2,1,0:T(8,128)S(1)}, u32[]{:S(2)}) copy-start(f32[5,16,2048]{2,1,0:T(8,128)S(1)} %bitcast_dynamic-update-slice_fusion.fac_ref) | copy-start | bytes 1966084
  8.3 1.0 %copy-start.2 = (bf16[3,6,2048]{2,1,0:T(8,128)(2,1)}, bf16[3,6,2048]{2,1,0:T(8,128)(2,1)S(1)}, u32[]{:S(2)}) copy-start(bf16[3,6,2048]{2,1,0:T(8,128)(2,1)S(1)} %collective-permute-done.rim_ref) | copy-start | bytes 221188

commit v10 on v9

--- a/solution.py
+++ b/solution.py
@@ -173,6 +173,36 @@
     settle(current, final)
 
 
+def rim_kernel(count, tail_ref, out_ref, slot, send_sem, recv_sem):
+    me = lax.axis_index("ctx")
+    lane = lax.axis_index("tp")
+    barrier = pltpu.get_barrier_semaphore()
+    for other in (me - 1, me + 1):
+        @pl.when((other >= 0) & (other < count))
+        def _():
+            pl.semaphore_signal(barrier, inc=1, device_id=(other, lane), device_id_type=pl.DeviceIdType.MESH)
+    pl.semaphore_wait(barrier, (me + count - 1) // count + (2 * count - 2 - me) // count)
+
+    def transfer(target):
+        return pltpu.make_async_remote_copy(
+            src_ref=tail_ref, dst_ref=slot, send_sem=send_sem, recv_sem=recv_sem,
+            device_id=(target, lane), device_id_type=pl.DeviceIdType.MESH)
+
+    @pl.when(me + 1 < count)
+    def _():
+        transfer(me + 1).start()
+    out_ref[...] = jnp.zeros(out_ref.shape, out_ref.dtype)
+
+    @pl.when(me >= 1)
+    def _():
+        transfer(me - 1).wait_recv()
+        out_ref[...] = slot[...]
+
+    @pl.when(me + 1 < count)
+    def _():
+        transfer(me + 1).wait_send()
+
+
 def body(query_proj, key_proj, value_proj, short_filter, residues, decay_rate, skip_gain, doc_lengths):
     row_count, channels = query_proj.shape
     ctx_count = lax.axis_size("ctx")
@@ -200,7 +230,16 @@
     masks = jnp.broadcast_to(jnp.stack([since, keep, cont, small])[:, :, None], (4, row_count, LANES))
 
     stacked = jnp.stack([query_proj, key_proj, value_proj])
-    rim = from_behind(stacked[:, row_count - TAPS + 1:, :], "ctx", 1)
+    tail = stacked[:, row_count - TAPS + 1:, :]
+    rim = pl.pallas_call(
+        functools.partial(rim_kernel, ctx_count),
+        out_shape=jax.ShapeDtypeStruct(tail.shape, tail.dtype),
+        in_specs=[pl.BlockSpec(memory_space=pltpu.VMEM)],
+        out_specs=pl.BlockSpec(memory_space=pltpu.VMEM),
+        scratch_shapes=[pltpu.VMEM(tail.shape, tail.dtype), pltpu.SemaphoreType.DMA, pltpu.SemaphoreType.DMA],
+        compiler_params=pltpu.CompilerParams(collective_id=1, has_side_effects=True),
+        interpret=INTERPRET,
+    )(tail)
     log_decay = jnp.log1p(-decay_rate)
     lam = jnp.exp(log_decay)
     amp = residues * jnp.sqrt(decay_rate * (2.0 - decay_rate))

time: 69 us -> 76.6 us (1.11)
  the two profiles are of different devices: /device:TPU:31 before, /device:TPU:7 now
where the time goes in v10:
time: 76.6 us; the launch traced here: 76.1 us
  Pallas kernels  66.2 us (86%)
  other arithmetic  5.32 us (7%)
  between operations  3.31 us (4%)
  local copies, waits for them, and re-layouts  1.29 us (2%)
    pallas_call x1, Pallas kernels, body(): pl.pallas_call(functools.partial(scan_kernel, ctx_count, tuple(spans)), o...  31 us
    pallas_call x1, Pallas kernels, body(): pl.pallas_call(local_kernel, grid=(channels // LANES_LOCAL,), in_specs=[c...  21.1 us
    pallas_call x1, Pallas kernels, body(): pl.pallas_call(fix_kernel, grid=(channels // LANES_FIX,), in_specs=[wide(...  8.3 us
    pallas_call x1, Pallas kernels, body(): pl.pallas_call(functools.partial(rim_kernel, ctx_count), out_shape=jax.Sh...  5.73 us

profile of v10, /device:TPU:7, one launch (start us, length us, event | category | flops | bytes accessed | tf_op | source)
XLA Modules:
  0.0 76.1 jit_solution(6218742151510270707)
XLA Ops:
  0.0 0.0 copy-start
  0.0 0.0 copy-start.2
  0.0 0.9 %reduce-window.9 = s32[8,1]{0,1:T(1,128)S(1)} reduce-window(s32[8,1]{0,1:T(1,128)} %bitcast.29, s32[]{:T(128)} %constant.101.clone.1), window={size=8x1 pad=7_0x0_0}, to_apply=%region_0.0 | reduce-window | flops 56 | bytes 68 | tf_op jit(solution)/shard_map/reduce-window.4
  0.9 1.4 %and_reduce_fusion.2 = (pred[]{:T(512)}, pred[]{:T(512)}, pred[]{:T(512)}, pred[]{:T(512)}, pred[]{:T(512)}, /*index=5*/s32[8]{0:T(128)S(1)}) fusion(s32[]{:T(128)S(6)} %mul.138, s32[]{:T(128)S(6)} %mul.114, s32[]{:T(128)S(6)} %mul.118, s32[]{:T(128)S(6)} %mul.133, s32[]{:T(128)S(6)} %mul.128, s32[]{:T(128)S(6)} %mul.123, s32[]{:T(128)S(6)} %mul.117, ...), kind=kLoop, calls=%fused_computation.21 | loop fusion | flops 139 | bytes 129 | tf_op jit(solution)/shard_map/reduce_or | solution.py:267
  5.5 0.1 select_reduce_fusion
  5.6 0.2 and_reduce_fusion
  5.9 0.3 scatter.9
  6.2 1.5 %pad_maximum_fusion.tail_ref = bf16[3,6,2048]{2,1,0:T(8,128)(2,1)} fusion(bf16[1,256,2048]{2,1,0:T(8,128)(2,1)} %bitcast.23, bf16[1,256,2048]{2,1,0:T(8,128)(2,1)} %bitcast.22, bf16[1,256,2048]{2,1,0:T(8,128)(2,1)} %bitcast.24), kind=kLoop, calls=%fused_computation.9 | loop fusion | flops 221184 | bytes 3219456 | tf_op jit(solution)/shard_map/stack | solution.py:232
  7.6 5.7 %shard_map.82.rim_ref = bf16[3,6,2048]{2,1,0:T(8,128)(2,1)} custom-call(bf16[3,6,2048]{2,1,0:T(8,128)(2,1)} %pad_maximum_fusion.tail_ref), custom_call_target="tpu_custom_call" | custom-call | tf_op jit(solution)/shard_map/pallas_call | solution.py:234
  13.4 0.0 copy-done
  13.4 0.0 copy-done.2
  13.4 0.8 %negate_log-plus-one_fusion = (f32[16,2048]{1,0:T(8,128)}, f32[16,2048]{1,0:T(8,128)}, f32[16,2048]{1,0:T(8,128)}) fusion(f32[16,2048]{1,0:T(8,128)S(1)} %copy-done, f32[16,2048]{1,0:T(8,128)S(1)} %copy-done.2), kind=kLoop, calls=%fused_computation.8 | loop fusion | flops 131072 | bytes 655360 | tf_op jit(solution)/shard_map/log1p | solution.py:243
  14.2 1.0 %broadcast_in_dim.16.mask_ref = f32[4,256,128]{2,1,0:T(8,128)} broadcast(f32[4,256]{1,0:T(4,128)S(1)} %pad_maximum_fusion.2), dimensions={0,1} | broadcast | bytes 528384 | tf_op jit(solution)/shard_map/broadcast_in_dim | solution.py:230
  15.2 0.1 bitcast_dynamic-update-slice_fusion.4
  15.3 0.1 bitcast_dynamic-update-slice_fusion.3
  15.4 0.1 bitcast_dynamic-update-slice_fusion.2
  15.5 0.1 bitcast_dynamic-update-slice_fusion.1
  15.5 0.1 bitcast_dynamic-update-slice_fusion.fac_ref
  15.6 0.0 copy-start.1
  15.6 21.1 %shard_map.83 = (f32[256,2048]{1,0:T(8,128)}, f32[16,16,2048]{2,1,0:T(8,128)}, f32[16,2048]{1,0:T(8,128)}) custom-call(bf16[256,2048]{1,0:T(8,128)(2,1)} %k_ref.1, bf16[256,2048]{1,0:T(8,128)(2,1)} %v_ref.1, bf16[3,6,2048]{2,1,0:T(8,128)(2,1)} %shard_map.82.rim_ref, f32[3,7,2048]{2,1,0:T(8,128)} %filt_ref.3, f32[16,2048]{1,0:T(8,128)} %get-tuple-element.49.amp_ref, ...), custom_call_target="tpu_custom_call" | custom-call | tf_op jit(solution)/shard_map/pallas_call | solution.py:251
  36.8 0.0 copy-done.1
  36.8 31.0 %shard_map.84 = (f32[16,2048]{1,0:T(8,128)}, f32[256,2048]{1,0:T(8,128)}) custom-call(f32[16,2048]{1,0:T(8,128)} %get-tuple-element.35.own_ref, f32[5,16,2048]{2,1,0:T(8,128)} %copy-done.1, bf16[256,2048]{1,0:T(8,128)(2,1)} %q_ref.1, bf16[3,6,2048]{2,1,0:T(8,128)(2,1)} %shard_map.82.rim_ref, f32[3,7,2048]{2,1,0:T(8,128)} %filt_ref.3, ...), custom_call_target="tpu_custom_call" | custom-call | tf_op jit(solution)/shard_map/pallas_call | solution.py:282
  67.8 8.3 %shard_map.85 = bf16[256,2048]{1,0:T(8,128)(2,1)} custom-call(f32[256,2048]{1,0:T(8,128)} %get-tuple-element.34.acc_ref, f32[256,2048]{1,0:T(8,128)} %get-tuple-element.36.qs_ref, f32[16,16,2048]{2,1,0:T(8,128)} %get-tuple-element.37.cl_ref, f32[16,2048]{1,0:T(8,128)} %get-tuple-element.38.hin_ref, f32[16,2048]{1,0:T(8,128)} %get-tuple-element.49.amp_ref, ...), custom_call_target="tpu_custom_call" | custom-call | tf_op jit(solution)/shard_map/pallas_call | solution.py:299
  (9 shorter events, 0.1 us)
Async XLA Ops:
  0.0 13.4 %copy-start = (f32[16,2048]{1,0:T(8,128)S(1)}, f32[16,2048]{1,0:T(8,128)}, u32[]{:S(2)}) copy-start(f32[16,2048]{1,0:T(8,128)} %param.17) | copy-start | bytes 393220
  0.0 13.4 %copy-start.2 = (f32[16,2048]{1,0:T(8,128)S(1)}, f32[16,2048]{1,0:T(8,128)}, u32[]{:S(2)}) copy-start(f32[16,2048]{1,0:T(8,128)} %param.16) | copy-start | bytes 393220
  15.6 21.1 %copy-start.1 = (f32[5,16,2048]{2,1,0:T(8,128)}, f32[5,16,2048]{2,1,0:T(8,128)S(1)}, u32[]{:S(2)}) copy-start(f32[5,16,2048]{2,1,0:T(8,128)S(1)} %bitcast_dynamic-update-slice_fusion.fac_ref) | copy-start | bytes 1966084

commit v11 on v9

--- a/solution.py
+++ b/solution.py
@@ -52,7 +52,7 @@
         def step(j, states):
             x = g_ref[pl.ds(j, SEGMENTS, stride=seg_rows), :]
             keep = keep_ref[pl.ds(j, SEGMENTS, stride=seg_rows), :]
-            new_states = [lam[m] * (keep * states[m]) + x for m in range(MODES)]
+            new_states = [(lam[m] * keep) * states[m] + x for m in range(MODES)]
             terms = [amp[m] * new_states[m] for m in range(MODES)] + [skip * x]
             while len(terms) > 1:
                 terms = [terms[i] + terms[i + 1] for i in range(0, len(terms) - 1, 2)] + terms[len(terms) - len(terms) % 2:]

time: 69 us -> 69.1 us (level)
  no operation moved by 1% of the time
where the time goes in v11:
time: 69.1 us; the launch traced here: 68.7 us
  Pallas kernels  59.4 us (86%)
  other arithmetic  3.37 us (5%)
  between operations  3.34 us (5%)
  local copies, waits for them, and re-layouts  1.3 us (2%)
  starting transfers between devices  1.29 us (2%)
    pallas_call x1, Pallas kernels, body(): pl.pallas_call(functools.partial(scan_kernel, ctx_count, tuple(spans)), o...  30.1 us
    pallas_call x1, Pallas kernels, body(): pl.pallas_call(local_kernel, grid=(channels // LANES_LOCAL,), in_specs=[c...  21 us
    pallas_call x1, Pallas kernels, body(): pl.pallas_call(fix_kernel, grid=(channels // LANES_FIX,), in_specs=[wide(...  8.3 us
  transfers between devices with their start and end apart: 1, of which 0 were waited for; matrix products, arithmetic and copies ran while one was open for 4% of the time, Pallas kernels for 0%

profile of v11, /device:TPU:31, one launch (start us, length us, event | category | flops | bytes accessed | tf_op | source)
XLA Modules:
  0.0 68.7 jit_solution(6504142143805202572)
XLA Ops:
  0.0 0.0 copy-start.4
  0.0 0.0 copy-start
  0.0 0.0 copy-start.3
  0.0 0.9 %pad_maximum_fusion = bf16[3,6,2048]{2,1,0:T(8,128)(2,1)S(1)} fusion(bf16[1,256,2048]{2,1,0:T(8,128)(2,1)} %bitcast.23, bf16[1,256,2048]{2,1,0:T(8,128)(2,1)} %bitcast.22, bf16[1,256,2048]{2,1,0:T(8,128)(2,1)} %bitcast.24), kind=kLoop, calls=%fused_computation.9 | loop fusion | flops 221184 | bytes 3219456 | tf_op jit(solution)/shard_map/stack | solution.py:202
  0.9 1.3 %collective-permute-start = (bf16[3,6,2048]{2,1,0:T(8,128)(2,1)S(1)}, bf16[3,6,2048]{2,1,0:T(8,128)(2,1)S(1)}, u32[]{:S(2)}, u32[]{:S(2)}) collective-permute-start(bf16[3,6,2048]{2,1,0:T(8,128)(2,1)S(1)} %pad_maximum_fusion), channel_id=1, source_target_pairs={{0,4},{4,8},{8,12},{12,16},{16,20},{20,24},{24,28},{28,32},{32,36}... | collective-permute-start | bytes 221192 | tf_op jit(solution)/shard_map/ppermute | solution.py:22
  2.2 0.0 copy-done.4
  2.2 0.2 reduce-window.9
  2.4 0.8 %and_reduce_fusion.2 = (pred[]{:T(512)}, pred[]{:T(512)}, pred[]{:T(512)}, pred[]{:T(512)}, pred[]{:T(512)}, /*index=5*/s32[8]{0:T(128)S(1)}) fusion(s32[]{:T(128)S(6)} %mul.138, s32[]{:T(128)S(6)} %mul.114, s32[]{:T(128)S(6)} %mul.118, s32[]{:T(128)S(6)} %mul.133, s32[]{:T(128)S(6)} %mul.128, s32[]{:T(128)S(6)} %mul.123, s32[]{:T(128)S(6)} %mul.117, ...), kind=kLoop, calls=%fused_computation.21 | loop fusion | flops 139 | bytes 129 | tf_op jit(solution)/shard_map/reduce_or | solution.py:228
  3.2 0.1 select_reduce_fusion
  6.5 0.2 and_reduce_fusion
  6.7 0.0 copy-done
  6.7 0.0 copy-done.3
  6.7 0.8 %negate_log-plus-one_fusion = (f32[16,2048]{1,0:T(8,128)}, f32[16,2048]{1,0:T(8,128)}, f32[16,2048]{1,0:T(8,128)}) fusion(f32[16,2048]{1,0:T(8,128)S(1)} %copy-done, f32[16,2048]{1,0:T(8,128)S(1)} %copy-done.3), kind=kLoop, calls=%fused_computation.8 | loop fusion | flops 131072 | bytes 655360 | tf_op jit(solution)/shard_map/log1p | solution.py:204
  7.5 0.1 bitcast_dynamic-update-slice_fusion.4
  7.6 0.1 bitcast_dynamic-update-slice_fusion.3
  7.7 0.1 bitcast_dynamic-update-slice_fusion.2
  7.8 0.1 bitcast_dynamic-update-slice_fusion.1
  7.9 0.1 bitcast_dynamic-update-slice_fusion.fac_ref
  8.0 0.0 copy-start.1
  8.0 0.3 scatter.9
  8.2 0.0 collective-permute-done.rim_ref
  8.3 0.0 copy-start.2
  8.3 1.0 %broadcast_in_dim.16.mask_ref = f32[4,256,128]{2,1,0:T(8,128)} broadcast(f32[4,256]{1,0:T(4,128)S(1)} %pad_maximum_fusion.2), dimensions={0,1} | broadcast | bytes 528384 | tf_op jit(solution)/shard_map/broadcast_in_dim | solution.py:200
  9.3 0.0 copy-done.2
  9.3 21.0 %shard_map.82 = (f32[256,2048]{1,0:T(8,128)}, f32[16,16,2048]{2,1,0:T(8,128)}, f32[16,2048]{1,0:T(8,128)}) custom-call(bf16[256,2048]{1,0:T(8,128)(2,1)} %k_ref.1, bf16[256,2048]{1,0:T(8,128)(2,1)} %v_ref.1, bf16[3,6,2048]{2,1,0:T(8,128)(2,1)} %copy-done.2, f32[3,7,2048]{2,1,0:T(8,128)} %filt_ref.3, f32[16,2048]{1,0:T(8,128)} %get-tuple-element.49.amp_ref, ...), custom_call_target="tpu_custom_call" | custom-call | tf_op jit(solution)/shard_map/pallas_call | solution.py:212
  30.3 0.0 copy-done.1
  30.3 30.1 %shard_map.83 = (f32[16,2048]{1,0:T(8,128)}, f32[256,2048]{1,0:T(8,128)}) custom-call(f32[16,2048]{1,0:T(8,128)} %get-tuple-element.35.own_ref, f32[5,16,2048]{2,1,0:T(8,128)} %copy-done.1, bf16[256,2048]{1,0:T(8,128)(2,1)} %q_ref.1, bf16[3,6,2048]{2,1,0:T(8,128)(2,1)} %copy-done.2, f32[3,7,2048]{2,1,0:T(8,128)} %filt_ref.3, ...), custom_call_target="tpu_custom_call" | custom-call | tf_op jit(solution)/shard_map/pallas_call | solution.py:243
  60.4 8.3 %shard_map.84 = bf16[256,2048]{1,0:T(8,128)(2,1)} custom-call(f32[256,2048]{1,0:T(8,128)} %get-tuple-element.34.acc_ref, f32[256,2048]{1,0:T(8,128)} %get-tuple-element.36.qs_ref, f32[16,16,2048]{2,1,0:T(8,128)} %get-tuple-element.37.cl_ref, f32[16,2048]{1,0:T(8,128)} %get-tuple-element.38.hin_ref, f32[16,2048]{1,0:T(8,128)} %get-tuple-element.49.amp_ref, ...), custom_call_target="tpu_custom_call" | custom-call | tf_op jit(solution)/shard_map/pallas_call | solution.py:260
  (9 shorter events, 0.1 us)
Async XLA Ops:
  0.0 2.2 %copy-start.4 = (s32[8]{0:T(128)S(1)}, s32[8]{0:T(128)}, u32[]{:S(2)}) copy-start(s32[8]{0:T(128)} %param.19) | copy-start | bytes 100
  0.0 6.7 %copy-start = (f32[16,2048]{1,0:T(8,128)S(1)}, f32[16,2048]{1,0:T(8,128)}, u32[]{:S(2)}) copy-start(f32[16,2048]{1,0:T(8,128)} %param.17) | copy-start | bytes 393220
  0.0 6.7 %copy-start.3 = (f32[16,2048]{1,0:T(8,128)S(1)}, f32[16,2048]{1,0:T(8,128)}, u32[]{:S(2)}) copy-start(f32[16,2048]{1,0:T(8,128)} %param.16) | copy-start | bytes 393220
  0.9 7.4 %collective-permute-start = (bf16[3,6,2048]{2,1,0:T(8,128)(2,1)S(1)}, bf16[3,6,2048]{2,1,0:T(8,128)(2,1)S(1)}, u32[]{:S(2)}, u32[]{:S(2)}) collective-permute-start(bf16[3,6,2048]{2,1,0:T(8,128)(2,1)S(1)} %pad_maximum_fusion), channel_id=1, source_target_pairs={{0,4},{4,8},{8,12},{12,16},{16,20},{20,24},{24,28},{28,32},{32,36}... | collective-permute-start | bytes 221192 | tf_op jit(solution)/shard_map/ppermute | solution.py:22
  8.0 22.3 %copy-start.1 = (f32[5,16,2048]{2,1,0:T(8,128)}, f32[5,16,2048]{2,1,0:T(8,128)S(1)}, u32[]{:S(2)}) copy-start(f32[5,16,2048]{2,1,0:T(8,128)S(1)} %bitcast_dynamic-update-slice_fusion.fac_ref) | copy-start | bytes 1966084
  8.3 1.0 %copy-start.2 = (bf16[3,6,2048]{2,1,0:T(8,128)(2,1)}, bf16[3,6,2048]{2,1,0:T(8,128)(2,1)S(1)}, u32[]{:S(2)}) copy-start(bf16[3,6,2048]{2,1,0:T(8,128)(2,1)S(1)} %collective-permute-done.rim_ref) | copy-start | bytes 221188

commit v12 on v11

--- a/solution.py
+++ b/solution.py
@@ -10,7 +10,7 @@
 MODES = 16
 TAPS = 7
 LANES = 128
-LANES_FIX = 256
+LANES_FIX = 512
 LANES_LOCAL = 512
 SEGMENTS = 8
 INTERPRET = False

time: 69.1 us -> 67.7 us (0.980)
  Pallas kernels: 59.4 us -> 58.1 us
    pallas_call x1, Pallas kernels: 8.3 us -> 7.03 us  [body(): pl.pallas_call(fix_kernel, grid=(channels // LANES_FIX,), in_specs=[wide(...]
where the time goes in v12:
time: 67.7 us; the launch traced here: 67.4 us
  Pallas kernels  58.1 us (86%)
  other arithmetic  3.37 us (5%)
  between operations  3.34 us (5%)
  local copies, waits for them, and re-layouts  1.3 us (2%)
  starting transfers between devices  1.29 us (2%)
    pallas_call x1, Pallas kernels, body(): pl.pallas_call(functools.partial(scan_kernel, ctx_count, tuple(spans)), o...  30.1 us
    pallas_call x1, Pallas kernels, body(): pl.pallas_call(local_kernel, grid=(channels // LANES_LOCAL,), in_specs=[c...  21 us
    pallas_call x1, Pallas kernels, body(): pl.pallas_call(fix_kernel, grid=(channels // LANES_FIX,), in_specs=[wide(...  7.03 us
  transfers between devices with their start and end apart: 1, of which 0 were waited for; matrix products, arithmetic and copies ran while one was open for 4% of the time, Pallas kernels for 0%

profile of v12, /device:TPU:31, one launch (start us, length us, event | category | flops | bytes accessed | tf_op | source)
XLA Modules:
  0.0 67.4 jit_solution(7114357908130029715)
XLA Ops:
  0.0 0.0 copy-start.4
  0.0 0.0 copy-start
  0.0 0.0 copy-start.3
  0.0 0.9 %pad_maximum_fusion = bf16[3,6,2048]{2,1,0:T(8,128)(2,1)S(1)} fusion(bf16[1,256,2048]{2,1,0:T(8,128)(2,1)} %bitcast.23, bf16[1,256,2048]{2,1,0:T(8,128)(2,1)} %bitcast.22, bf16[1,256,2048]{2,1,0:T(8,128)(2,1)} %bitcast.24), kind=kLoop, calls=%fused_computation.9 | loop fusion | flops 221184 | bytes 3219456 | tf_op jit(solution)/shard_map/stack | solution.py:202
  0.9 1.3 %collective-permute-start = (bf16[3,6,2048]{2,1,0:T(8,128)(2,1)S(1)}, bf16[3,6,2048]{2,1,0:T(8,128)(2,1)S(1)}, u32[]{:S(2)}, u32[]{:S(2)}) collective-permute-start(bf16[3,6,2048]{2,1,0:T(8,128)(2,1)S(1)} %pad_maximum_fusion), channel_id=1, source_target_pairs={{0,4},{4,8},{8,12},{12,16},{16,20},{20,24},{24,28},{28,32},{32,36}... | collective-permute-start | bytes 221192 | tf_op jit(solution)/shard_map/ppermute | solution.py:22
  2.2 0.0 copy-done.4
  2.2 0.2 reduce-window.9
  2.4 0.8 %and_reduce_fusion.2 = (pred[]{:T(512)}, pred[]{:T(512)}, pred[]{:T(512)}, pred[]{:T(512)}, pred[]{:T(512)}, /*index=5*/s32[8]{0:T(128)S(1)}) fusion(s32[]{:T(128)S(6)} %mul.138, s32[]{:T(128)S(6)} %mul.114, s32[]{:T(128)S(6)} %mul.118, s32[]{:T(128)S(6)} %mul.133, s32[]{:T(128)S(6)} %mul.128, s32[]{:T(128)S(6)} %mul.123, s32[]{:T(128)S(6)} %mul.117, ...), kind=kLoop, calls=%fused_computation.21 | loop fusion | flops 139 | bytes 129 | tf_op jit(solution)/shard_map/reduce_or | solution.py:228
  3.2 0.1 select_reduce_fusion
  6.5 0.2 and_reduce_fusion
  6.7 0.0 copy-done
  6.7 0.0 copy-done.3
  6.7 0.8 %negate_log-plus-one_fusion = (f32[16,2048]{1,0:T(8,128)}, f32[16,2048]{1,0:T(8,128)}, f32[16,2048]{1,0:T(8,128)}) fusion(f32[16,2048]{1,0:T(8,128)S(1)} %copy-done, f32[16,2048]{1,0:T(8,128)S(1)} %copy-done.3), kind=kLoop, calls=%fused_computation.8 | loop fusion | flops 131072 | bytes 655360 | tf_op jit(solution)/shard_map/log1p | solution.py:204
  7.5 0.1 bitcast_dynamic-update-slice_fusion.4
  7.6 0.1 bitcast_dynamic-update-slice_fusion.3
  7.7 0.1 bitcast_dynamic-update-slice_fusion.2
  7.8 0.1 bitcast_dynamic-update-slice_fusion.1
  7.9 0.1 bitcast_dynamic-update-slice_fusion.fac_ref
  8.0 0.0 copy-start.1
  8.0 0.3 scatter.9
  8.2 0.0 collective-permute-done.rim_ref
  8.3 0.0 copy-start.2
  8.3 1.0 %broadcast_in_dim.16.mask_ref = f32[4,256,128]{2,1,0:T(8,128)} broadcast(f32[4,256]{1,0:T(4,128)S(1)} %pad_maximum_fusion.2), dimensions={0,1} | broadcast | bytes 528384 | tf_op jit(solution)/shard_map/broadcast_in_dim | solution.py:200
  9.3 0.0 copy-done.2
  9.3 21.0 %shard_map.82 = (f32[256,2048]{1,0:T(8,128)}, f32[16,16,2048]{2,1,0:T(8,128)}, f32[16,2048]{1,0:T(8,128)}) custom-call(bf16[256,2048]{1,0:T(8,128)(2,1)} %k_ref.1, bf16[256,2048]{1,0:T(8,128)(2,1)} %v_ref.1, bf16[3,6,2048]{2,1,0:T(8,128)(2,1)} %copy-done.2, f32[3,7,2048]{2,1,0:T(8,128)} %filt_ref.3, f32[16,2048]{1,0:T(8,128)} %get-tuple-element.49.amp_ref, ...), custom_call_target="tpu_custom_call" | custom-call | tf_op jit(solution)/shard_map/pallas_call | solution.py:212
  30.3 0.0 copy-done.1
  30.3 30.1 %shard_map.83 = (f32[16,2048]{1,0:T(8,128)}, f32[256,2048]{1,0:T(8,128)}) custom-call(f32[16,2048]{1,0:T(8,128)} %get-tuple-element.35.own_ref, f32[5,16,2048]{2,1,0:T(8,128)} %copy-done.1, bf16[256,2048]{1,0:T(8,128)(2,1)} %q_ref.1, bf16[3,6,2048]{2,1,0:T(8,128)(2,1)} %copy-done.2, f32[3,7,2048]{2,1,0:T(8,128)} %filt_ref.3, ...), custom_call_target="tpu_custom_call" | custom-call | tf_op jit(solution)/shard_map/pallas_call | solution.py:243
  60.4 7.0 %shard_map.84 = bf16[256,2048]{1,0:T(8,128)(2,1)} custom-call(f32[256,2048]{1,0:T(8,128)} %get-tuple-element.34.acc_ref, f32[256,2048]{1,0:T(8,128)} %get-tuple-element.36.qs_ref, f32[16,16,2048]{2,1,0:T(8,128)} %get-tuple-element.37.cl_ref, f32[16,2048]{1,0:T(8,128)} %get-tuple-element.38.hin_ref, f32[16,2048]{1,0:T(8,128)} %get-tuple-element.49.amp_ref, ...), custom_call_target="tpu_custom_call" | custom-call | tf_op jit(solution)/shard_map/pallas_call | solution.py:260
  (9 shorter events, 0.1 us)
Async XLA Ops:
  0.0 2.2 %copy-start.4 = (s32[8]{0:T(128)S(1)}, s32[8]{0:T(128)}, u32[]{:S(2)}) copy-start(s32[8]{0:T(128)} %param.19) | copy-start | bytes 100
  0.0 6.7 %copy-start = (f32[16,2048]{1,0:T(8,128)S(1)}, f32[16,2048]{1,0:T(8,128)}, u32[]{:S(2)}) copy-start(f32[16,2048]{1,0:T(8,128)} %param.17) | copy-start | bytes 393220
  0.0 6.7 %copy-start.3 = (f32[16,2048]{1,0:T(8,128)S(1)}, f32[16,2048]{1,0:T(8,128)}, u32[]{:S(2)}) copy-start(f32[16,2048]{1,0:T(8,128)} %param.16) | copy-start | bytes 393220
  0.9 7.4 %collective-permute-start = (bf16[3,6,2048]{2,1,0:T(8,128)(2,1)S(1)}, bf16[3,6,2048]{2,1,0:T(8,128)(2,1)S(1)}, u32[]{:S(2)}, u32[]{:S(2)}) collective-permute-start(bf16[3,6,2048]{2,1,0:T(8,128)(2,1)S(1)} %pad_maximum_fusion), channel_id=1, source_target_pairs={{0,4},{4,8},{8,12},{12,16},{16,20},{20,24},{24,28},{28,32},{32,36}... | collective-permute-start | bytes 221192 | tf_op jit(solution)/shard_map/ppermute | solution.py:22
  8.0 22.3 %copy-start.1 = (f32[5,16,2048]{2,1,0:T(8,128)}, f32[5,16,2048]{2,1,0:T(8,128)S(1)}, u32[]{:S(2)}) copy-start(f32[5,16,2048]{2,1,0:T(8,128)S(1)} %bitcast_dynamic-update-slice_fusion.fac_ref) | copy-start | bytes 1966084
  8.3 1.0 %copy-start.2 = (bf16[3,6,2048]{2,1,0:T(8,128)(2,1)}, bf16[3,6,2048]{2,1,0:T(8,128)(2,1)S(1)}, u32[]{:S(2)}) copy-start(bf16[3,6,2048]{2,1,0:T(8,128)(2,1)S(1)} %collective-permute-done.rim_ref) | copy-start | bytes 221188

commit v13 on v12

--- a/solution.py
+++ b/solution.py
@@ -10,7 +10,7 @@
 MODES = 16
 TAPS = 7
 LANES = 128
-LANES_FIX = 512
+LANES_FIX = 1024
 LANES_LOCAL = 512
 SEGMENTS = 8
 INTERPRET = False

time: 67.7 us -> 68.3 us (level)
  Pallas kernels: 58.1 us -> 58.8 us
where the time goes in v13:
time: 68.3 us; the launch traced here: 68.1 us
  Pallas kernels  58.8 us (86%)
  other arithmetic  3.37 us (5%)
  between operations  3.34 us (5%)
  local copies, waits for them, and re-layouts  1.3 us (2%)
  starting transfers between devices  1.29 us (2%)
    pallas_call x1, Pallas kernels, body(): pl.pallas_call(functools.partial(scan_kernel, ctx_count, tuple(spans)), o...  30.1 us
    pallas_call x1, Pallas kernels, body(): pl.pallas_call(local_kernel, grid=(channels // LANES_LOCAL,), in_specs=[c...  21 us
    pallas_call x1, Pallas kernels, body(): pl.pallas_call(fix_kernel, grid=(channels // LANES_FIX,), in_specs=[wide(...  7.71 us
  transfers between devices with their start and end apart: 1, of which 0 were waited for; matrix products, arithmetic and copies ran while one was open for 4% of the time, Pallas kernels for 0%

profile of v13, /device:TPU:31, one launch (start us, length us, event | category | flops | bytes accessed | tf_op | source)
XLA Modules:
  0.0 68.1 jit_solution(2768580138593789217)
XLA Ops:
  0.0 0.0 copy-start.4
  0.0 0.0 copy-start
  0.0 0.0 copy-start.3
  0.0 0.9 %pad_maximum_fusion = bf16[3,6,2048]{2,1,0:T(8,128)(2,1)S(1)} fusion(bf16[1,256,2048]{2,1,0:T(8,128)(2,1)} %bitcast.23, bf16[1,256,2048]{2,1,0:T(8,128)(2,1)} %bitcast.22, bf16[1,256,2048]{2,1,0:T(8,128)(2,1)} %bitcast.24), kind=kLoop, calls=%fused_computation.9 | loop fusion | flops 221184 | bytes 3219456 | tf_op jit(solution)/shard_map/stack | solution.py:202
  0.9 1.3 %collective-permute-start = (bf16[3,6,2048]{2,1,0:T(8,128)(2,1)S(1)}, bf16[3,6,2048]{2,1,0:T(8,128)(2,1)S(1)}, u32[]{:S(2)}, u32[]{:S(2)}) collective-permute-start(bf16[3,6,2048]{2,1,0:T(8,128)(2,1)S(1)} %pad_maximum_fusion), channel_id=1, source_target_pairs={{0,4},{4,8},{8,12},{12,16},{16,20},{20,24},{24,28},{28,32},{32,36}... | collective-permute-start | bytes 221192 | tf_op jit(solution)/shard_map/ppermute | solution.py:22
  2.2 0.0 copy-done.4
  2.2 0.2 reduce-window.9
  2.4 0.8 %and_reduce_fusion.2 = (pred[]{:T(512)}, pred[]{:T(512)}, pred[]{:T(512)}, pred[]{:T(512)}, pred[]{:T(512)}, /*index=5*/s32[8]{0:T(128)S(1)}) fusion(s32[]{:T(128)S(6)} %mul.138, s32[]{:T(128)S(6)} %mul.114, s32[]{:T(128)S(6)} %mul.118, s32[]{:T(128)S(6)} %mul.133, s32[]{:T(128)S(6)} %mul.128, s32[]{:T(128)S(6)} %mul.123, s32[]{:T(128)S(6)} %mul.117, ...), kind=kLoop, calls=%fused_computation.21 | loop fusion | flops 139 | bytes 129 | tf_op jit(solution)/shard_map/reduce_or | solution.py:228
  3.2 0.1 select_reduce_fusion
  6.5 0.2 and_reduce_fusion
  6.7 0.0 copy-done
  6.7 0.0 copy-done.3
  6.7 0.8 %negate_log-plus-one_fusion = (f32[16,2048]{1,0:T(8,128)}, f32[16,2048]{1,0:T(8,128)}, f32[16,2048]{1,0:T(8,128)}) fusion(f32[16,2048]{1,0:T(8,128)S(1)} %copy-done, f32[16,2048]{1,0:T(8,128)S(1)} %copy-done.3), kind=kLoop, calls=%fused_computation.8 | loop fusion | flops 131072 | bytes 655360 | tf_op jit(solution)/shard_map/log1p | solution.py:204
  7.5 0.1 bitcast_dynamic-update-slice_fusion.4
  7.6 0.1 bitcast_dynamic-update-slice_fusion.3
  7.7 0.1 bitcast_dynamic-update-slice_fusion.2
  7.8 0.1 bitcast_dynamic-update-slice_fusion.1
  7.9 0.1 bitcast_dynamic-update-slice_fusion.fac_ref
  8.0 0.0 copy-start.1
  8.0 0.3 scatter.9
  8.2 0.0 collective-permute-done.rim_ref
  8.3 0.0 copy-start.2
  8.3 1.0 %broadcast_in_dim.16.mask_ref = f32[4,256,128]{2,1,0:T(8,128)} broadcast(f32[4,256]{1,0:T(4,128)S(1)} %pad_maximum_fusion.2), dimensions={0,1} | broadcast | bytes 528384 | tf_op jit(solution)/shard_map/broadcast_in_dim | solution.py:200
  9.3 0.0 copy-done.2
  9.3 21.0 %shard_map.82 = (f32[256,2048]{1,0:T(8,128)}, f32[16,16,2048]{2,1,0:T(8,128)}, f32[16,2048]{1,0:T(8,128)}) custom-call(bf16[256,2048]{1,0:T(8,128)(2,1)} %k_ref.1, bf16[256,2048]{1,0:T(8,128)(2,1)} %v_ref.1, bf16[3,6,2048]{2,1,0:T(8,128)(2,1)} %copy-done.2, f32[3,7,2048]{2,1,0:T(8,128)} %filt_ref.3, f32[16,2048]{1,0:T(8,128)} %get-tuple-element.49.amp_ref, ...), custom_call_target="tpu_custom_call" | custom-call | tf_op jit(solution)/shard_map/pallas_call | solution.py:212
  30.3 0.0 copy-done.1
  30.3 30.1 %shard_map.83 = (f32[16,2048]{1,0:T(8,128)}, f32[256,2048]{1,0:T(8,128)}) custom-call(f32[16,2048]{1,0:T(8,128)} %get-tuple-element.35.own_ref, f32[5,16,2048]{2,1,0:T(8,128)} %copy-done.1, bf16[256,2048]{1,0:T(8,128)(2,1)} %q_ref.1, bf16[3,6,2048]{2,1,0:T(8,128)(2,1)} %copy-done.2, f32[3,7,2048]{2,1,0:T(8,128)} %filt_ref.3, ...), custom_call_target="tpu_custom_call" | custom-call | tf_op jit(solution)/shard_map/pallas_call | solution.py:243
  60.4 7.7 %shard_map.84 = bf16[256,2048]{1,0:T(8,128)(2,1)} custom-call(f32[256,2048]{1,0:T(8,128)} %get-tuple-element.34.acc_ref, f32[256,2048]{1,0:T(8,128)} %get-tuple-element.36.qs_ref, f32[16,16,2048]{2,1,0:T(8,128)} %get-tuple-element.37.cl_ref, f32[16,2048]{1,0:T(8,128)} %get-tuple-element.38.hin_ref, f32[16,2048]{1,0:T(8,128)} %get-tuple-element.49.amp_ref, ...), custom_call_target="tpu_custom_call" | custom-call | tf_op jit(solution)/shard_map/pallas_call | solution.py:260
  (9 shorter events, 0.1 us)
Async XLA Ops:
  0.0 2.2 %copy-start.4 = (s32[8]{0:T(128)S(1)}, s32[8]{0:T(128)}, u32[]{:S(2)}) copy-start(s32[8]{0:T(128)} %param.19) | copy-start | bytes 100
  0.0 6.7 %copy-start = (f32[16,2048]{1,0:T(8,128)S(1)}, f32[16,2048]{1,0:T(8,128)}, u32[]{:S(2)}) copy-start(f32[16,2048]{1,0:T(8,128)} %param.17) | copy-start | bytes 393220
  0.0 6.7 %copy-start.3 = (f32[16,2048]{1,0:T(8,128)S(1)}, f32[16,2048]{1,0:T(8,128)}, u32[]{:S(2)}) copy-start(f32[16,2048]{1,0:T(8,128)} %param.16) | copy-start | bytes 393220
  0.9 7.4 %collective-permute-start = (bf16[3,6,2048]{2,1,0:T(8,128)(2,1)S(1)}, bf16[3,6,2048]{2,1,0:T(8,128)(2,1)S(1)}, u32[]{:S(2)}, u32[]{:S(2)}) collective-permute-start(bf16[3,6,2048]{2,1,0:T(8,128)(2,1)S(1)} %pad_maximum_fusion), channel_id=1, source_target_pairs={{0,4},{4,8},{8,12},{12,16},{16,20},{20,24},{24,28},{28,32},{32,36}... | collective-permute-start | bytes 221192 | tf_op jit(solution)/shard_map/ppermute | solution.py:22
  8.0 22.3 %copy-start.1 = (f32[5,16,2048]{2,1,0:T(8,128)}, f32[5,16,2048]{2,1,0:T(8,128)S(1)}, u32[]{:S(2)}) copy-start(f32[5,16,2048]{2,1,0:T(8,128)S(1)} %bitcast_dynamic-update-slice_fusion.fac_ref) | copy-start | bytes 1966084
  8.3 1.0 %copy-start.2 = (bf16[3,6,2048]{2,1,0:T(8,128)(2,1)}, bf16[3,6,2048]{2,1,0:T(8,128)(2,1)S(1)}, u32[]{:S(2)}) copy-start(bf16[3,6,2048]{2,1,0:T(8,128)(2,1)S(1)} %collective-permute-done.rim_ref) | copy-start | bytes 221188

commit v14 on v12

--- a/solution.py
+++ b/solution.py
@@ -11,7 +11,7 @@
 TAPS = 7
 LANES = 128
 LANES_FIX = 512
-LANES_LOCAL = 512
+LANES_LOCAL = 1024
 SEGMENTS = 8
 INTERPRET = False
 

time: 67.7 us -> 68.3 us (level)
  no operation moved by 1% of the time
where the time goes in v14:
time: 68.3 us; the launch traced here: 68 us
  Pallas kernels  58.7 us (86%)
  other arithmetic  3.37 us (5%)
  between operations  3.34 us (5%)
  local copies, waits for them, and re-layouts  1.3 us (2%)
  starting transfers between devices  1.29 us (2%)
    pallas_call x1, Pallas kernels, body(): pl.pallas_call(functools.partial(scan_kernel, ctx_count, tuple(spans)), o...  30.1 us
    pallas_call x1, Pallas kernels, body(): pl.pallas_call(local_kernel, grid=(channels // LANES_LOCAL,), in_specs=[c...  21.6 us
    pallas_call x1, Pallas kernels, body(): pl.pallas_call(fix_kernel, grid=(channels // LANES_FIX,), in_specs=[wide(...  7.03 us
  transfers between devices with their start and end apart: 1, of which 0 were waited for; matrix products, arithmetic and copies ran while one was open for 4% of the time, Pallas kernels for 0%

profile of v14, /device:TPU:31, one launch (start us, length us, event | category | flops | bytes accessed | tf_op | source)
XLA Modules:
  0.0 68.0 jit_solution(1900996891497540525)
XLA Ops:
  0.0 0.0 copy-start.4
  0.0 0.0 copy-start
  0.0 0.0 copy-start.3
  0.0 0.9 %pad_maximum_fusion = bf16[3,6,2048]{2,1,0:T(8,128)(2,1)S(1)} fusion(bf16[1,256,2048]{2,1,0:T(8,128)(2,1)} %bitcast.23, bf16[1,256,2048]{2,1,0:T(8,128)(2,1)} %bitcast.22, bf16[1,256,2048]{2,1,0:T(8,128)(2,1)} %bitcast.24), kind=kLoop, calls=%fused_computation.9 | loop fusion | flops 221184 | bytes 3219456 | tf_op jit(solution)/shard_map/stack | solution.py:202
  0.9 1.3 %collective-permute-start = (bf16[3,6,2048]{2,1,0:T(8,128)(2,1)S(1)}, bf16[3,6,2048]{2,1,0:T(8,128)(2,1)S(1)}, u32[]{:S(2)}, u32[]{:S(2)}) collective-permute-start(bf16[3,6,2048]{2,1,0:T(8,128)(2,1)S(1)} %pad_maximum_fusion), channel_id=1, source_target_pairs={{0,4},{4,8},{8,12},{12,16},{16,20},{20,24},{24,28},{28,32},{32,36}... | collective-permute-start | bytes 221192 | tf_op jit(solution)/shard_map/ppermute | solution.py:22
  2.2 0.0 copy-done.4
  2.2 0.2 reduce-window.9
  2.4 0.8 %and_reduce_fusion.2 = (pred[]{:T(512)}, pred[]{:T(512)}, pred[]{:T(512)}, pred[]{:T(512)}, pred[]{:T(512)}, /*index=5*/s32[8]{0:T(128)S(1)}) fusion(s32[]{:T(128)S(6)} %mul.138, s32[]{:T(128)S(6)} %mul.114, s32[]{:T(128)S(6)} %mul.118, s32[]{:T(128)S(6)} %mul.133, s32[]{:T(128)S(6)} %mul.128, s32[]{:T(128)S(6)} %mul.123, s32[]{:T(128)S(6)} %mul.117, ...), kind=kLoop, calls=%fused_computation.21 | loop fusion | flops 139 | bytes 129 | tf_op jit(solution)/shard_map/reduce_or | solution.py:228
  3.2 0.1 select_reduce_fusion
  6.5 0.2 and_reduce_fusion
  6.7 0.0 copy-done
  6.7 0.0 copy-done.3
  6.7 0.8 %negate_log-plus-one_fusion = (f32[16,2048]{1,0:T(8,128)}, f32[16,2048]{1,0:T(8,128)}, f32[16,2048]{1,0:T(8,128)}) fusion(f32[16,2048]{1,0:T(8,128)S(1)} %copy-done, f32[16,2048]{1,0:T(8,128)S(1)} %copy-done.3), kind=kLoop, calls=%fused_computation.8 | loop fusion | flops 131072 | bytes 655360 | tf_op jit(solution)/shard_map/log1p | solution.py:204
  7.5 0.1 bitcast_dynamic-update-slice_fusion.4
  7.6 0.1 bitcast_dynamic-update-slice_fusion.3
  7.7 0.1 bitcast_dynamic-update-slice_fusion.2
  7.8 0.1 bitcast_dynamic-update-slice_fusion.1
  7.9 0.1 bitcast_dynamic-update-slice_fusion.fac_ref
  8.0 0.0 copy-start.1
  8.0 0.3 scatter.9
  8.2 0.0 collective-permute-done.rim_ref
  8.3 0.0 copy-start.2
  8.3 1.0 %broadcast_in_dim.16.mask_ref = f32[4,256,128]{2,1,0:T(8,128)} broadcast(f32[4,256]{1,0:T(4,128)S(1)} %pad_maximum_fusion.2), dimensions={0,1} | broadcast | bytes 528384 | tf_op jit(solution)/shard_map/broadcast_in_dim | solution.py:200
  9.3 0.0 copy-done.2
  9.3 21.6 %shard_map.82 = (f32[256,2048]{1,0:T(8,128)}, f32[16,16,2048]{2,1,0:T(8,128)}, f32[16,2048]{1,0:T(8,128)}) custom-call(bf16[256,2048]{1,0:T(8,128)(2,1)} %k_ref.1, bf16[256,2048]{1,0:T(8,128)(2,1)} %v_ref.1, bf16[3,6,2048]{2,1,0:T(8,128)(2,1)} %copy-done.2, f32[3,7,2048]{2,1,0:T(8,128)} %filt_ref.3, f32[16,2048]{1,0:T(8,128)} %get-tuple-element.49.amp_ref, ...), custom_call_target="tpu_custom_call" | custom-call | tf_op jit(solution)/shard_map/pallas_call | solution.py:212
  30.9 0.0 copy-done.1
  30.9 30.1 %shard_map.83 = (f32[16,2048]{1,0:T(8,128)}, f32[256,2048]{1,0:T(8,128)}) custom-call(f32[16,2048]{1,0:T(8,128)} %get-tuple-element.35.own_ref, f32[5,16,2048]{2,1,0:T(8,128)} %copy-done.1, bf16[256,2048]{1,0:T(8,128)(2,1)} %q_ref.1, bf16[3,6,2048]{2,1,0:T(8,128)(2,1)} %copy-done.2, f32[3,7,2048]{2,1,0:T(8,128)} %filt_ref.3, ...), custom_call_target="tpu_custom_call" | custom-call | tf_op jit(solution)/shard_map/pallas_call | solution.py:243
  61.0 7.0 %shard_map.84 = bf16[256,2048]{1,0:T(8,128)(2,1)} custom-call(f32[256,2048]{1,0:T(8,128)} %get-tuple-element.34.acc_ref, f32[256,2048]{1,0:T(8,128)} %get-tuple-element.36.qs_ref, f32[16,16,2048]{2,1,0:T(8,128)} %get-tuple-element.37.cl_ref, f32[16,2048]{1,0:T(8,128)} %get-tuple-element.38.hin_ref, f32[16,2048]{1,0:T(8,128)} %get-tuple-element.49.amp_ref, ...), custom_call_target="tpu_custom_call" | custom-call | tf_op jit(solution)/shard_map/pallas_call | solution.py:260
  (9 shorter events, 0.1 us)
Async XLA Ops:
  0.0 2.2 %copy-start.4 = (s32[8]{0:T(128)S(1)}, s32[8]{0:T(128)}, u32[]{:S(2)}) copy-start(s32[8]{0:T(128)} %param.19) | copy-start | bytes 100
  0.0 6.7 %copy-start = (f32[16,2048]{1,0:T(8,128)S(1)}, f32[16,2048]{1,0:T(8,128)}, u32[]{:S(2)}) copy-start(f32[16,2048]{1,0:T(8,128)} %param.17) | copy-start | bytes 393220
  0.0 6.7 %copy-start.3 = (f32[16,2048]{1,0:T(8,128)S(1)}, f32[16,2048]{1,0:T(8,128)}, u32[]{:S(2)}) copy-start(f32[16,2048]{1,0:T(8,128)} %param.16) | copy-start | bytes 393220
  0.9 7.4 %collective-permute-start = (bf16[3,6,2048]{2,1,0:T(8,128)(2,1)S(1)}, bf16[3,6,2048]{2,1,0:T(8,128)(2,1)S(1)}, u32[]{:S(2)}, u32[]{:S(2)}) collective-permute-start(bf16[3,6,2048]{2,1,0:T(8,128)(2,1)S(1)} %pad_maximum_fusion), channel_id=1, source_target_pairs={{0,4},{4,8},{8,12},{12,16},{16,20},{20,24},{24,28},{28,32},{32,36}... | collective-permute-start | bytes 221192 | tf_op jit(solution)/shard_map/ppermute | solution.py:22
  8.0 23.0 %copy-start.1 = (f32[5,16,2048]{2,1,0:T(8,128)}, f32[5,16,2048]{2,1,0:T(8,128)S(1)}, u32[]{:S(2)}) copy-start(f32[5,16,2048]{2,1,0:T(8,128)S(1)} %bitcast_dynamic-update-slice_fusion.fac_ref) | copy-start | bytes 1966084
  8.3 1.0 %copy-start.2 = (bf16[3,6,2048]{2,1,0:T(8,128)(2,1)}, bf16[3,6,2048]{2,1,0:T(8,128)(2,1)S(1)}, u32[]{:S(2)}) copy-start(bf16[3,6,2048]{2,1,0:T(8,128)(2,1)S(1)} %collective-permute-done.rim_ref) | copy-start | bytes 221188

commit v15 on v12

--- a/solution.py
+++ b/solution.py
@@ -123,10 +123,26 @@
         partners = partners + (me + count - d) // count + (2 * count - 1 - me - d) // count
     pl.semaphore_wait(barrier, partners)
 
-    def transfer(src, slot, target):
-        return pltpu.make_async_remote_copy(
-            src_ref=src, dst_ref=slots.at[slot], send_sem=send_sems.at[slot], recv_sem=recv_sems.at[slot],
-            device_id=(target, lane), device_id_type=pl.DeviceIdType.MESH)
+    half = slots.shape[2] // 2
+
+    class transfer:
+        def __init__(self, src, slot, target):
+            self.parts = [pltpu.make_async_remote_copy(
+                src_ref=src.at[:, pl.ds(h * half, half)], dst_ref=slots.at[slot, :, pl.ds(h * half, half)],
+                send_sem=send_sems.at[2 * slot + h], recv_sem=recv_sems.at[2 * slot + h],
+                device_id=(target, lane), device_id_type=pl.DeviceIdType.MESH) for h in range(2)]
+
+        def start(self):
+            for part in self.parts:
+                part.start()
+
+        def wait_send(self):
+            for part in self.parts:
+                part.wait_send()
+
+        def wait_recv(self):
+            for part in self.parts:
+                part.wait_recv()
 
     def exchange(src, sends):
         for slot, d in sends:
@@ -248,8 +264,8 @@
         scratch_shapes=[
             pltpu.VMEM((len(spans), MODES, channels), f32),
             pltpu.VMEM((len(spans) + 2, MODES, channels), f32),
-            pltpu.SemaphoreType.DMA((len(spans) + 2,)),
-            pltpu.SemaphoreType.DMA((len(spans) + 2,)),
+            pltpu.SemaphoreType.DMA((2 * len(spans) + 4,)),
+            pltpu.SemaphoreType.DMA((2 * len(spans) + 4,)),
             pltpu.VMEM((row_count + 8, LANES), f32),
         ],
         compiler_params=pltpu.CompilerParams(collective_id=0, has_side_effects=True),

time: 67.7 us -> 67.9 us (level)
  no operation moved by 1% of the time
where the time goes in v15:
time: 67.9 us; the launch traced here: 67.5 us
  Pallas kernels  58.2 us (86%)
  other arithmetic  3.37 us (5%)
  between operations  3.34 us (5%)
  local copies, waits for them, and re-layouts  1.3 us (2%)
  starting transfers between devices  1.29 us (2%)
    pallas_call x1, Pallas kernels, body(): pl.pallas_call(functools.partial(scan_kernel, ctx_count, tuple(spans)), o...  30.2 us
    pallas_call x1, Pallas kernels, body(): pl.pallas_call(local_kernel, grid=(channels // LANES_LOCAL,), in_specs=[c...  21 us
    pallas_call x1, Pallas kernels, body(): pl.pallas_call(fix_kernel, grid=(channels // LANES_FIX,), in_specs=[wide(...  7.03 us
  transfers between devices with their start and end apart: 1, of which 0 were waited for; matrix products, arithmetic and copies ran while one was open for 4% of the time, Pallas kernels for 0%

profile of v15, /device:TPU:31, one launch (start us, length us, event | category | flops | bytes accessed | tf_op | source)
XLA Modules:
  0.0 67.5 jit_solution(9520659999361753364)
XLA Ops:
  0.0 0.0 copy-start.4
  0.0 0.0 copy-start
  0.0 0.0 copy-start.3
  0.0 0.9 %pad_maximum_fusion = bf16[3,6,2048]{2,1,0:T(8,128)(2,1)S(1)} fusion(bf16[1,256,2048]{2,1,0:T(8,128)(2,1)} %bitcast.23, bf16[1,256,2048]{2,1,0:T(8,128)(2,1)} %bitcast.22, bf16[1,256,2048]{2,1,0:T(8,128)(2,1)} %bitcast.24), kind=kLoop, calls=%fused_computation.9 | loop fusion | flops 221184 | bytes 3219456 | tf_op jit(solution)/shard_map/stack | solution.py:218
  0.9 1.3 %collective-permute-start = (bf16[3,6,2048]{2,1,0:T(8,128)(2,1)S(1)}, bf16[3,6,2048]{2,1,0:T(8,128)(2,1)S(1)}, u32[]{:S(2)}, u32[]{:S(2)}) collective-permute-start(bf16[3,6,2048]{2,1,0:T(8,128)(2,1)S(1)} %pad_maximum_fusion), channel_id=1, source_target_pairs={{0,4},{4,8},{8,12},{12,16},{16,20},{20,24},{24,28},{28,32},{32,36}... | collective-permute-start | bytes 221192 | tf_op jit(solution)/shard_map/ppermute | solution.py:22
  2.2 0.0 copy-done.4
  2.2 0.2 reduce-window.9
  2.4 0.8 %and_reduce_fusion.2 = (pred[]{:T(512)}, pred[]{:T(512)}, pred[]{:T(512)}, pred[]{:T(512)}, pred[]{:T(512)}, /*index=5*/s32[8]{0:T(128)S(1)}) fusion(s32[]{:T(128)S(6)} %mul.138, s32[]{:T(128)S(6)} %mul.114, s32[]{:T(128)S(6)} %mul.118, s32[]{:T(128)S(6)} %mul.133, s32[]{:T(128)S(6)} %mul.128, s32[]{:T(128)S(6)} %mul.123, s32[]{:T(128)S(6)} %mul.117, ...), kind=kLoop, calls=%fused_computation.21 | loop fusion | flops 139 | bytes 129 | tf_op jit(solution)/shard_map/reduce_or | solution.py:244
  3.2 0.1 select_reduce_fusion
  6.5 0.2 and_reduce_fusion
  6.7 0.0 copy-done
  6.7 0.0 copy-done.3
  6.7 0.8 %negate_log-plus-one_fusion = (f32[16,2048]{1,0:T(8,128)}, f32[16,2048]{1,0:T(8,128)}, f32[16,2048]{1,0:T(8,128)}) fusion(f32[16,2048]{1,0:T(8,128)S(1)} %copy-done, f32[16,2048]{1,0:T(8,128)S(1)} %copy-done.3), kind=kLoop, calls=%fused_computation.8 | loop fusion | flops 131072 | bytes 655360 | tf_op jit(solution)/shard_map/log1p | solution.py:220
  7.5 0.1 bitcast_dynamic-update-slice_fusion.4
  7.6 0.1 bitcast_dynamic-update-slice_fusion.3
  7.7 0.1 bitcast_dynamic-update-slice_fusion.2
  7.8 0.1 bitcast_dynamic-update-slice_fusion.1
  7.9 0.1 bitcast_dynamic-update-slice_fusion.fac_ref
  8.0 0.0 copy-start.1
  8.0 0.3 scatter.9
  8.2 0.0 collective-permute-done.rim_ref
  8.3 0.0 copy-start.2
  8.3 1.0 %broadcast_in_dim.16.mask_ref = f32[4,256,128]{2,1,0:T(8,128)} broadcast(f32[4,256]{1,0:T(4,128)S(1)} %pad_maximum_fusion.2), dimensions={0,1} | broadcast | bytes 528384 | tf_op jit(solution)/shard_map/broadcast_in_dim | solution.py:216
  9.3 0.0 copy-done.2
  9.3 21.0 %shard_map.82 = (f32[256,2048]{1,0:T(8,128)}, f32[16,16,2048]{2,1,0:T(8,128)}, f32[16,2048]{1,0:T(8,128)}) custom-call(bf16[256,2048]{1,0:T(8,128)(2,1)} %k_ref.1, bf16[256,2048]{1,0:T(8,128)(2,1)} %v_ref.1, bf16[3,6,2048]{2,1,0:T(8,128)(2,1)} %copy-done.2, f32[3,7,2048]{2,1,0:T(8,128)} %filt_ref.3, f32[16,2048]{1,0:T(8,128)} %get-tuple-element.49.amp_ref, ...), custom_call_target="tpu_custom_call" | custom-call | tf_op jit(solution)/shard_map/pallas_call | solution.py:228
  30.3 0.0 copy-done.1
  30.3 30.2 %shard_map.83 = (f32[16,2048]{1,0:T(8,128)}, f32[256,2048]{1,0:T(8,128)}) custom-call(f32[16,2048]{1,0:T(8,128)} %get-tuple-element.35.own_ref, f32[5,16,2048]{2,1,0:T(8,128)} %copy-done.1, bf16[256,2048]{1,0:T(8,128)(2,1)} %q_ref.1, bf16[3,6,2048]{2,1,0:T(8,128)(2,1)} %copy-done.2, f32[3,7,2048]{2,1,0:T(8,128)} %filt_ref.3, ...), custom_call_target="tpu_custom_call" | custom-call | tf_op jit(solution)/shard_map/pallas_call | solution.py:259
  60.5 7.0 %shard_map.84 = bf16[256,2048]{1,0:T(8,128)(2,1)} custom-call(f32[256,2048]{1,0:T(8,128)} %get-tuple-element.34.acc_ref, f32[256,2048]{1,0:T(8,128)} %get-tuple-element.36.qs_ref, f32[16,16,2048]{2,1,0:T(8,128)} %get-tuple-element.37.cl_ref, f32[16,2048]{1,0:T(8,128)} %get-tuple-element.38.hin_ref, f32[16,2048]{1,0:T(8,128)} %get-tuple-element.49.amp_ref, ...), custom_call_target="tpu_custom_call" | custom-call | tf_op jit(solution)/shard_map/pallas_call | solution.py:276
  (9 shorter events, 0.1 us)
Async XLA Ops:
  0.0 2.2 %copy-start.4 = (s32[8]{0:T(128)S(1)}, s32[8]{0:T(128)}, u32[]{:S(2)}) copy-start(s32[8]{0:T(128)} %param.19) | copy-start | bytes 100
  0.0 6.7 %copy-start = (f32[16,2048]{1,0:T(8,128)S(1)}, f32[16,2048]{1,0:T(8,128)}, u32[]{:S(2)}) copy-start(f32[16,2048]{1,0:T(8,128)} %param.17) | copy-start | bytes 393220
  0.0 6.7 %copy-start.3 = (f32[16,2048]{1,0:T(8,128)S(1)}, f32[16,2048]{1,0:T(8,128)}, u32[]{:S(2)}) copy-start(f32[16,2048]{1,0:T(8,128)} %param.16) | copy-start | bytes 393220
  0.9 7.4 %collective-permute-start = (bf16[3,6,2048]{2,1,0:T(8,128)(2,1)S(1)}, bf16[3,6,2048]{2,1,0:T(8,128)(2,1)S(1)}, u32[]{:S(2)}, u32[]{:S(2)}) collective-permute-start(bf16[3,6,2048]{2,1,0:T(8,128)(2,1)S(1)} %pad_maximum_fusion), channel_id=1, source_target_pairs={{0,4},{4,8},{8,12},{12,16},{16,20},{20,24},{24,28},{28,32},{32,36}... | collective-permute-start | bytes 221192 | tf_op jit(solution)/shard_map/ppermute | solution.py:22
  8.0 22.3 %copy-start.1 = (f32[5,16,2048]{2,1,0:T(8,128)}, f32[5,16,2048]{2,1,0:T(8,128)S(1)}, u32[]{:S(2)}) copy-start(f32[5,16,2048]{2,1,0:T(8,128)S(1)} %bitcast_dynamic-update-slice_fusion.fac_ref) | copy-start | bytes 1966084
  8.3 1.0 %copy-start.2 = (bf16[3,6,2048]{2,1,0:T(8,128)(2,1)}, bf16[3,6,2048]{2,1,0:T(8,128)(2,1)S(1)}, u32[]{:S(2)}) copy-start(bf16[3,6,2048]{2,1,0:T(8,128)(2,1)S(1)} %collective-permute-done.rim_ref) | copy-start | bytes 221188

commit v16 on v12

--- a/solution.py
+++ b/solution.py
@@ -60,7 +60,7 @@
             return tuple(new_states)
 
         zero = jnp.zeros((SEGMENTS, LANES), jnp.float32)
-        ends = lax.fori_loop(0, seg_rows, step, tuple([zero] * MODES), unroll=2)
+        ends = lax.fori_loop(0, seg_rows, step, tuple([zero] * MODES), unroll=4)
         acc_ref[:, lanes] = sum_ref[...]
         for m in range(MODES):
             seg_decay = jnp.exp(float(seg_rows) * jnp.log(lam_ref[m:m + 1, lanes]))

time: 67.7 us -> 65.4 us (0.966)
  Pallas kernels: 58.1 us -> 55.8 us
    pallas_call x1, Pallas kernels: 21 us -> 18.7 us  [body(): pl.pallas_call(local_kernel, grid=(channels // LANES_LOCAL,), in_specs=[c...]
where the time goes in v16:
time: 65.4 us; the launch traced here: 65.1 us
  Pallas kernels  55.8 us (85%)
  other arithmetic  3.37 us (5%)
  between operations  3.34 us (5%)
  local copies, waits for them, and re-layouts  1.3 us (2%)
  starting transfers between devices  1.29 us (2%)
    pallas_call x1, Pallas kernels, body(): pl.pallas_call(functools.partial(scan_kernel, ctx_count, tuple(spans)), o...  30.1 us
    pallas_call x1, Pallas kernels, body(): pl.pallas_call(local_kernel, grid=(channels // LANES_LOCAL,), in_specs=[c...  18.7 us
    pallas_call x1, Pallas kernels, body(): pl.pallas_call(fix_kernel, grid=(channels // LANES_FIX,), in_specs=[wide(...  7.03 us
  transfers between devices with their start and end apart: 1, of which 0 were waited for; matrix products, arithmetic and copies ran while one was open for 4% of the time, Pallas kernels for 0%

profile of v16, /device:TPU:31, one launch (start us, length us, event | category | flops | bytes accessed | tf_op | source)
XLA Modules:
  0.0 65.1 jit_solution(6924242512662229744)
XLA Ops:
  0.0 0.0 copy-start.4
  0.0 0.0 copy-start
  0.0 0.0 copy-start.3
  0.0 0.9 %pad_maximum_fusion = bf16[3,6,2048]{2,1,0:T(8,128)(2,1)S(1)} fusion(bf16[1,256,2048]{2,1,0:T(8,128)(2,1)} %bitcast.23, bf16[1,256,2048]{2,1,0:T(8,128)(2,1)} %bitcast.22, bf16[1,256,2048]{2,1,0:T(8,128)(2,1)} %bitcast.24), kind=kLoop, calls=%fused_computation.9 | loop fusion | flops 221184 | bytes 3219456 | tf_op jit(solution)/shard_map/stack | solution.py:202
  0.9 1.3 %collective-permute-start = (bf16[3,6,2048]{2,1,0:T(8,128)(2,1)S(1)}, bf16[3,6,2048]{2,1,0:T(8,128)(2,1)S(1)}, u32[]{:S(2)}, u32[]{:S(2)}) collective-permute-start(bf16[3,6,2048]{2,1,0:T(8,128)(2,1)S(1)} %pad_maximum_fusion), channel_id=1, source_target_pairs={{0,4},{4,8},{8,12},{12,16},{16,20},{20,24},{24,28},{28,32},{32,36}... | collective-permute-start | bytes 221192 | tf_op jit(solution)/shard_map/ppermute | solution.py:22
  2.2 0.0 copy-done.4
  2.2 0.2 reduce-window.9
  2.4 0.8 %and_reduce_fusion.2 = (pred[]{:T(512)}, pred[]{:T(512)}, pred[]{:T(512)}, pred[]{:T(512)}, pred[]{:T(512)}, /*index=5*/s32[8]{0:T(128)S(1)}) fusion(s32[]{:T(128)S(6)} %mul.138, s32[]{:T(128)S(6)} %mul.114, s32[]{:T(128)S(6)} %mul.118, s32[]{:T(128)S(6)} %mul.133, s32[]{:T(128)S(6)} %mul.128, s32[]{:T(128)S(6)} %mul.123, s32[]{:T(128)S(6)} %mul.117, ...), kind=kLoop, calls=%fused_computation.21 | loop fusion | flops 139 | bytes 129 | tf_op jit(solution)/shard_map/reduce_or | solution.py:228
  3.2 0.1 select_reduce_fusion
  6.5 0.2 and_reduce_fusion
  6.7 0.0 copy-done
  6.7 0.0 copy-done.3
  6.7 0.8 %negate_log-plus-one_fusion = (f32[16,2048]{1,0:T(8,128)}, f32[16,2048]{1,0:T(8,128)}, f32[16,2048]{1,0:T(8,128)}) fusion(f32[16,2048]{1,0:T(8,128)S(1)} %copy-done, f32[16,2048]{1,0:T(8,128)S(1)} %copy-done.3), kind=kLoop, calls=%fused_computation.8 | loop fusion | flops 131072 | bytes 655360 | tf_op jit(solution)/shard_map/log1p | solution.py:204
  7.5 0.1 bitcast_dynamic-update-slice_fusion.4
  7.6 0.1 bitcast_dynamic-update-slice_fusion.3
  7.7 0.1 bitcast_dynamic-update-slice_fusion.2
  7.8 0.1 bitcast_dynamic-update-slice_fusion.1
  7.9 0.1 bitcast_dynamic-update-slice_fusion.fac_ref
  8.0 0.0 copy-start.1
  8.0 0.3 scatter.9
  8.2 0.0 collective-permute-done.rim_ref
  8.3 0.0 copy-start.2
  8.3 1.0 %broadcast_in_dim.16.mask_ref = f32[4,256,128]{2,1,0:T(8,128)} broadcast(f32[4,256]{1,0:T(4,128)S(1)} %pad_maximum_fusion.2), dimensions={0,1} | broadcast | bytes 528384 | tf_op jit(solution)/shard_map/broadcast_in_dim | solution.py:200
  9.3 0.0 copy-done.2
  9.3 18.7 %shard_map.82 = (f32[256,2048]{1,0:T(8,128)}, f32[16,16,2048]{2,1,0:T(8,128)}, f32[16,2048]{1,0:T(8,128)}) custom-call(bf16[256,2048]{1,0:T(8,128)(2,1)} %k_ref.1, bf16[256,2048]{1,0:T(8,128)(2,1)} %v_ref.1, bf16[3,6,2048]{2,1,0:T(8,128)(2,1)} %copy-done.2, f32[3,7,2048]{2,1,0:T(8,128)} %filt_ref.3, f32[16,2048]{1,0:T(8,128)} %get-tuple-element.49.amp_ref, ...), custom_call_target="tpu_custom_call" | custom-call | tf_op jit(solution)/shard_map/pallas_call | solution.py:212
  28.0 0.0 copy-done.1
  28.0 30.1 %shard_map.83 = (f32[16,2048]{1,0:T(8,128)}, f32[256,2048]{1,0:T(8,128)}) custom-call(f32[16,2048]{1,0:T(8,128)} %get-tuple-element.35.own_ref, f32[5,16,2048]{2,1,0:T(8,128)} %copy-done.1, bf16[256,2048]{1,0:T(8,128)(2,1)} %q_ref.1, bf16[3,6,2048]{2,1,0:T(8,128)(2,1)} %copy-done.2, f32[3,7,2048]{2,1,0:T(8,128)} %filt_ref.3, ...), custom_call_target="tpu_custom_call" | custom-call | tf_op jit(solution)/shard_map/pallas_call | solution.py:243
  58.1 7.0 %shard_map.84 = bf16[256,2048]{1,0:T(8,128)(2,1)} custom-call(f32[256,2048]{1,0:T(8,128)} %get-tuple-element.34.acc_ref, f32[256,2048]{1,0:T(8,128)} %get-tuple-element.36.qs_ref, f32[16,16,2048]{2,1,0:T(8,128)} %get-tuple-element.37.cl_ref, f32[16,2048]{1,0:T(8,128)} %get-tuple-element.38.hin_ref, f32[16,2048]{1,0:T(8,128)} %get-tuple-element.49.amp_ref, ...), custom_call_target="tpu_custom_call" | custom-call | tf_op jit(solution)/shard_map/pallas_call | solution.py:260
  (9 shorter events, 0.1 us)
Async XLA Ops:
  0.0 2.2 %copy-start.4 = (s32[8]{0:T(128)S(1)}, s32[8]{0:T(128)}, u32[]{:S(2)}) copy-start(s32[8]{0:T(128)} %param.19) | copy-start | bytes 100
  0.0 6.7 %copy-start = (f32[16,2048]{1,0:T(8,128)S(1)}, f32[16,2048]{1,0:T(8,128)}, u32[]{:S(2)}) copy-start(f32[16,2048]{1,0:T(8,128)} %param.17) | copy-start | bytes 393220
  0.0 6.7 %copy-start.3 = (f32[16,2048]{1,0:T(8,128)S(1)}, f32[16,2048]{1,0:T(8,128)}, u32[]{:S(2)}) copy-start(f32[16,2048]{1,0:T(8,128)} %param.16) | copy-start | bytes 393220
  0.9 7.4 %collective-permute-start = (bf16[3,6,2048]{2,1,0:T(8,128)(2,1)S(1)}, bf16[3,6,2048]{2,1,0:T(8,128)(2,1)S(1)}, u32[]{:S(2)}, u32[]{:S(2)}) collective-permute-start(bf16[3,6,2048]{2,1,0:T(8,128)(2,1)S(1)} %pad_maximum_fusion), channel_id=1, source_target_pairs={{0,4},{4,8},{8,12},{12,16},{16,20},{20,24},{24,28},{28,32},{32,36}... | collective-permute-start | bytes 221192 | tf_op jit(solution)/shard_map/ppermute | solution.py:22
  8.0 20.0 %copy-start.1 = (f32[5,16,2048]{2,1,0:T(8,128)}, f32[5,16,2048]{2,1,0:T(8,128)S(1)}, u32[]{:S(2)}) copy-start(f32[5,16,2048]{2,1,0:T(8,128)S(1)} %bitcast_dynamic-update-slice_fusion.fac_ref) | copy-start | bytes 1966084
  8.3 1.0 %copy-start.2 = (bf16[3,6,2048]{2,1,0:T(8,128)(2,1)}, bf16[3,6,2048]{2,1,0:T(8,128)(2,1)S(1)}, u32[]{:S(2)}) copy-start(bf16[3,6,2048]{2,1,0:T(8,128)(2,1)S(1)} %collective-permute-done.rim_ref) | copy-start | bytes 221188

commit v17 on v16

--- a/solution.py
+++ b/solution.py
@@ -60,7 +60,7 @@
             return tuple(new_states)
 
         zero = jnp.zeros((SEGMENTS, LANES), jnp.float32)
-        ends = lax.fori_loop(0, seg_rows, step, tuple([zero] * MODES), unroll=4)
+        ends = lax.fori_loop(0, seg_rows, step, tuple([zero] * MODES), unroll=8)
         acc_ref[:, lanes] = sum_ref[...]
         for m in range(MODES):
             seg_decay = jnp.exp(float(seg_rows) * jnp.log(lam_ref[m:m + 1, lanes]))

time: 65.4 us -> 64.5 us (0.986)
  Pallas kernels: 55.8 us -> 54.8 us
    pallas_call x1, Pallas kernels: 18.7 us -> 17.7 us  [body(): pl.pallas_call(local_kernel, grid=(channels // LANES_LOCAL,), in_specs=[c...]
where the time goes in v17:
time: 64.5 us; the launch traced here: 64.1 us
  Pallas kernels  54.8 us (85%)
  other arithmetic  3.37 us (5%)
  between operations  3.34 us (5%)
  local copies, waits for them, and re-layouts  1.3 us (2%)
  starting transfers between devices  1.29 us (2%)
    pallas_call x1, Pallas kernels, body(): pl.pallas_call(functools.partial(scan_kernel, ctx_count, tuple(spans)), o...  30.1 us
    pallas_call x1, Pallas kernels, body(): pl.pallas_call(local_kernel, grid=(channels // LANES_LOCAL,), in_specs=[c...  17.7 us
    pallas_call x1, Pallas kernels, body(): pl.pallas_call(fix_kernel, grid=(channels // LANES_FIX,), in_specs=[wide(...  7.03 us
    ppermute x1, starting transfers between devices, from_behind(): lax.ppermute(value, axis, [(source, source + steps) for source in range(f...  1.29 us
  transfers between devices with their start and end apart: 1, of which 0 were waited for; matrix products, arithmetic and copies ran while one was open for 4% of the time, Pallas kernels for 0%

profile of v17, /device:TPU:31, one launch (start us, length us, event | category | flops | bytes accessed | tf_op | source)
XLA Modules:
  0.0 64.1 jit_solution(1202328566558856161)
XLA Ops:
  0.0 0.0 copy-start.4
  0.0 0.0 copy-start
  0.0 0.0 copy-start.3
  0.0 0.9 %pad_maximum_fusion = bf16[3,6,2048]{2,1,0:T(8,128)(2,1)S(1)} fusion(bf16[1,256,2048]{2,1,0:T(8,128)(2,1)} %bitcast.23, bf16[1,256,2048]{2,1,0:T(8,128)(2,1)} %bitcast.22, bf16[1,256,2048]{2,1,0:T(8,128)(2,1)} %bitcast.24), kind=kLoop, calls=%fused_computation.9 | loop fusion | flops 221184 | bytes 3219456 | tf_op jit(solution)/shard_map/stack | solution.py:202
  0.9 1.3 %collective-permute-start = (bf16[3,6,2048]{2,1,0:T(8,128)(2,1)S(1)}, bf16[3,6,2048]{2,1,0:T(8,128)(2,1)S(1)}, u32[]{:S(2)}, u32[]{:S(2)}) collective-permute-start(bf16[3,6,2048]{2,1,0:T(8,128)(2,1)S(1)} %pad_maximum_fusion), channel_id=1, source_target_pairs={{0,4},{4,8},{8,12},{12,16},{16,20},{20,24},{24,28},{28,32},{32,36}... | collective-permute-start | bytes 221192 | tf_op jit(solution)/shard_map/ppermute | solution.py:22
  2.2 0.0 copy-done.4
  2.2 0.2 reduce-window.9
  2.4 0.8 %and_reduce_fusion.2 = (pred[]{:T(512)}, pred[]{:T(512)}, pred[]{:T(512)}, pred[]{:T(512)}, pred[]{:T(512)}, /*index=5*/s32[8]{0:T(128)S(1)}) fusion(s32[]{:T(128)S(6)} %mul.138, s32[]{:T(128)S(6)} %mul.114, s32[]{:T(128)S(6)} %mul.118, s32[]{:T(128)S(6)} %mul.133, s32[]{:T(128)S(6)} %mul.128, s32[]{:T(128)S(6)} %mul.123, s32[]{:T(128)S(6)} %mul.117, ...), kind=kLoop, calls=%fused_computation.21 | loop fusion | flops 139 | bytes 129 | tf_op jit(solution)/shard_map/reduce_or | solution.py:228
  3.2 0.1 select_reduce_fusion
  6.5 0.2 and_reduce_fusion
  6.7 0.0 copy-done
  6.7 0.0 copy-done.3
  6.7 0.8 %negate_log-plus-one_fusion = (f32[16,2048]{1,0:T(8,128)}, f32[16,2048]{1,0:T(8,128)}, f32[16,2048]{1,0:T(8,128)}) fusion(f32[16,2048]{1,0:T(8,128)S(1)} %copy-done, f32[16,2048]{1,0:T(8,128)S(1)} %copy-done.3), kind=kLoop, calls=%fused_computation.8 | loop fusion | flops 131072 | bytes 655360 | tf_op jit(solution)/shard_map/log1p | solution.py:204
  7.5 0.1 bitcast_dynamic-update-slice_fusion.4
  7.6 0.1 bitcast_dynamic-update-slice_fusion.3
  7.7 0.1 bitcast_dynamic-update-slice_fusion.2
  7.8 0.1 bitcast_dynamic-update-slice_fusion.1
  7.9 0.1 bitcast_dynamic-update-slice_fusion.fac_ref
  8.0 0.0 copy-start.1
  8.0 0.3 scatter.9
  8.2 0.0 collective-permute-done.rim_ref
  8.3 0.0 copy-start.2
  8.3 1.0 %broadcast_in_dim.16.mask_ref = f32[4,256,128]{2,1,0:T(8,128)} broadcast(f32[4,256]{1,0:T(4,128)S(1)} %pad_maximum_fusion.2), dimensions={0,1} | broadcast | bytes 528384 | tf_op jit(solution)/shard_map/broadcast_in_dim | solution.py:200
  9.3 0.0 copy-done.2
  9.3 17.7 %shard_map.82 = (f32[256,2048]{1,0:T(8,128)}, f32[16,16,2048]{2,1,0:T(8,128)}, f32[16,2048]{1,0:T(8,128)}) custom-call(bf16[256,2048]{1,0:T(8,128)(2,1)} %k_ref.1, bf16[256,2048]{1,0:T(8,128)(2,1)} %v_ref.1, bf16[3,6,2048]{2,1,0:T(8,128)(2,1)} %copy-done.2, f32[3,7,2048]{2,1,0:T(8,128)} %filt_ref.3, f32[16,2048]{1,0:T(8,128)} %get-tuple-element.49.amp_ref, ...), custom_call_target="tpu_custom_call" | custom-call | tf_op jit(solution)/shard_map/pallas_call | solution.py:212
  27.0 0.0 copy-done.1
  27.0 30.1 %shard_map.83 = (f32[16,2048]{1,0:T(8,128)}, f32[256,2048]{1,0:T(8,128)}) custom-call(f32[16,2048]{1,0:T(8,128)} %get-tuple-element.35.own_ref, f32[5,16,2048]{2,1,0:T(8,128)} %copy-done.1, bf16[256,2048]{1,0:T(8,128)(2,1)} %q_ref.1, bf16[3,6,2048]{2,1,0:T(8,128)(2,1)} %copy-done.2, f32[3,7,2048]{2,1,0:T(8,128)} %filt_ref.3, ...), custom_call_target="tpu_custom_call" | custom-call | tf_op jit(solution)/shard_map/pallas_call | solution.py:243
  57.1 7.0 %shard_map.84 = bf16[256,2048]{1,0:T(8,128)(2,1)} custom-call(f32[256,2048]{1,0:T(8,128)} %get-tuple-element.34.acc_ref, f32[256,2048]{1,0:T(8,128)} %get-tuple-element.36.qs_ref, f32[16,16,2048]{2,1,0:T(8,128)} %get-tuple-element.37.cl_ref, f32[16,2048]{1,0:T(8,128)} %get-tuple-element.38.hin_ref, f32[16,2048]{1,0:T(8,128)} %get-tuple-element.49.amp_ref, ...), custom_call_target="tpu_custom_call" | custom-call | tf_op jit(solution)/shard_map/pallas_call | solution.py:260
  (9 shorter events, 0.1 us)
Async XLA Ops:
  0.0 2.2 %copy-start.4 = (s32[8]{0:T(128)S(1)}, s32[8]{0:T(128)}, u32[]{:S(2)}) copy-start(s32[8]{0:T(128)} %param.19) | copy-start | bytes 100
  0.0 6.7 %copy-start = (f32[16,2048]{1,0:T(8,128)S(1)}, f32[16,2048]{1,0:T(8,128)}, u32[]{:S(2)}) copy-start(f32[16,2048]{1,0:T(8,128)} %param.17) | copy-start | bytes 393220
  0.0 6.7 %copy-start.3 = (f32[16,2048]{1,0:T(8,128)S(1)}, f32[16,2048]{1,0:T(8,128)}, u32[]{:S(2)}) copy-start(f32[16,2048]{1,0:T(8,128)} %param.16) | copy-start | bytes 393220
  0.9 7.4 %collective-permute-start = (bf16[3,6,2048]{2,1,0:T(8,128)(2,1)S(1)}, bf16[3,6,2048]{2,1,0:T(8,128)(2,1)S(1)}, u32[]{:S(2)}, u32[]{:S(2)}) collective-permute-start(bf16[3,6,2048]{2,1,0:T(8,128)(2,1)S(1)} %pad_maximum_fusion), channel_id=1, source_target_pairs={{0,4},{4,8},{8,12},{12,16},{16,20},{20,24},{24,28},{28,32},{32,36}... | collective-permute-start | bytes 221192 | tf_op jit(solution)/shard_map/ppermute | solution.py:22
  8.0 19.1 %copy-start.1 = (f32[5,16,2048]{2,1,0:T(8,128)}, f32[5,16,2048]{2,1,0:T(8,128)S(1)}, u32[]{:S(2)}) copy-start(f32[5,16,2048]{2,1,0:T(8,128)S(1)} %bitcast_dynamic-update-slice_fusion.fac_ref) | copy-start | bytes 1966084
  8.3 1.0 %copy-start.2 = (bf16[3,6,2048]{2,1,0:T(8,128)(2,1)}, bf16[3,6,2048]{2,1,0:T(8,128)(2,1)S(1)}, u32[]{:S(2)}) copy-start(bf16[3,6,2048]{2,1,0:T(8,128)(2,1)S(1)} %collective-permute-done.rim_ref) | copy-start | bytes 221188

commit v18 on v17

--- a/solution.py
+++ b/solution.py
@@ -60,7 +60,7 @@
             return tuple(new_states)
 
         zero = jnp.zeros((SEGMENTS, LANES), jnp.float32)
-        ends = lax.fori_loop(0, seg_rows, step, tuple([zero] * MODES), unroll=8)
+        ends = lax.fori_loop(0, seg_rows, step, tuple([zero] * MODES), unroll=16)
         acc_ref[:, lanes] = sum_ref[...]
         for m in range(MODES):
             seg_decay = jnp.exp(float(seg_rows) * jnp.log(lam_ref[m:m + 1, lanes]))

time: 64.5 us -> 64.2 us (level)
  no operation moved by 1% of the time
where the time goes in v18:
time: 64.2 us; the launch traced here: 63.8 us
  Pallas kernels  54.5 us (85%)
  other arithmetic  3.37 us (5%)
  between operations  3.34 us (5%)
  local copies, waits for them, and re-layouts  1.3 us (2%)
  starting transfers between devices  1.29 us (2%)
    pallas_call x1, Pallas kernels, body(): pl.pallas_call(functools.partial(scan_kernel, ctx_count, tuple(spans)), o...  30.1 us
    pallas_call x1, Pallas kernels, body(): pl.pallas_call(local_kernel, grid=(channels // LANES_LOCAL,), in_specs=[c...  17.4 us
    pallas_call x1, Pallas kernels, body(): pl.pallas_call(fix_kernel, grid=(channels // LANES_FIX,), in_specs=[wide(...  7.03 us
    ppermute x1, starting transfers between devices, from_behind(): lax.ppermute(value, axis, [(source, source + steps) for source in range(f...  1.29 us
  transfers between devices with their start and end apart: 1, of which 0 were waited for; matrix products, arithmetic and copies ran while one was open for 4% of the time, Pallas kernels for 0%

profile of v18, /device:TPU:31, one launch (start us, length us, event | category | flops | bytes accessed | tf_op | source)
XLA Modules:
  0.0 63.8 jit_solution(1303193782781902328)
XLA Ops:
  0.0 0.0 copy-start.4
  0.0 0.0 copy-start
  0.0 0.0 copy-start.3
  0.0 0.9 %pad_maximum_fusion = bf16[3,6,2048]{2,1,0:T(8,128)(2,1)S(1)} fusion(bf16[1,256,2048]{2,1,0:T(8,128)(2,1)} %bitcast.23, bf16[1,256,2048]{2,1,0:T(8,128)(2,1)} %bitcast.22, bf16[1,256,2048]{2,1,0:T(8,128)(2,1)} %bitcast.24), kind=kLoop, calls=%fused_computation.9 | loop fusion | flops 221184 | bytes 3219456 | tf_op jit(solution)/shard_map/stack | solution.py:202
  0.9 1.3 %collective-permute-start = (bf16[3,6,2048]{2,1,0:T(8,128)(2,1)S(1)}, bf16[3,6,2048]{2,1,0:T(8,128)(2,1)S(1)}, u32[]{:S(2)}, u32[]{:S(2)}) collective-permute-start(bf16[3,6,2048]{2,1,0:T(8,128)(2,1)S(1)} %pad_maximum_fusion), channel_id=1, source_target_pairs={{0,4},{4,8},{8,12},{12,16},{16,20},{20,24},{24,28},{28,32},{32,36}... | collective-permute-start | bytes 221192 | tf_op jit(solution)/shard_map/ppermute | solution.py:22
  2.2 0.0 copy-done.4
  2.2 0.2 reduce-window.9
  2.4 0.8 %and_reduce_fusion.2 = (pred[]{:T(512)}, pred[]{:T(512)}, pred[]{:T(512)}, pred[]{:T(512)}, pred[]{:T(512)}, /*index=5*/s32[8]{0:T(128)S(1)}) fusion(s32[]{:T(128)S(6)} %mul.138, s32[]{:T(128)S(6)} %mul.114, s32[]{:T(128)S(6)} %mul.118, s32[]{:T(128)S(6)} %mul.133, s32[]{:T(128)S(6)} %mul.128, s32[]{:T(128)S(6)} %mul.123, s32[]{:T(128)S(6)} %mul.117, ...), kind=kLoop, calls=%fused_computation.21 | loop fusion | flops 139 | bytes 129 | tf_op jit(solution)/shard_map/reduce_or | solution.py:228
  3.2 0.1 select_reduce_fusion
  6.5 0.2 and_reduce_fusion
  6.7 0.0 copy-done
  6.7 0.0 copy-done.3
  6.7 0.8 %negate_log-plus-one_fusion = (f32[16,2048]{1,0:T(8,128)}, f32[16,2048]{1,0:T(8,128)}, f32[16,2048]{1,0:T(8,128)}) fusion(f32[16,2048]{1,0:T(8,128)S(1)} %copy-done, f32[16,2048]{1,0:T(8,128)S(1)} %copy-done.3), kind=kLoop, calls=%fused_computation.8 | loop fusion | flops 131072 | bytes 655360 | tf_op jit(solution)/shard_map/log1p | solution.py:204
  7.5 0.1 bitcast_dynamic-update-slice_fusion.4
  7.6 0.1 bitcast_dynamic-update-slice_fusion.3
  7.7 0.1 bitcast_dynamic-update-slice_fusion.2
  7.8 0.1 bitcast_dynamic-update-slice_fusion.1
  7.9 0.1 bitcast_dynamic-update-slice_fusion.fac_ref
  8.0 0.0 copy-start.1
  8.0 0.3 scatter.9
  8.2 0.0 collective-permute-done.rim_ref
  8.3 0.0 copy-start.2
  8.3 1.0 %broadcast_in_dim.16.mask_ref = f32[4,256,128]{2,1,0:T(8,128)} broadcast(f32[4,256]{1,0:T(4,128)S(1)} %pad_maximum_fusion.2), dimensions={0,1} | broadcast | bytes 528384 | tf_op jit(solution)/shard_map/broadcast_in_dim | solution.py:200
  9.3 0.0 copy-done.2
  9.3 17.4 %shard_map.82 = (f32[256,2048]{1,0:T(8,128)}, f32[16,16,2048]{2,1,0:T(8,128)}, f32[16,2048]{1,0:T(8,128)}) custom-call(bf16[256,2048]{1,0:T(8,128)(2,1)} %k_ref.1, bf16[256,2048]{1,0:T(8,128)(2,1)} %v_ref.1, bf16[3,6,2048]{2,1,0:T(8,128)(2,1)} %copy-done.2, f32[3,7,2048]{2,1,0:T(8,128)} %filt_ref.3, f32[16,2048]{1,0:T(8,128)} %get-tuple-element.49.amp_ref, ...), custom_call_target="tpu_custom_call" | custom-call | tf_op jit(solution)/shard_map/pallas_call | solution.py:212
  26.7 0.0 copy-done.1
  26.7 30.1 %shard_map.83 = (f32[16,2048]{1,0:T(8,128)}, f32[256,2048]{1,0:T(8,128)}) custom-call(f32[16,2048]{1,0:T(8,128)} %get-tuple-element.35.own_ref, f32[5,16,2048]{2,1,0:T(8,128)} %copy-done.1, bf16[256,2048]{1,0:T(8,128)(2,1)} %q_ref.1, bf16[3,6,2048]{2,1,0:T(8,128)(2,1)} %copy-done.2, f32[3,7,2048]{2,1,0:T(8,128)} %filt_ref.3, ...), custom_call_target="tpu_custom_call" | custom-call | tf_op jit(solution)/shard_map/pallas_call | solution.py:243
  56.8 7.0 %shard_map.84 = bf16[256,2048]{1,0:T(8,128)(2,1)} custom-call(f32[256,2048]{1,0:T(8,128)} %get-tuple-element.34.acc_ref, f32[256,2048]{1,0:T(8,128)} %get-tuple-element.36.qs_ref, f32[16,16,2048]{2,1,0:T(8,128)} %get-tuple-element.37.cl_ref, f32[16,2048]{1,0:T(8,128)} %get-tuple-element.38.hin_ref, f32[16,2048]{1,0:T(8,128)} %get-tuple-element.49.amp_ref, ...), custom_call_target="tpu_custom_call" | custom-call | tf_op jit(solution)/shard_map/pallas_call | solution.py:260
  (9 shorter events, 0.1 us)
Async XLA Ops:
  0.0 2.2 %copy-start.4 = (s32[8]{0:T(128)S(1)}, s32[8]{0:T(128)}, u32[]{:S(2)}) copy-start(s32[8]{0:T(128)} %param.19) | copy-start | bytes 100
  0.0 6.7 %copy-start = (f32[16,2048]{1,0:T(8,128)S(1)}, f32[16,2048]{1,0:T(8,128)}, u32[]{:S(2)}) copy-start(f32[16,2048]{1,0:T(8,128)} %param.17) | copy-start | bytes 393220
  0.0 6.7 %copy-start.3 = (f32[16,2048]{1,0:T(8,128)S(1)}, f32[16,2048]{1,0:T(8,128)}, u32[]{:S(2)}) copy-start(f32[16,2048]{1,0:T(8,128)} %param.16) | copy-start | bytes 393220
  0.9 7.4 %collective-permute-start = (bf16[3,6,2048]{2,1,0:T(8,128)(2,1)S(1)}, bf16[3,6,2048]{2,1,0:T(8,128)(2,1)S(1)}, u32[]{:S(2)}, u32[]{:S(2)}) collective-permute-start(bf16[3,6,2048]{2,1,0:T(8,128)(2,1)S(1)} %pad_maximum_fusion), channel_id=1, source_target_pairs={{0,4},{4,8},{8,12},{12,16},{16,20},{20,24},{24,28},{28,32},{32,36}... | collective-permute-start | bytes 221192 | tf_op jit(solution)/shard_map/ppermute | solution.py:22
  8.0 18.8 %copy-start.1 = (f32[5,16,2048]{2,1,0:T(8,128)}, f32[5,16,2048]{2,1,0:T(8,128)S(1)}, u32[]{:S(2)}) copy-start(f32[5,16,2048]{2,1,0:T(8,128)S(1)} %bitcast_dynamic-update-slice_fusion.fac_ref) | copy-start | bytes 1966084
  8.3 1.0 %copy-start.2 = (bf16[3,6,2048]{2,1,0:T(8,128)(2,1)}, bf16[3,6,2048]{2,1,0:T(8,128)(2,1)S(1)}, u32[]{:S(2)}) copy-start(bf16[3,6,2048]{2,1,0:T(8,128)(2,1)S(1)} %collective-permute-done.rim_ref) | copy-start | bytes 221188

commit v19 on v18

--- a/solution.py
+++ b/solution.py
@@ -60,7 +60,7 @@
             return tuple(new_states)
 
         zero = jnp.zeros((SEGMENTS, LANES), jnp.float32)
-        ends = lax.fori_loop(0, seg_rows, step, tuple([zero] * MODES), unroll=16)
+        ends = lax.fori_loop(0, seg_rows, step, tuple([zero] * MODES), unroll=32)
         acc_ref[:, lanes] = sum_ref[...]
         for m in range(MODES):
             seg_decay = jnp.exp(float(seg_rows) * jnp.log(lam_ref[m:m + 1, lanes]))

time: 64.2 us -> 63.4 us (0.988)
  Pallas kernels: 54.5 us -> 53.8 us
    pallas_call x1, Pallas kernels: 17.4 us -> 16.7 us  [body(): pl.pallas_call(local_kernel, grid=(channels // LANES_LOCAL,), in_specs=[c...]
where the time goes in v19:
time: 63.4 us; the launch traced here: 63.1 us
  Pallas kernels  53.8 us (85%)
  other arithmetic  3.37 us (5%)
  between operations  3.35 us (5%)
  local copies, waits for them, and re-layouts  1.3 us (2%)
  starting transfers between devices  1.29 us (2%)
    pallas_call x1, Pallas kernels, body(): pl.pallas_call(functools.partial(scan_kernel, ctx_count, tuple(spans)), o...  30.1 us
    pallas_call x1, Pallas kernels, body(): pl.pallas_call(local_kernel, grid=(channels // LANES_LOCAL,), in_specs=[c...  16.7 us
    pallas_call x1, Pallas kernels, body(): pl.pallas_call(fix_kernel, grid=(channels // LANES_FIX,), in_specs=[wide(...  7.03 us
    ppermute x1, starting transfers between devices, from_behind(): lax.ppermute(value, axis, [(source, source + steps) for source in range(f...  1.29 us
  transfers between devices with their start and end apart: 1, of which 0 were waited for; matrix products, arithmetic and copies ran while one was open for 4% of the time, Pallas kernels for 0%

profile of v19, /device:TPU:31, one launch (start us, length us, event | category | flops | bytes accessed | tf_op | source)
XLA Modules:
  0.0 63.1 jit_solution(3869153153445774676)
XLA Ops:
  0.0 0.0 copy-start.4
  0.0 0.0 copy-start
  0.0 0.0 copy-start.3
  0.0 0.9 %pad_maximum_fusion = bf16[3,6,2048]{2,1,0:T(8,128)(2,1)S(1)} fusion(bf16[1,256,2048]{2,1,0:T(8,128)(2,1)} %bitcast.23, bf16[1,256,2048]{2,1,0:T(8,128)(2,1)} %bitcast.22, bf16[1,256,2048]{2,1,0:T(8,128)(2,1)} %bitcast.24), kind=kLoop, calls=%fused_computation.9 | loop fusion | flops 221184 | bytes 3219456 | tf_op jit(solution)/shard_map/stack | solution.py:202
  0.9 1.3 %collective-permute-start = (bf16[3,6,2048]{2,1,0:T(8,128)(2,1)S(1)}, bf16[3,6,2048]{2,1,0:T(8,128)(2,1)S(1)}, u32[]{:S(2)}, u32[]{:S(2)}) collective-permute-start(bf16[3,6,2048]{2,1,0:T(8,128)(2,1)S(1)} %pad_maximum_fusion), channel_id=1, source_target_pairs={{0,4},{4,8},{8,12},{12,16},{16,20},{20,24},{24,28},{28,32},{32,36}... | collective-permute-start | bytes 221192 | tf_op jit(solution)/shard_map/ppermute | solution.py:22
  2.2 0.0 copy-done.4
  2.2 0.2 reduce-window.9
  2.4 0.8 %and_reduce_fusion.2 = (pred[]{:T(512)}, pred[]{:T(512)}, pred[]{:T(512)}, pred[]{:T(512)}, pred[]{:T(512)}, /*index=5*/s32[8]{0:T(128)S(1)}) fusion(s32[]{:T(128)S(6)} %mul.138, s32[]{:T(128)S(6)} %mul.114, s32[]{:T(128)S(6)} %mul.118, s32[]{:T(128)S(6)} %mul.133, s32[]{:T(128)S(6)} %mul.128, s32[]{:T(128)S(6)} %mul.123, s32[]{:T(128)S(6)} %mul.117, ...), kind=kLoop, calls=%fused_computation.21 | loop fusion | flops 139 | bytes 129 | tf_op jit(solution)/shard_map/reduce_or | solution.py:228
  3.2 0.1 select_reduce_fusion
  6.5 0.2 and_reduce_fusion
  6.7 0.0 copy-done
  6.7 0.0 copy-done.3
  6.7 0.8 %negate_log-plus-one_fusion = (f32[16,2048]{1,0:T(8,128)}, f32[16,2048]{1,0:T(8,128)}, f32[16,2048]{1,0:T(8,128)}) fusion(f32[16,2048]{1,0:T(8,128)S(1)} %copy-done, f32[16,2048]{1,0:T(8,128)S(1)} %copy-done.3), kind=kLoop, calls=%fused_computation.8 | loop fusion | flops 131072 | bytes 655360 | tf_op jit(solution)/shard_map/log1p | solution.py:204
  7.5 0.1 bitcast_dynamic-update-slice_fusion.4
  7.6 0.1 bitcast_dynamic-update-slice_fusion.3
  7.7 0.1 bitcast_dynamic-update-slice_fusion.2
  7.8 0.1 bitcast_dynamic-update-slice_fusion.1
  7.9 0.1 bitcast_dynamic-update-slice_fusion.fac_ref
  8.0 0.0 copy-start.1
  8.0 0.3 scatter.9
  8.2 0.0 collective-permute-done.rim_ref
  8.3 0.0 copy-start.2
  8.3 1.0 %broadcast_in_dim.16.mask_ref = f32[4,256,128]{2,1,0:T(8,128)} broadcast(f32[4,256]{1,0:T(4,128)S(1)} %pad_maximum_fusion.2), dimensions={0,1} | broadcast | bytes 528384 | tf_op jit(solution)/shard_map/broadcast_in_dim | solution.py:200
  9.3 0.0 copy-done.2
  9.3 16.7 %shard_map.82 = (f32[256,2048]{1,0:T(8,128)}, f32[16,16,2048]{2,1,0:T(8,128)}, f32[16,2048]{1,0:T(8,128)}) custom-call(bf16[256,2048]{1,0:T(8,128)(2,1)} %k_ref.1, bf16[256,2048]{1,0:T(8,128)(2,1)} %v_ref.1, bf16[3,6,2048]{2,1,0:T(8,128)(2,1)} %copy-done.2, f32[3,7,2048]{2,1,0:T(8,128)} %filt_ref.3, f32[16,2048]{1,0:T(8,128)} %get-tuple-element.49.amp_ref, ...), custom_call_target="tpu_custom_call" | custom-call | tf_op jit(solution)/shard_map/pallas_call | solution.py:212
  26.0 0.0 copy-done.1
  26.0 30.1 %shard_map.83 = (f32[16,2048]{1,0:T(8,128)}, f32[256,2048]{1,0:T(8,128)}) custom-call(f32[16,2048]{1,0:T(8,128)} %get-tuple-element.35.own_ref, f32[5,16,2048]{2,1,0:T(8,128)} %copy-done.1, bf16[256,2048]{1,0:T(8,128)(2,1)} %q_ref.1, bf16[3,6,2048]{2,1,0:T(8,128)(2,1)} %copy-done.2, f32[3,7,2048]{2,1,0:T(8,128)} %filt_ref.3, ...), custom_call_target="tpu_custom_call" | custom-call | tf_op jit(solution)/shard_map/pallas_call | solution.py:243
  56.1 7.0 %shard_map.84 = bf16[256,2048]{1,0:T(8,128)(2,1)} custom-call(f32[256,2048]{1,0:T(8,128)} %get-tuple-element.34.acc_ref, f32[256,2048]{1,0:T(8,128)} %get-tuple-element.36.qs_ref, f32[16,16,2048]{2,1,0:T(8,128)} %get-tuple-element.37.cl_ref, f32[16,2048]{1,0:T(8,128)} %get-tuple-element.38.hin_ref, f32[16,2048]{1,0:T(8,128)} %get-tuple-element.49.amp_ref, ...), custom_call_target="tpu_custom_call" | custom-call | tf_op jit(solution)/shard_map/pallas_call | solution.py:260
  (9 shorter events, 0.1 us)
Async XLA Ops:
  0.0 2.2 %copy-start.4 = (s32[8]{0:T(128)S(1)}, s32[8]{0:T(128)}, u32[]{:S(2)}) copy-start(s32[8]{0:T(128)} %param.19) | copy-start | bytes 100
  0.0 6.7 %copy-start = (f32[16,2048]{1,0:T(8,128)S(1)}, f32[16,2048]{1,0:T(8,128)}, u32[]{:S(2)}) copy-start(f32[16,2048]{1,0:T(8,128)} %param.17) | copy-start | bytes 393220
  0.0 6.7 %copy-start.3 = (f32[16,2048]{1,0:T(8,128)S(1)}, f32[16,2048]{1,0:T(8,128)}, u32[]{:S(2)}) copy-start(f32[16,2048]{1,0:T(8,128)} %param.16) | copy-start | bytes 393220
  0.9 7.4 %collective-permute-start = (bf16[3,6,2048]{2,1,0:T(8,128)(2,1)S(1)}, bf16[3,6,2048]{2,1,0:T(8,128)(2,1)S(1)}, u32[]{:S(2)}, u32[]{:S(2)}) collective-permute-start(bf16[3,6,2048]{2,1,0:T(8,128)(2,1)S(1)} %pad_maximum_fusion), channel_id=1, source_target_pairs={{0,4},{4,8},{8,12},{12,16},{16,20},{20,24},{24,28},{28,32},{32,36}... | collective-permute-start | bytes 221192 | tf_op jit(solution)/shard_map/ppermute | solution.py:22
  8.0 18.0 %copy-start.1 = (f32[5,16,2048]{2,1,0:T(8,128)}, f32[5,16,2048]{2,1,0:T(8,128)S(1)}, u32[]{:S(2)}) copy-start(f32[5,16,2048]{2,1,0:T(8,128)S(1)} %bitcast_dynamic-update-slice_fusion.fac_ref) | copy-start | bytes 1966084
  8.3 1.0 %copy-start.2 = (bf16[3,6,2048]{2,1,0:T(8,128)(2,1)}, bf16[3,6,2048]{2,1,0:T(8,128)(2,1)S(1)}, u32[]{:S(2)}) copy-start(bf16[3,6,2048]{2,1,0:T(8,128)(2,1)S(1)} %collective-permute-done.rim_ref) | copy-start | bytes 221188
